TPU v7x, 32 devices: a whole 2x2x4 slice. The times are simulated.
32 devices in a mesh: ctx: 8 (over y, x, core), fsdp: 4 (over z).
Axes of the slice: x: 2, y: 2, z: 4, core: 2. Of those that a mesh axis runs over, the one named last changes fastest.
Arguments:
- tokens: bfloat16 [2, 4, 2048, 1024], P(None, 'fsdp', 'ctx'), may hold values from -6 to 6
- cotangent: bfloat16 [2, 4, 2048, 1024], P(None, 'fsdp', 'ctx'), may hold values from -6 to 6
- lengths: int32 [2, 4, 2], P(None, 'fsdp'), may hold values from 512 to 1536, as said below
- order: int32 [2, 4, 16], P(None, 'fsdp'), may hold values from 0 to 15, each once within a row
- w_qkv: bfloat16 [1024, 3072], P('fsdp'), may hold values from -0.1875 to 0.1875
- w_out: bfloat16 [1024, 1024], P('fsdp'), may hold values from -3 to 3
- w_up: bfloat16 [1024, 4096], P('fsdp'), may hold values from -0.1875 to 0.1875
- w_down: bfloat16 [4096, 1024], P('fsdp'), may hold values from -0.09375 to 0.09375
- q_bias: bfloat16 [1024], P('fsdp'), may hold values from -3 to 3
- v_bias: bfloat16 [1024], P('fsdp'), may hold values from -0.19921875 to 0.19921875
- out_bias: bfloat16 [1024], P('fsdp'), may hold values from -1.5 to 1.5
- norm1_gain: bfloat16 [1024], P('fsdp'), may hold values from 0.5 to 1.5
- norm1_bias: bfloat16 [1024], P('fsdp'), may hold values from -0.59765625 to 0.59765625
- up_bias: bfloat16 [4096], P('fsdp'), may hold values from -1.1953125 to 1.1953125
- down_bias: bfloat16 [1024], P('fsdp'), may hold values from -0.59765625 to 0.59765625
- norm2_gain: bfloat16 [1024], P('fsdp'), may hold values from 0.5 to 1.5
- norm2_bias: bfloat16 [1024], P('fsdp'), may hold values from -0.59765625 to 0.59765625
Outputs:
- mixed: bfloat16 [2, 4, 2048, 1024], P(None, 'fsdp', 'ctx')
- tokens_grad: bfloat16 [2, 4, 2048, 1024], P(None, 'fsdp', 'ctx')
- w_qkv_grad: float32 [1024, 3072], P(('ctx', 'fsdp'))
- w_out_grad: float32 [1024, 1024], P(('ctx', 'fsdp'))
- w_up_grad: float32 [1024, 4096], P(('ctx', 'fsdp'))
- w_down_grad: float32 [4096, 1024], P(('ctx', 'fsdp'))
- q_bias_grad: float32 [1024], P(('ctx', 'fsdp'))
- v_bias_grad: float32 [1024], P(('ctx', 'fsdp'))
- out_bias_grad: float32 [1024], P(('ctx', 'fsdp'))
- norm1_gain_grad: float32 [1024], P(('ctx', 'fsdp'))
- norm1_bias_grad: float32 [1024], P(('ctx', 'fsdp'))
- up_bias_grad: float32 [4096], P(('ctx', 'fsdp'))
- down_bias_grad: float32 [1024], P(('ctx', 'fsdp'))
- norm2_gain_grad: float32 [1024], P(('ctx', 'fsdp'))
- norm2_bias_grad: float32 [1024], P(('ctx', 'fsdp'))
Inputs may be any that keep to these rules, and one draw needn't show every extreme that they name: The 2 lengths of each group add up to 2048. `order`: each row names every block position of its group once.
All inputs are finite; a program needn't handle non-finite values.
Results may differ from a plain program's by a relative error of at most 0.029.
Values may be sent and summed in bfloat16 or wider, within the bound.
No kernel may reach another device: no remote copies, remote signals or barrier semaphores. Data moves between devices by JAX's collectives and lax.ppermute only.
A program may use at most 256 MiB of HBM per device.

v0:
```python
from functools import partial
import math

import jax
import jax.numpy as jnp
from jax import lax
from jax.sharding import PartitionSpec as P

D = 1024
H = 16
HD = 64
BLK = 128
MB = 2


NEGATIVE = -1e30
EPSILON = 1e-05


def outer_sum(left_rows, right_rows):
    return lax.dot_general(
        left_rows, right_rows, (((0,), (0,)), ((), ())), preferred_element_type=jnp.float32
    )


def back_dot(left_rows, weight):
    return lax.dot_general(
        left_rows, weight, (((1,), (1,)), ((), ())), preferred_element_type=jnp.float32
    )


def norm_forward(values_in, gain_vec, shift_vec):
    center = values_in - jnp.mean(values_in, -1, keepdims=True)
    inverse = lax.rsqrt(jnp.mean(center * center, -1, keepdims=True) + EPSILON)
    normed = center * inverse
    return (normed * gain_vec + shift_vec, normed, inverse)


def norm_backward(grad_out, normed, inverse, gain_vec):
    grad_norm = grad_out * gain_vec
    inner = (
        grad_norm
        - jnp.mean(grad_norm, -1, keepdims=True)
        - normed * jnp.mean(grad_norm * normed, -1, keepdims=True)
    )
    return (inverse * inner, jnp.sum(grad_out * normed, 0), jnp.sum(grad_out, 0))


def block_picker(wanted, carry, pieces):
    count = pieces[0].shape[0] // BLK
    inside = jnp.logical_and(wanted >= 0, wanted < count)
    safe_index = jnp.clip(wanted, 0, count - 1)
    result = []
    for held, piece in zip(carry, pieces):
        shaped = piece.reshape(count, BLK, piece.shape[1])
        taken = jnp.take(shaped, safe_index, axis=0)
        result.append(jnp.where(inside[:, None, None], taken, held))
    return tuple(result)


def dealt_segments(order_row, length_row):
    offsets = jnp.arange(BLK, dtype=jnp.int32)
    anchor = (order_row[:, None] * BLK + offsets[None, :]).reshape(-1)
    bounds = jnp.cumsum(length_row)[:-1]
    return jnp.sum((anchor[:, None] >= bounds[None, :]).astype(jnp.int32), 1)


def key_steps(count):
    block_rows = 512
    return (block_rows, count // block_rows)


def forward_fold(queries, segment_query, segment_all, scaling, carry, pieces):
    key_rows, value_rows = pieces
    block_rows, steps = key_steps(key_rows.shape[0])

    def forward_step(block_index, running):
        peak_val, denom, accumulated = running
        offset = block_index * block_rows
        key_block = lax.dynamic_slice_in_dim(key_rows, offset, block_rows, 0).reshape(
            block_rows, H, HD
        )
        value_block = lax.dynamic_slice_in_dim(value_rows, offset, block_rows, 0).reshape(
            block_rows, H, HD
        )
        segment_keys = lax.dynamic_slice_in_dim(segment_all, offset, block_rows, 0)
        allowed = (segment_query[:, None] == segment_keys[None, :])[None]
        scores = (
            jnp.einsum("rhd,khd->hrk", queries, key_block, preferred_element_type=jnp.float32)
            * scaling
        )
        scores = jnp.where(allowed, scores, NEGATIVE)
        fresh_peak = jnp.maximum(peak_val, jnp.max(scores, -1))
        numerators = jnp.where(allowed, jnp.exp(scores - fresh_peak[:, :, None]), 0.0)
        shrink = jnp.exp(peak_val - fresh_peak)
        denom = denom * shrink + jnp.sum(numerators, -1)
        accumulated = accumulated * shrink.T[:, :, None] + jnp.einsum(
            "hrk,khd->rhd",
            numerators.astype(jnp.bfloat16),
            value_block,
            preferred_element_type=jnp.float32,
        )
        return (fresh_peak, denom, accumulated)

    return lax.fori_loop(0, steps, forward_step, carry)


def backward_fold(
    queries, grad_attn, segment_query, segment_all, log_total, row_delta, scaling, carry, pieces
):
    key_rows, value_rows = pieces
    block_rows, steps = key_steps(key_rows.shape[0])

    def backward_step(block_index, running):
        grad_query, grad_keys, grad_values = running
        offset = block_index * block_rows
        key_block = lax.dynamic_slice_in_dim(key_rows, offset, block_rows, 0).reshape(
            block_rows, H, HD
        )
        value_block = lax.dynamic_slice_in_dim(value_rows, offset, block_rows, 0).reshape(
            block_rows, H, HD
        )
        segment_keys = lax.dynamic_slice_in_dim(segment_all, offset, block_rows, 0)
        allowed = (segment_query[:, None] == segment_keys[None, :])[None]
        scores = (
            jnp.einsum("rhd,khd->hrk", queries, key_block, preferred_element_type=jnp.float32)
            * scaling
        )
        scores = jnp.where(allowed, scores, NEGATIVE)
        probs = jnp.where(allowed, jnp.exp(scores - log_total[:, :, None]), 0.0)
        grad_probs = jnp.einsum(
            "rhd,khd->hrk", grad_attn, value_block, preferred_element_type=jnp.float32
        )
        grad_scores = (probs * (grad_probs - row_delta[:, :, None]) * scaling).astype(jnp.bfloat16)
        grad_query = grad_query + jnp.einsum(
            "hrk,khd->rhd", grad_scores, key_block, preferred_element_type=jnp.float32
        )
        key_part = jnp.einsum(
            "hrk,rhd->khd", grad_scores, queries, preferred_element_type=jnp.float32
        ).reshape(block_rows, D)
        value_part = jnp.einsum(
            "hrk,rhd->khd",
            probs.astype(jnp.bfloat16),
            grad_attn,
            preferred_element_type=jnp.float32,
        ).reshape(block_rows, D)
        grad_keys = lax.dynamic_update_slice_in_dim(
            grad_keys,
            lax.dynamic_slice_in_dim(grad_keys, offset, block_rows, 0) + key_part,
            offset,
            0,
        )
        grad_values = lax.dynamic_update_slice_in_dim(
            grad_values,
            lax.dynamic_slice_in_dim(grad_values, offset, block_rows, 0) + value_part,
            offset,
            0,
        )
        return (grad_query, grad_keys, grad_values)

    return lax.fori_loop(0, steps, backward_step, carry)


def on_device(
    tokens,
    cotangent,
    lengths,
    order,
    w_qkv,
    w_out,
    w_up,
    w_down,
    q_bias,
    v_bias,
    out_bias,
    norm1_gain,
    norm1_bias,
    up_bias,
    down_bias,
    norm2_gain,
    norm2_bias,
):
    shards = (
        w_qkv,
        w_out,
        w_up,
        w_down,
        q_bias,
        v_bias,
        out_bias,
        norm1_gain,
        norm1_bias,
        up_bias,
        down_bias,
        norm2_gain,
        norm2_bias,
    )
    my_ctx = lax.axis_index("ctx")
    ctx_count = lax.axis_size("ctx")
    rows = tokens.shape[2]
    per_device = rows // BLK
    whole_rows = rows * ctx_count
    scaling = 1.0 / math.sqrt(HD)
    mine = my_ctx * per_device + jnp.arange(per_device, dtype=jnp.int32)
    empty_blocks = jnp.zeros((per_device, BLK, D), jnp.bfloat16)
    mixed_list = []
    grad_list = []
    totals = None
    for micro in range(MB):
        order_row = order[micro, 0]
        segment_all = dealt_segments(order_row, lengths[micro, 0])
        segment_query = lax.dynamic_slice_in_dim(segment_all, my_ctx * rows, rows, 0)
        wanted = jnp.take(order_row, mine)
        (token_blocks,) = block_picker(
            wanted, (empty_blocks,), (lax.all_gather(tokens[micro, 0], "ctx", axis=0, tiled=True),)
        )
        token_rows = token_blocks.reshape(rows, D)
        cot_rows = cotangent[micro, 0].astype(jnp.float32)
        gathered = (
            lax.all_gather(shards[0], "fsdp", axis=0, tiled=True),
            lax.all_gather(shards[1], "fsdp", axis=0, tiled=True),
            lax.all_gather(shards[2], "fsdp", axis=0, tiled=True),
            lax.all_gather(shards[3], "fsdp", axis=0, tiled=True),
            lax.all_gather(shards[4], "fsdp", axis=0, tiled=True),
            lax.all_gather(shards[5], "fsdp", axis=0, tiled=True),
            lax.all_gather(shards[6], "fsdp", axis=0, tiled=True),
            lax.all_gather(shards[7], "fsdp", axis=0, tiled=True),
            lax.all_gather(shards[8], "fsdp", axis=0, tiled=True),
            lax.all_gather(shards[9], "fsdp", axis=0, tiled=True),
            lax.all_gather(shards[10], "fsdp", axis=0, tiled=True),
            lax.all_gather(shards[11], "fsdp", axis=0, tiled=True),
            lax.all_gather(shards[12], "fsdp", axis=0, tiled=True),
        )
        (
            qkv_full,
            out_full,
            up_full,
            down_full,
            qbias_full,
            vbias_full,
            obias_full,
            gain_one,
            shift_one,
            ubias_full,
            dbias_full,
            gain_two,
            shift_two,
        ) = gathered
        full_bias = jnp.concatenate([qbias_full, jnp.zeros_like(qbias_full), vbias_full]).astype(
            jnp.float32
        )
        qkv_rows = (
            jnp.dot(token_rows, qkv_full, preferred_element_type=jnp.float32) + full_bias
        ).astype(jnp.bfloat16)
        queries = qkv_rows[:, :D].reshape(rows, H, HD)
        key_rows = qkv_rows[:, D : 2 * D]
        value_rows = qkv_rows[:, 2 * D :]
        start_state = (
            jnp.full((H, rows), NEGATIVE, jnp.float32),
            jnp.zeros((H, rows), jnp.float32),
            jnp.zeros((rows, H, HD), jnp.float32),
        )
        peak_val, denom, accumulated = forward_fold(
            queries,
            segment_query,
            segment_all,
            scaling,
            start_state,
            (
                lax.all_gather(key_rows, "ctx", axis=0, tiled=True),
                lax.all_gather(value_rows, "ctx", axis=0, tiled=True),
            ),
        )
        log_total = peak_val + jnp.log(denom)
        attn_float = accumulated / denom.T[:, :, None]
        attn_low = attn_float.reshape(rows, D).astype(jnp.bfloat16)
        first_in = (
            token_rows.astype(jnp.float32)
            + jnp.dot(attn_low, out_full, preferred_element_type=jnp.float32)
            + obias_full.astype(jnp.float32)
        )
        first_out, normed_one, inverse_one = norm_forward(
            first_in, gain_one.astype(jnp.float32), shift_one.astype(jnp.float32)
        )
        first_low = first_out.astype(jnp.bfloat16)
        hidden_in = jnp.dot(
            first_low, up_full, preferred_element_type=jnp.float32
        ) + ubias_full.astype(jnp.float32)
        activated, gelu_back = jax.vjp(partial(jax.nn.gelu, approximate=False), hidden_in)
        act_low = activated.astype(jnp.bfloat16)
        second_in = (
            first_out
            + jnp.dot(act_low, down_full, preferred_element_type=jnp.float32)
            + dbias_full.astype(jnp.float32)
        )
        second_out, normed_two, inverse_two = norm_forward(
            second_in, gain_two.astype(jnp.float32), shift_two.astype(jnp.float32)
        )
        mixed_list.append(second_out.astype(jnp.bfloat16))
        (
            qkv_full,
            out_full,
            up_full,
            down_full,
            qbias_full,
            vbias_full,
            obias_full,
            gain_one,
            shift_one,
            ubias_full,
            dbias_full,
            gain_two,
            shift_two,
        ) = (
            lax.all_gather(shards[0], "fsdp", axis=0, tiled=True),
            lax.all_gather(shards[1], "fsdp", axis=0, tiled=True),
            lax.all_gather(shards[2], "fsdp", axis=0, tiled=True),
            lax.all_gather(shards[3], "fsdp", axis=0, tiled=True),
            lax.all_gather(shards[4], "fsdp", axis=0, tiled=True),
            lax.all_gather(shards[5], "fsdp", axis=0, tiled=True),
            lax.all_gather(shards[6], "fsdp", axis=0, tiled=True),
            lax.all_gather(shards[7], "fsdp", axis=0, tiled=True),
            lax.all_gather(shards[8], "fsdp", axis=0, tiled=True),
            lax.all_gather(shards[9], "fsdp", axis=0, tiled=True),
            lax.all_gather(shards[10], "fsdp", axis=0, tiled=True),
            lax.all_gather(shards[11], "fsdp", axis=0, tiled=True),
            lax.all_gather(shards[12], "fsdp", axis=0, tiled=True),
        )
        grad_second, grad_gain_two, grad_shift_two = norm_backward(
            cot_rows, normed_two, inverse_two, gain_two.astype(jnp.float32)
        )
        grad_down_low = grad_second.astype(jnp.bfloat16)
        grad_down_weight = outer_sum(act_low, grad_down_low)
        grad_down_bias = jnp.sum(grad_down_low.astype(jnp.float32), 0)
        (grad_hidden,) = gelu_back(back_dot(grad_down_low, down_full))
        grad_hidden_low = grad_hidden.astype(jnp.bfloat16)
        grad_up_weight = outer_sum(first_low, grad_hidden_low)
        grad_up_bias = jnp.sum(grad_hidden_low.astype(jnp.float32), 0)
        grad_first = grad_second + back_dot(grad_hidden_low, up_full)
        grad_first_in, grad_gain_one, grad_shift_one = norm_backward(
            grad_first, normed_one, inverse_one, gain_one.astype(jnp.float32)
        )
        grad_branch = grad_first_in.astype(jnp.bfloat16)
        grad_out_weight = outer_sum(attn_low, grad_branch)
        grad_out_bias = jnp.sum(grad_branch.astype(jnp.float32), 0)
        grad_attn = back_dot(grad_branch, out_full).astype(jnp.bfloat16).reshape(rows, H, HD)
        row_delta = jnp.sum(grad_attn.astype(jnp.float32) * attn_float, -1).T
        start_back = (
            jnp.zeros((rows, H, HD), jnp.float32),
            jnp.zeros((whole_rows, D), jnp.float32),
            jnp.zeros((whole_rows, D), jnp.float32),
        )
        grad_query, grad_keys_all, grad_values_all = backward_fold(
            queries,
            grad_attn,
            segment_query,
            segment_all,
            log_total,
            row_delta,
            scaling,
            start_back,
            (
                lax.all_gather(key_rows, "ctx", axis=0, tiled=True),
                lax.all_gather(value_rows, "ctx", axis=0, tiled=True),
            ),
        )
        grad_keys, grad_values = (
            lax.psum_scatter(
                grad_keys_all.astype(jnp.bfloat16), "ctx", scatter_dimension=0, tiled=True
            ).astype(jnp.float32),
            lax.psum_scatter(
                grad_values_all.astype(jnp.bfloat16), "ctx", scatter_dimension=0, tiled=True
            ).astype(jnp.float32),
        )
        grad_qkv = jnp.concatenate([grad_query.reshape(rows, D), grad_keys, grad_values], 1).astype(
            jnp.bfloat16
        )
        grad_qkv_weight = outer_sum(token_rows, grad_qkv)
        column_sums = jnp.sum(grad_qkv.astype(jnp.float32), 0)
        grad_tokens = (grad_first_in + back_dot(grad_qkv, qkv_full)).astype(jnp.bfloat16)
        parts = (
            grad_qkv_weight,
            grad_out_weight,
            grad_up_weight,
            grad_down_weight,
            column_sums[:D],
            column_sums[2 * D :],
            grad_out_bias,
            grad_gain_one,
            grad_shift_one,
            grad_up_bias,
            grad_down_bias,
            grad_gain_two,
            grad_shift_two,
        )
        shares = (
            lax.psum_scatter(parts[0], ("ctx", "fsdp"), scatter_dimension=0, tiled=True),
            lax.psum_scatter(parts[1], ("ctx", "fsdp"), scatter_dimension=0, tiled=True),
            lax.psum_scatter(parts[2], ("ctx", "fsdp"), scatter_dimension=0, tiled=True),
            lax.psum_scatter(parts[3], ("ctx", "fsdp"), scatter_dimension=0, tiled=True),
            lax.psum_scatter(parts[4], ("ctx", "fsdp"), scatter_dimension=0, tiled=True),
            lax.psum_scatter(parts[5], ("ctx", "fsdp"), scatter_dimension=0, tiled=True),
            lax.psum_scatter(parts[6], ("ctx", "fsdp"), scatter_dimension=0, tiled=True),
            lax.psum_scatter(parts[7], ("ctx", "fsdp"), scatter_dimension=0, tiled=True),
            lax.psum_scatter(parts[8], ("ctx", "fsdp"), scatter_dimension=0, tiled=True),
            lax.psum_scatter(parts[9], ("ctx", "fsdp"), scatter_dimension=0, tiled=True),
            lax.psum_scatter(parts[10], ("ctx", "fsdp"), scatter_dimension=0, tiled=True),
            lax.psum_scatter(parts[11], ("ctx", "fsdp"), scatter_dimension=0, tiled=True),
            lax.psum_scatter(parts[12], ("ctx", "fsdp"), scatter_dimension=0, tiled=True),
        )
        totals = (
            shares
            if totals is None
            else tuple((held + added for held, added in zip(totals, shares)))
        )
        positions = jnp.arange(order_row.shape[0], dtype=jnp.int32)
        inverse_order = jnp.sum(
            jnp.where(order_row[None, :] == positions[:, None], positions[None, :], 0), 1
        )
        home_wanted = jnp.take(inverse_order, mine)
        (home_grad,) = block_picker(
            home_wanted, (empty_blocks,), (lax.all_gather(grad_tokens, "ctx", axis=0, tiled=True),)
        )
        grad_list.append(home_grad.reshape(rows, D))
    mixed_out = jnp.stack(mixed_list)[:, None]
    grad_out = jnp.stack(grad_list)[:, None]
    return (
        mixed_out,
        grad_out,
        totals[0],
        totals[1],
        totals[2],
        totals[3],
        totals[4],
        totals[5],
        totals[6],
        totals[7],
        totals[8],
        totals[9],
        totals[10],
        totals[11],
        totals[12],
    )


def solution(mesh):
    placed = (
        P(None, "fsdp", "ctx", None),
        P(None, "fsdp", "ctx", None),
        P(None, "fsdp", None),
        P(None, "fsdp", None),
        P("fsdp", None),
        P("fsdp", None),
        P("fsdp", None),
        P("fsdp", None),
        P("fsdp"),
        P("fsdp"),
        P("fsdp"),
        P("fsdp"),
        P("fsdp"),
        P("fsdp"),
        P("fsdp"),
        P("fsdp"),
        P("fsdp"),
    )
    return jax.shard_map(
        on_device,
        mesh=mesh,
        in_specs=placed,
        out_specs=(
            P(None, "fsdp", "ctx", None),
            P(None, "fsdp", "ctx", None),
            P(("ctx", "fsdp"), None),
            P(("ctx", "fsdp"), None),
            P(("ctx", "fsdp"), None),
            P(("ctx", "fsdp"), None),
            P(("ctx", "fsdp")),
            P(("ctx", "fsdp")),
            P(("ctx", "fsdp")),
            P(("ctx", "fsdp")),
            P(("ctx", "fsdp")),
            P(("ctx", "fsdp")),
            P(("ctx", "fsdp")),
            P(("ctx", "fsdp")),
            P(("ctx", "fsdp")),
        ),
        check_vma=False,
    )
```

profile of v0, /device:TPU:0, one launch (start us, length us, event | category | flops | bytes accessed | tf_op | source)
XLA Modules:
  0.0 2330.2 jit_solution(15622117317376291300)
XLA Ops:
  11.1 12.6 all-gather.3
  23.7 7.6 all-gather.2
  32.1 17.8 all-gather.43.cloned.1.call-done
  52.9 114.0 %all-gather.23.cloned.1.call-done = bf16[1024,3072]{1,0:T(8,128)(2,1)} async-done(((bf16[256,3072]{1,0:T(8,128)(2,1)}), bf16[1024,3072]{1,0:T(8,128)(2,1)}) %all-gather.23.cloned.1.call-update) | async-done | bytes 6291472 | tf_op jit(solution)/shard_map/all_gather | solution.py:220
  174.0 30.4 %all-gather.45.cloned.1.call-done = bf16[1,1,2048,1024]{3,2,1,0:T(8,128)(2,1)} async-done(((bf16[1,1,256,1024]{3,2,1,0:T(8,128)(2,1)}), bf16[1,1,2048,1024]{3,2,1,0:T(8,128)(2,1)}) %all-gather.45.cloned.1.call-update) | async-done | bytes 4194320 | tf_op jit(solution)/shard_map/all_gather | solution.py:215
  215.7 10.9 all-gather.7
  226.6 11.9 all_gather.103
  238.5 7.6 all-gather.4
  246.3 9.6 all-gather.6
  255.9 7.6 all-gather.5
  263.5 9.6 all-gather.8
  296.0 67.4 %while.72 = (s32[]{:T(128)}, f32[16,256]{1,0:T(8,128)S(1)}, f32[16,256]{1,0:T(8,128)S(1)}, f32[256,16,64]{0,2,1:T(8,128)}, s32[256]{0:T(256)S(1)}, /*index=5*/s3...) while((s32[]{:T(128)}, f32[16,256]{1,0:T(8,128)S(1)}, ...), condition=%wide.region_4.7_spmd.clone, body=%wide.region_1.6_spmd.clone.sunk | while | flops 565075968 | bytes 68426976 | solution.py:105
  374.5 144.0 %all-gather.31.cloned.1.call-done = bf16[1024,4096]{1,0:T(8,128)(2,1)} async-done(((bf16[256,4096]{1,0:T(8,128)(2,1)}), bf16[1024,4096]{1,0:T(8,128)(2,1)}) %all-gather.31.cloned.1.call-update) | async-done | bytes 8388624 | tf_op jit(solution)/shard_map/all_gather | solution.py:222
  518.4 16.3 multiply_convert_fusion.1
  534.7 133.2 %all-gather.33.cloned.1.call-done = bf16[4096,1024]{1,0:T(8,128)(2,1)} async-done(((bf16[1024,1024]{1,0:T(8,128)(2,1)}), bf16[4096,1024]{1,0:T(8,128)(2,1)}) %all-gather.33.cloned.1.call-update) | async-done | bytes 8388624 | tf_op jit(solution)/shard_map/all_gather | solution.py:223
  675.6 29.6 %all-gather.37.cloned.1.call-done = bf16[2048,1024]{1,0:T(8,128)(2,1)} async-done(((bf16[256,1024]{1,0:T(8,128)(2,1)}), bf16[2048,1024]{1,0:T(8,128)(2,1)}) %all-gather.37.cloned.1.call-update) | async-done | bytes 4194320 | tf_op jit(solution)/shard_map/all_gather | solution.py:271
  711.7 67.1 %while.73 = (s32[]{:T(128)}, f32[16,256]{1,0:T(8,128)S(1)}, f32[16,256]{1,0:T(8,128)S(1)}, f32[256,16,64]{0,2,1:T(8,128)}, s32[256]{0:T(256)S(1)}, /*index=5*/s3...) while((s32[]{:T(128)}, f32[16,256]{1,0:T(8,128)S(1)}, ...), condition=%wide.region_13.16_spmd.clone, body=%wide.region_10.15_spmd.clone.sunk | while | flops 565075968 | bytes 68426976 | solution.py:105
  783.0 16.0 multiply_convert_fusion
  805.9 12.2 convert_reduce_fusion.1
  825.6 11.8 convert_reduce_fusion
  837.4 8.6 convert_reduce_fusion.9
  857.8 99.0 %while.75 = (s32[]{:T(128)}, f32[256,16,64]{0,2,1:T(8,128)S(1)}, f32[2048,1024]{0,1:T(8,128)}, f32[2048,1024]{0,1:T(8,128)}, bf16[2048,1024]{0,1:T(8,128)(2,1)},...) while((s32[]{:T(128)}, f32[256,16,64]{0,2,1:T(8,128)S(1)}, ...), condition=%wide.region_35.38_spmd.clone, body=%wide.region_34.37_spmd.clone.sunk | while | flops 1371144192 | bytes 116841752 | solution.py:161
  982.2 108.1 %while.74 = (s32[]{:T(128)}, f32[256,16,64]{0,2,1:T(8,128)}, f32[2048,1024]{0,1:T(8,128)}, f32[2048,1024]{0,1:T(8,128)}, bf16[2048,1024]{0,1:T(8,128)(2,1)}, /*i...) while((s32[]{:T(128)}, f32[256,16,64]{0,2,1:T(8,128)}, ...), condition=%wide.region_25.28_spmd.clone, body=%wide.region_24.27_spmd.clone.sunk | while | flops 1371144192 | bytes 116841752 | solution.py:161
  1110.0 37.5 %reduce-scatter.11.cloned.1.call-done = bf16[256,1024]{0,1:T(8,128)(2,1)} async-done(((bf16[2048,1024]{0,1:T(8,128)(2,1)}), bf16[256,1024]{0,1:T(8,128)(2,1)}) %reduce-scatter.11.cloned.1.call-update) | async-done | bytes 524304 | tf_op jit(solution)/shard_map/reduce_scatter | solution.py:371
  1147.5 54.9 %reduce-scatter.9.cloned.1.call-done = bf16[256,1024]{0,1:T(8,128)(2,1)} async-done(((bf16[2048,1024]{0,1:T(8,128)(2,1)}), bf16[256,1024]{0,1:T(8,128)(2,1)}) %reduce-scatter.9.cloned.1.call-update) | async-done | bytes 524304 | tf_op jit(solution)/shard_map/reduce_scatter | solution.py:368
  1229.6 10.0 convolution_add_fusion.1
  1244.1 9.8 convolution_add_fusion
  1260.1 40.5 %all-reduce.9 = (f32[1024]{0:T(1024)S(1)}, f32[1024]{0:T(1024)S(1)}, f32[1024]{0:T(1024)S(1)}, f32[1024]{0:T(1024)S(1)}, f32[1024]{0:T(1024)S(1)}, /*index=5*/f3...) all-reduce(f32[1024]{0:T(1024)S(1)} %get-tuple-element.1270, ...), channel_id=25, replica_groups=mesh['ctx'=8,'fsdp'=4] {'ctx','fsdp'}, use_global_device_ids=true, to_apply=%region_47.50.clone | all-reduce | flops 12288 | bytes 98304
  1312.8 118.1 %reduce-scatter.19.cloned.1.call-done = f32[32,1024]{1,0:T(8,128)} async-done(((f32[1024,1024]{1,0:T(8,128)}), f32[32,1024]{1,0:T(8,128)}) %reduce-scatter.19.cloned.1.call-update) | async-done | bytes 131088 | tf_op jit(solution)/shard_map/reduce_scatter | solution.py:398
  1430.8 160.8 %reduce-scatter.17.cloned.1.call-done = f32[32,3072]{1,0:T(8,128)} async-done(((f32[1024,3072]{1,0:T(8,128)}), f32[32,3072]{1,0:T(8,128)}) %reduce-scatter.17.cloned.1.call-update) | async-done | bytes 393232 | tf_op jit(solution)/shard_map/reduce_scatter | solution.py:397
  1591.6 366.3 %reduce-scatter.21.cloned.1.call-done = f32[32,4096]{1,0:T(8,128)} async-done(((f32[1024,4096]{1,0:T(8,128)}), f32[32,4096]{1,0:T(8,128)}) %reduce-scatter.21.cloned.1.call-update) | async-done | bytes 524304 | tf_op jit(solution)/shard_map/reduce_scatter | solution.py:399
  1957.9 365.0 %reduce-scatter.23.cloned.1.call-done = f32[128,1024]{1,0:T(8,128)} async-done(((f32[4096,1024]{1,0:T(8,128)}), f32[128,1024]{1,0:T(8,128)}) %reduce-scatter.23.cloned.1.call-update) | async-done | bytes 524304 | tf_op jit(solution)/shard_map/reduce_scatter | solution.py:400
  (586 shorter events, 538.6 us)
Async XLA Ops:
  7.2 42.7 %all-gather.43.cloned.1.call-start = ((), (), s32[]{:S(2)}) async-start(), calls=%async_computation.22 | async-start | bytes 4718592 | tf_op jit(solution)/shard_map/all_gather | solution.py:215
  9.5 157.4 %all-gather.23.cloned.1.call-start = ((), (), s32[]{:S(2)}) async-start(), calls=%async_computation.8 | async-start | bytes 7864320 | tf_op jit(solution)/shard_map/all_gather | solution.py:220
  10.3 194.1 %all-gather.45.cloned.1.call-start = ((), (), s32[]{:S(2)}) async-start(), calls=%async_computation.23 | async-start | bytes 4718592 | tf_op jit(solution)/shard_map/all_gather | solution.py:215
  11.0 271.9 %all-gather.25.cloned.1.call-start = ((), (), s32[]{:S(2)}) async-start(), calls=%async_computation.9 | async-start | bytes 4718592 | tf_op jit(solution)/shard_map/all_gather | solution.py:270
  31.4 141.9 %copy-start.79 = (s32[1024]{0:T(1024)}, s32[1024]{0:T(1024)S(1)}, u32[]{:S(2)}) copy-start(s32[1024]{0:T(1024)S(1)} %pad_clamp_fusion.4) | copy-start | bytes 12292
  31.4 140.1 %copy-start.2 = (s32[16]{0:T(128)}, s32[16]{0:T(128)S(1)}, u32[]{:S(2)}) copy-start(s32[16]{0:T(128)S(1)} %get-tuple-element.1275) | copy-start | bytes 196
  31.4 141.9 %copy-start.4 = (s32[16]{0:T(128)}, s32[16]{0:T(128)S(1)}, u32[]{:S(2)}) copy-start(s32[16]{0:T(128)S(1)} %get-tuple-element.1276) | copy-start | bytes 196
  52.9 318.7 %copy-start.31 = (bf16[2,128,1024]{2,1,0:T(8,128)(2,1)}, bf16[2,128,1024]{2,1,0:T(8,128)(2,1)S(1)}, u32[]{:S(2)}) copy-start(bf16[2,128,1024]{2,1,0:T(8,128)(2,1)S(1)} %select_select_fusion.3) | copy-start | bytes 1572868
  172.6 116.8 %all-gather.27.cloned.1.call-start = ((), (), s32[]{:S(2)}) async-start(), calls=%async_computation.10 | async-start | bytes 4718592 | tf_op jit(solution)/shard_map/all_gather | solution.py:271
  173.2 190.2 %all-gather.35.cloned.1.call-start = ((), (), s32[]{:S(2)}) async-start(), calls=%async_computation.14 | async-start | bytes 4718592 | tf_op jit(solution)/shard_map/all_gather | solution.py:270
  213.3 158.2 %all-gather.29.cloned.1.call-start = ((), (), s32[]{:S(2)}) async-start(), calls=%async_computation.11 | async-start | bytes 2621440 | tf_op jit(solution)/shard_map/all_gather | solution.py:221
  214.1 304.3 %all-gather.31.cloned.1.call-start = ((), (), s32[]{:S(2)}) async-start(), calls=%async_computation.12 | async-start | bytes 10485760 | tf_op jit(solution)/shard_map/all_gather | solution.py:222
  214.8 453.1 %all-gather.33.cloned.1.call-start = ((), (), s32[]{:S(2)}) async-start(), calls=%async_computation.13 | async-start | bytes 10485760 | tf_op jit(solution)/shard_map/all_gather | solution.py:223
  215.5 489.6 %all-gather.37.cloned.1.call-start = ((), (), s32[]{:S(2)}) async-start(), calls=%async_computation.15 | async-start | bytes 4718592 | tf_op jit(solution)/shard_map/all_gather | solution.py:271
  255.8 543.2 %copy-start.57 = (f32[4,1,256]{2,1,0:T(1,128)}, f32[4,1,256]{2,1,0:T(1,128)S(1)}, u32[]{:S(2)}) copy-start(f32[4,1,256]{2,1,0:T(1,128)S(1)} %convert_element_type.318) | copy-start | bytes 12292
  263.4 582.6 %copy-start.55 = (f32[4,1,256]{2,1,0:T(1,128)}, f32[4,1,256]{2,1,0:T(1,128)S(1)}, u32[]{:S(2)}) copy-start(f32[4,1,256]{2,1,0:T(1,128)S(1)} %convert_element_type.317) | copy-start | bytes 12292
  282.6 819.9 %reduce-scatter.15.cloned.1.call-start = ((), (), s32[]{:S(2)}) async-start(), calls=%async_computation.20 | async-start | bytes 4718592 | tf_op jit(solution)/shard_map/reduce_scatter | solution.py:371
  371.5 163.2 %copy-start.37 = (bf16[256,16,64]{0,2,1:T(8,128)(2,1)}, bf16[256,16,64]{0,2,1:T(8,128)(2,1)S(1)}, u32[]{:S(2)}) copy-start(bf16[256,16,64]{0,2,1:T(8,128)(2,1)S(1)} %fusion.102) | copy-start | bytes 1572868
  374.2 293.7 %copy-start.17 = (f32[256,1024]{1,0:T(8,128)}, f32[256,1024]{1,0:T(8,128)S(1)}, u32[]{:S(2)}) copy-start(f32[256,1024]{1,0:T(8,128)S(1)} %get-tuple-element.1290) | copy-start | bytes 3145732
  374.2 463.2 %copy-start.65 = (f32[256]{0:T(256)}, f32[256]{0:T(256)S(1)}, u32[]{:S(2)}) copy-start(f32[256]{0:T(256)S(1)} %broadcast_multiply_fusion.11) | copy-start | bytes 3076
  374.4 463.0 %copy-start.77 = (f32[256]{0:T(256)}, f32[256]{0:T(256)S(1)}, u32[]{:S(2)}) copy-start(f32[256]{0:T(256)S(1)} %add_rsqrt_fusion.3) | copy-start | bytes 3076
  711.7 68.4 %copy-start.27 = (bf16[2,128,1024]{2,1,0:T(8,128)(2,1)S(1)}, bf16[2,128,1024]{2,1,0:T(8,128)(2,1)}, u32[]{:S(2)}) copy-start(bf16[2,128,1024]{2,1,0:T(8,128)(2,1)} %copy-done.26) | copy-start | bytes 1572868
  962.9 139.7 %reduce-scatter.13.cloned.1.call-start = ((), (), s32[]{:S(2)}) async-start(), calls=%async_computation.19 | async-start | bytes 4718592 | tf_op jit(solution)/shard_map/reduce_scatter | solution.py:368
  973.5 174.0 %reduce-scatter.11.cloned.1.call-start = ((), (), s32[]{:S(2)}) async-start(), calls=%async_computation.17 | async-start | bytes 4718592 | tf_op jit(solution)/shard_map/reduce_scatter | solution.py:371
  1096.3 106.1 %reduce-scatter.9.cloned.1.call-start = ((), (), s32[]{:S(2)}) async-start(), calls=%async_computation.16 | async-start | bytes 4718592 | tf_op jit(solution)/shard_map/reduce_scatter | solution.py:368
  1102.4 203.4 %all-gather.41.cloned.1.call-start = ((), (), s32[]{:S(2)}) async-start(), calls=%async_computation.21 | async-start | bytes 4718592 | tf_op jit(solution)/shard_map/all_gather | solution.py:422
  1109.6 199.0 %all-gather.39.cloned.1.call-start = ((), (), s32[]{:S(2)}) async-start(), calls=%async_computation.18 | async-start | bytes 4718592 | tf_op jit(solution)/shard_map/all_gather | solution.py:422
  1110.0 103.5 %copy-start.35 = (bf16[256,16,64]{0,2,1:T(8,128)(2,1)}, bf16[256,16,64]{0,2,1:T(8,128)(2,1)S(1)}, u32[]{:S(2)}) copy-start(bf16[256,16,64]{0,2,1:T(8,128)(2,1)S(1)} %convert.16) | copy-start | bytes 1572868
  1208.5 222.3 %reduce-scatter.19.cloned.1.call-start = ((), (), s32[]{:S(2)}) async-start(), calls=%async_computation.25 | async-start | bytes 4325376 | tf_op jit(solution)/shard_map/reduce_scatter | solution.py:398
  1213.4 378.2 %reduce-scatter.17.cloned.1.call-start = ((), (), s32[]{:S(2)}) async-start(), calls=%async_computation.24 | async-start | bytes 12976128 | tf_op jit(solution)/shard_map/reduce_scatter | solution.py:397
  1224.0 733.8 %reduce-scatter.21.cloned.1.call-start = ((), (), s32[]{:S(2)}) async-start(), calls=%async_computation.26 | async-start | bytes 17301504 | tf_op jit(solution)/shard_map/reduce_scatter | solution.py:399
  1239.6 1083.3 %reduce-scatter.23.cloned.1.call-start = ((), (), s32[]{:S(2)}) async-start(), calls=%async_computation.27 | async-start | bytes 17301504 | tf_op jit(solution)/shard_map/reduce_scatter | solution.py:400
  (106 other events, 1004.2 us)
Sparse Core Ops, SparseCore 0:
  10.5 39.4 all-gather.42
  51.5 115.3 all-gather.22
  169.4 34.9 all-gather.44
  206.7 36.7 all-gather.24
  245.7 36.7 all-gather.26
  284.2 36.7 all-gather.34
  322.6 45.9 all-gather.28
  370.1 148.2 all-gather.30
  520.0 147.8 all-gather.32
  670.2 34.9 all-gather.36
  963.0 51.3 reduce-scatter.14
  1017.9 51.3 reduce-scatter.12
  1096.4 51.0 reduce-scatter.10
  1151.0 51.3 reduce-scatter.8
  1204.7 36.6 all-gather.40
  1243.2 37.2 all-gather.38
  1283.2 147.5 reduce-scatter.18
  1437.3 154.2 reduce-scatter.16
  1594.6 363.2 reduce-scatter.20
  1960.7 362.1 reduce-scatter.22
where the time goes:
time: 2340 us; the launch traced here: 2330 us
  waiting for transfers between devices  1580 us (68%)
  matrix products  361 us (15%)
  local copies, waits for them, and re-layouts  128 us (5%)
  blocking collectives  125 us (5%)
  other arithmetic  121 us (5%)
    reduce_scatter x1, waiting for transfers between devices, on_device(): lax.psum_scatter(parts[2], ('ctx', 'fsdp'), scatter_dimension=0, tiled=True)  366 us
    reduce_scatter x1, waiting for transfers between devices, on_device(): lax.psum_scatter(parts[3], ('ctx', 'fsdp'), scatter_dimension=0, tiled=True)  365 us
    reduce_scatter x1, waiting for transfers between devices, on_device(): lax.psum_scatter(parts[0], ('ctx', 'fsdp'), scatter_dimension=0, tiled=True)  161 us
    all_gather x1, waiting for transfers between devices, on_device(): lax.all_gather(shards[2], 'fsdp', axis=0, tiled=True)  144 us
    all_gather x1, waiting for transfers between devices, on_device(): lax.all_gather(shards[3], 'fsdp', axis=0, tiled=True)  133 us
    reduce_scatter x1, waiting for transfers between devices, on_device(): lax.psum_scatter(parts[1], ('ctx', 'fsdp'), scatter_dimension=0, tiled=True)  118 us
    all_gather x1, waiting for transfers between devices, on_device(): lax.all_gather(shards[0], 'fsdp', axis=0, tiled=True)  114 us
    dot_general x8, matrix products, back_dot(): lax.dot_general(left_rows, weight, (((1,), (1,)), ((), ())), preferred_el...  56.4 us
  transfers between devices with their start and end apart: 20, of which 12 were waited for; matrix products, arithmetic and copies ran while one was open for 15% of the time, Pallas kernels for 0%

commit v1 on v0

v1 whole, which is shorter than its diff:
```python
from functools import partial
import math

import jax
import jax.numpy as jnp
from jax import lax
from jax.experimental import pallas as pl
from jax.experimental.pallas import tpu as pltpu
from jax.sharding import PartitionSpec as P

D = 1024
H = 16
HD = 64
BLK = 128
MB = 2

NEGATIVE = -1e30
EPSILON = 1e-05
BF = jnp.bfloat16
F32 = jnp.float32


def contract(a, b, ca, cb):
    return lax.dot_general(a, b, (((ca,), (cb,)), ((), ())), preferred_element_type=F32)


def norm_forward(values_in, gain_vec, shift_vec):
    center = values_in - jnp.mean(values_in, -1, keepdims=True)
    inverse = lax.rsqrt(jnp.mean(center * center, -1, keepdims=True) + EPSILON)
    normed = center * inverse
    return (normed * gain_vec + shift_vec, normed, inverse)


def norm_backward(grad_out, normed, inverse, gain_vec):
    grad_norm = grad_out * gain_vec
    return inverse * (
        grad_norm
        - jnp.mean(grad_norm, -1, keepdims=True)
        - normed * jnp.mean(grad_norm * normed, -1, keepdims=True)
    )


def hop(value, mask):
    count = lax.axis_size("ctx")
    return lax.ppermute(value, "ctx", [(i, i ^ mask) for i in range(count)])


VMEM = pl.BlockSpec(memory_space=pltpu.VMEM)
SMEM = pl.BlockSpec(memory_space=pltpu.SMEM)
ANY = pl.BlockSpec(memory_space=pl.ANY)


def params(mib):
    return pltpu.CompilerParams(vmem_limit_bytes=mib << 20)


def struct(shape, dtype):
    return jax.ShapeDtypeStruct(shape, dtype)


def segment_lanes(first, rows, split, is_query):
    position = first + lax.broadcasted_iota(jnp.int32, (rows, HD), 0)
    lane = lax.broadcasted_iota(jnp.int32, (rows, HD), 1)
    second = (position >= split).astype(jnp.int32)
    if is_query:
        return jnp.where(lane == 1 - second, NEGATIVE, 0.0).astype(BF)
    return jnp.where(lane == second, 1.0, 0.0).astype(BF)


def key_range(q0, bq, split, bk, total):
    low = jnp.where(q0 >= split, split // bk, 0)
    high = jnp.where(q0 + bq <= split, (split + bk - 1) // bk, total // bk)
    return low, high


def attention_forward_kernel(scal, qkv, out, out_t, lse, qa, ka, vt, sc, *, heads, chunk, bq, bk):
    total = qkv.shape[0]
    chunks = total // chunk
    width = heads * HD
    split = scal[0]
    top = scal[1]
    for m in range(chunks):
        pos = pl.multiple_of(scal[2 + m], chunk)
        rows = slice(m * chunk, (m + 1) * chunk)
        qtail = segment_lanes(pos, chunk, split, True)
        ktail = segment_lanes(pos, chunk, split, False)
        for h in range(heads):
            q = qkv[rows, h * HD : (h + 1) * HD]
            k = qkv[rows, width + h * HD : width + (h + 1) * HD]
            q = (q.astype(F32) * 0.125).astype(BF)
            qa[h, pl.ds(pos, chunk), :] = jnp.concatenate([q, qtail], 1)
            ka[h, pl.ds(pos, chunk), :] = jnp.concatenate([k, ktail], 1)
        vt[:, pl.ds(pos, chunk)] = qkv[rows, 2 * width : 3 * width].T

    def q_step(qi, _):
        q0 = pl.multiple_of(qi * bq, bq)
        low, high = key_range(q0, bq, split, bk, total)

        def max_step(ki, carry):
            k0 = pl.multiple_of(ki * bk, bk)
            result = []
            for h in range(heads):
                st = contract(ka[h, pl.ds(k0, bk), :], qa[h, pl.ds(q0, bq), :], 1, 1)
                sc[h, pl.ds(k0, bk), :] = st
                result.append(jnp.maximum(carry[h], jnp.max(st.reshape(bk // 8, 8, bq), 0)))
            return tuple(result)

        start = tuple(jnp.full((8, bq), NEGATIVE, F32) for _ in range(heads))
        peaks = lax.fori_loop(low, high, max_step, start)
        peaks = [jnp.max(m, 0, keepdims=True) for m in peaks]

        def k_step(ki, carry):
            k0 = pl.multiple_of(ki * bk, bk)
            result = []
            for h in range(heads):
                total_p, acc = carry[2 * h : 2 * h + 2]
                p = jnp.exp(sc[h, pl.ds(k0, bk), :] - peaks[h])
                total_p = total_p + jnp.sum(p.reshape(bk // 8, 8, bq), 0)
                acc = acc + contract(
                    vt[h * HD : (h + 1) * HD, pl.ds(k0, bk)], p.astype(BF), 1, 0
                )
                result += [total_p, acc]
            return tuple(result)

        start = []
        for h in range(heads):
            start += [jnp.zeros((8, bq), F32), jnp.zeros((HD, bq), F32)]
        done = lax.fori_loop(low, high, k_step, tuple(start))
        pieces = []
        for h in range(heads):
            denom = jnp.sum(done[2 * h], 0, keepdims=True)
            pieces.append(done[2 * h + 1] / denom)
            lse[h : h + 1, pl.ds(q0, bq)] = peaks[h] + jnp.log(denom)
        turned = jnp.concatenate(pieces, 0)
        out_t[:, pl.ds(q0, bq)] = turned
        low_rows = turned.T.astype(BF)
        half = chunks // 2
        for i in range(bq // chunk):
            c = q0 // chunk + i
            out[c % half, (c // half) ^ top] = low_rows[i * chunk : (i + 1) * chunk]
        return 0

    lax.fori_loop(0, total // bq, q_step, 0)


def attention_forward(scal, qkv, chunk, bq=512, bk=512):
    total, triple = qkv.shape
    width = triple // 3
    heads = width // HD
    half = total // chunk // 2
    return pl.pallas_call(
        partial(attention_forward_kernel, heads=heads, chunk=chunk, bq=bq, bk=bk),
        out_shape=(
            struct((half, 2, chunk, width), BF),
            struct((width, total), F32),
            struct((heads, total), F32),
        ),
        in_specs=[SMEM, VMEM],
        out_specs=(VMEM, VMEM, VMEM),
        scratch_shapes=[
            pltpu.VMEM((heads, total, 128), BF),
            pltpu.VMEM((heads, total, 128), BF),
            pltpu.VMEM((width, total), BF),
            pltpu.VMEM((heads, total, bq), F32),
        ],
        compiler_params=params(56),
        cost_estimate=pl.CostEstimate(
            flops=8 * total * total * width, bytes_accessed=5 * total * width * 2, transcendentals=0
        ),
        name="attention_forward",
    )(scal, qkv)


def attention_backward_kernel(
    scal, qkv, grad, out_t, lse, dqkv, qa, ka, kt, va, ga, gt, dkv, dq, *, heads, chunk, bq, bk
):
    total = qkv.shape[0]
    chunks = total // chunk
    half = chunks // 2
    width = heads * HD
    split = scal[0]
    top = scal[1]
    blank = jnp.zeros((chunk, HD), BF)
    for m in range(chunks):
        pos = pl.multiple_of(scal[2 + m], chunk)
        rows = slice(m * chunk, (m + 1) * chunk)
        qtail = segment_lanes(pos, chunk, split, True)
        ktail = segment_lanes(pos, chunk, split, False)
        for h in range(heads):
            q = qkv[rows, h * HD : (h + 1) * HD]
            k = qkv[rows, width + h * HD : width + (h + 1) * HD]
            v = qkv[rows, 2 * width + h * HD : 2 * width + (h + 1) * HD]
            q = (q.astype(F32) * 0.125).astype(BF)
            qa[h, pl.ds(pos, chunk), :] = jnp.concatenate([q, qtail], 1)
            ka[h, pl.ds(pos, chunk), :] = jnp.concatenate([k, ktail], 1)
            va[h, pl.ds(pos, chunk), :] = jnp.concatenate([v, blank], 1)
        kt[:, pl.ds(pos, chunk)] = qkv[rows, width : 2 * width].T
    for j in range(half):
        for s in range(2):
            pos = pl.multiple_of((j + half * (s ^ top)) * chunk, chunk)
            for h in range(heads):
                g = grad[j, s, :, h * HD : (h + 1) * HD]
                ga[h, pl.ds(pos, chunk), :] = jnp.concatenate([g, blank], 1)
            gt[:, pl.ds(pos, chunk)] = grad[j, s].T
    dkv[...] = jnp.zeros_like(dkv)

    def q_step(qi, _):
        q0 = pl.multiple_of(qi * bq, bq)
        low, high = key_range(q0, bq, split, bk, total)
        product = gt[:, pl.ds(q0, bq)].astype(F32) * out_t[:, pl.ds(q0, bq)]
        delta = [jnp.sum(product[h * HD : (h + 1) * HD], 0, keepdims=True) for h in range(heads)]
        held_lse = lse[:, pl.ds(q0, bq)]
        totals = [held_lse[h : h + 1] for h in range(heads)]

        def k_step(ki, carry):
            k0 = pl.multiple_of(ki * bk, bk)
            result = []
            for h in range(heads):
                q = qa[h, pl.ds(q0, bq), :]
                g = ga[h, pl.ds(q0, bq), :]
                st = contract(ka[h, pl.ds(k0, bk), :], q, 1, 1)
                p = jnp.exp(st - totals[h])
                dp = contract(va[h, pl.ds(k0, bk), :], g, 1, 1)
                ds = (p * (dp - delta[h]) * 0.125).astype(BF)
                dkv[0, h, pl.ds(k0, bk), :] += contract(ds, q, 1, 0)
                dkv[1, h, pl.ds(k0, bk), :] += contract(p.astype(BF), g, 1, 0)
                result.append(
                    carry[h] + contract(kt[h * HD : (h + 1) * HD, pl.ds(k0, bk)], ds, 1, 0)
                )
            return tuple(result)

        start = tuple(jnp.zeros((HD, bq), F32) for _ in range(heads))
        turned = lax.fori_loop(low, high, k_step, start)
        dq[pl.ds(q0, bq), :] = jnp.concatenate(turned, 0).T.astype(BF)
        return 0

    lax.fori_loop(0, total // bq, q_step, 0)
    for m in range(chunks):
        pos = pl.multiple_of(scal[2 + m], chunk)
        rows = slice(m * chunk, (m + 1) * chunk)
        dqkv[rows, 0:width] = dq[pl.ds(pos, chunk), :]
        for h in range(0, heads, 2):
            for part, gain in ((0, 8.0), (1, 1.0)):
                pair = [dkv[part, h + e, pl.ds(pos, chunk), :][:, :HD] for e in range(2)]
                base = (1 + part) * width + h * HD
                dqkv[rows, base : base + 2 * HD] = (jnp.concatenate(pair, 1) * gain).astype(BF)


def attention_backward(scal, qkv, grad, out_t, lse, chunk, bq=512, bk=512):
    total, triple = qkv.shape
    width = triple // 3
    heads = width // HD
    wide = pltpu.VMEM((heads, total, 128), BF)
    return pl.pallas_call(
        partial(attention_backward_kernel, heads=heads, chunk=chunk, bq=bq, bk=bk),
        out_shape=struct((total, triple), BF),
        in_specs=[SMEM, VMEM, VMEM, VMEM, VMEM],
        out_specs=VMEM,
        scratch_shapes=[
            wide,
            wide,
            pltpu.VMEM((width, total), BF),
            wide,
            wide,
            pltpu.VMEM((width, total), BF),
            pltpu.VMEM((2, heads, total, 128), F32),
            pltpu.VMEM((total, width), BF),
        ],
        compiler_params=params(56),
        cost_estimate=pl.CostEstimate(
            flops=16 * total * total * width, bytes_accessed=9 * total * width * 2, transcendentals=0
        ),
        name="attention_backward",
    )(scal, qkv, grad, out_t, lse)


PIECES = (0, 2, 4, 6, 1, 3, 5, 7)
CHUNKS = (0, 4, 2, 6, 1, 5, 3, 7)


def start_all(copies):
    for copy in copies:
        copy.start()


def wait_all(copies):
    for copy in copies:
        copy.wait()


def carve_kernel(
    scal, tokens, cot, w_qkv, w_out, w_up, w_down, small,
    own, other, cot_own, cot_other, pack, up_slice, down_slice, sems,
):
    me, low, top = scal[0], scal[1], scal[2]
    pairs = []
    for k in range(3):
        columns = pl.ds(pl.multiple_of(k * D + low * 256, 256), 256)
        pairs.append((w_qkv.at[:, columns], pack.at[0:256, 256 * k : 256 * (k + 1)]))
    pairs.append((small, pack.at[256:272, :]))
    pairs += [(tokens.at[top, 0], own), (tokens.at[1 - top, 0], other)]
    for k in range(4):
        columns = pl.ds(pl.multiple_of(k * D + me * 128, 128), 128)
        pairs.append((w_up.at[:, columns], up_slice.at[:, 128 * k : 128 * (k + 1)]))
    columns = pl.ds(pl.multiple_of(me * 128, 128), 128)
    pairs.append((w_out.at[:, columns], up_slice.at[:, 512:640]))
    pairs.append((w_down.at[columns, :], down_slice))
    pairs += [(cot.at[top, 0], cot_own), (cot.at[1 - top, 0], cot_other)]
    copies = [pltpu.make_async_copy(a, b, sems.at[i]) for i, (a, b) in enumerate(pairs)]
    start_all(copies)
    wait_all(copies)


def carve(scal, tokens, cot, w_qkv, w_out, w_up, w_down, small):
    rows = tokens.shape[2]
    return pl.pallas_call(
        carve_kernel,
        out_shape=tuple(struct((rows, D), BF) for _ in range(4))
        + (struct((272, 768), BF), struct((256, 640), BF), struct((128, D), BF)),
        in_specs=[SMEM] + [ANY] * 7,
        out_specs=(ANY,) * 7,
        scratch_shapes=[pltpu.SemaphoreType.DMA((14,))],
        compiler_params=params(16),
        cost_estimate=pl.CostEstimate(flops=0, bytes_accessed=8 << 20, transcendentals=0),
        name="carve",
    )(scal, tokens, cot, w_qkv, w_out, w_up, w_down, small)


def project_kernel(scal, vecs, packed, *rest):
    pieces, (qkv, x_all, weight, sems) = rest[:8], rest[8:]
    chunk = pieces[0].shape[0]
    loads = [
        pltpu.make_async_copy(packed.at[f, 0:256], weight.at[256 * f : 256 * (f + 1)], sems.at[f])
        for f in range(4)
    ]
    moves = [
        pltpu.make_async_copy(piece, x_all.at[m * chunk : (m + 1) * chunk], sems.at[4 + m])
        for m, piece in enumerate(pieces)
    ]
    start_all(loads)
    start_all(moves)
    here = pl.ds(pl.multiple_of(scal[1] * 256, 256), 256)
    bias = jnp.concatenate([vecs[0:1, here], jnp.zeros((1, 256), F32), vecs[1:2, here]], 1)
    wait_all(loads)
    for m in range(8):
        moves[m].wait()
        rows = slice(m * chunk, (m + 1) * chunk)
        qkv[rows, :] = (contract(x_all[rows, :], weight[...], 1, 0) + bias).astype(BF)


def project(scal, vecs, packed, pieces):
    chunk = pieces[0].shape[0]
    return pl.pallas_call(
        project_kernel,
        out_shape=(struct((8 * chunk, 768), BF), struct((8 * chunk, D), BF)),
        in_specs=[SMEM, VMEM, ANY] + [ANY] * 8,
        out_specs=(VMEM, VMEM),
        scratch_shapes=[pltpu.VMEM((D, 768), BF), pltpu.SemaphoreType.DMA((12,))],
        compiler_params=params(40),
        cost_estimate=pl.CostEstimate(
            flops=2 * 8 * chunk * D * 768, bytes_accessed=13 << 20, transcendentals=0
        ),
        name="project",
    )(scal, vecs, packed, *pieces)


def up_pairs(scal, pieces, local, first, width, held):
    pairs = []
    for m in range(8):
        for k in range(3):
            base = pl.multiple_of(scal[4 + k] * 256, 256)
            columns = slice(first, first + width)
            if m == 3:
                lower = pl.ds(base, 128)
                upper = pl.ds(pl.multiple_of(base + 128, 128), 128)
                pairs.append((pieces[3].at[k, :, columns], held.at[m, lower]))
                pairs.append((pieces[4].at[k, :, columns], held.at[m, upper]))
            elif m == 7:
                lower = pl.ds(base, 128)
                upper = pl.ds(pl.multiple_of(base + 128, 128), 128)
                pairs.append((pieces[8].at[k, :, columns], held.at[m, lower]))
                pairs.append((pieces[9].at[k, :, columns], held.at[m, upper]))
            else:
                piece = pieces[m if m < 3 else m + 1]
                pairs.append((piece.at[k, :, columns], held.at[m, pl.ds(base, 256)]))
    own = pl.ds(pl.multiple_of(scal[3] * 256, 256), 256)
    w_up, w_out = local
    for m in range(8):
        block = scal[0] ^ PIECES[m]
        if first < 512:
            for k in range(4):
                columns = pl.ds(pl.multiple_of(k * D + block * 128, 128), 128)
                pairs.append((w_up.at[:, columns], held.at[m, own, 128 * k : 128 * (k + 1)]))
        if first + width > 512:
            columns = pl.ds(pl.multiple_of(block * 128, 128), 128)
            pairs.append((w_out.at[:, columns], held.at[m, own, 512 - first : 640 - first]))
    return pairs


def per_piece(pairs, owners, sems, base=0):
    groups = [[] for _ in range(8)]
    for i, ((source, target), m) in enumerate(zip(pairs, owners)):
        groups[m].append(pltpu.make_async_copy(source, target, sems.at[base + i]))
    return groups


def up_owners(first, width):
    owners = []
    for m in range(8):
        owners += [m] * (6 if m in (3, 7) else 3)
    for m in range(8):
        owners += [m] * ((4 if first < 512 else 0) + (1 if first + width > 512 else 0))
    return owners


def down_pairs(pieces, held):
    pairs, owners = [], []
    places = {3: (3, 4), 7: (8, 9)}
    for m in range(8):
        if m in places:
            for f in range(4):
                for e in range(2):
                    rows = slice(128 * f + 64 * e, 128 * f + 64 * (e + 1))
                    pairs.append((pieces[places[m][e]].at[f], held.at[m, rows]))
                    owners.append(m)
        else:
            piece = pieces[m if m < 3 else m + 1]
            for f in range(4):
                pairs.append((piece.at[f], held.at[m, 128 * f : 128 * (f + 1)]))
                owners.append(m)
    return pairs, owners


def attention_out_kernel(scal, attn, x, vecs, w_up, w_out, *rest):
    pieces, (y1, y1_low, n1, r1, held, mixed, sems) = rest[:10], rest[10:]
    pairs = up_pairs(scal, pieces, (w_up, w_out), 512, 128, held)
    groups = per_piece(pairs, up_owners(512, 128), sems)
    for group in groups:
        start_all(group)
    for m, group in enumerate(groups):
        wait_all(group)
        part = contract(attn[0], held[m, 0:256, :], 1, 0)
        for t in range(1, 4):
            part = part + contract(attn[t], held[m, 256 * t : 256 * (t + 1), :], 1, 0)
        mixed[scal[0] ^ PIECES[m]] = part
    branch = jnp.concatenate([mixed[b] for b in range(8)], 1)
    h1 = x[...].astype(F32) + branch + vecs[2:3]
    out, normed, inverse = norm_forward(h1, vecs[3:4], vecs[4:5])
    y1[...] = out
    y1_low[...] = out.astype(BF)
    n1[...] = normed
    r1[...] = jnp.broadcast_to(inverse, r1.shape)


def attention_out(scal, attn, x_all, vecs, w_up, w_out, pieces):
    rows = attn.shape[1]
    return pl.pallas_call(
        attention_out_kernel,
        grid=(1,),
        out_shape=(
            struct((rows, D), F32),
            struct((rows, D), BF),
            struct((rows, D), F32),
            struct((rows, 128), F32),
        ),
        in_specs=[SMEM, VMEM, pl.BlockSpec((rows, D), lambda i: (0, 0)), VMEM] + [ANY] * 12,
        out_specs=(VMEM,) * 4,
        scratch_shapes=[
            pltpu.VMEM((8, D, 128), BF),
            pltpu.VMEM((8, rows, 128), F32),
            pltpu.SemaphoreType.DMA((len(up_owners(512, 128)),)),
        ],
        compiler_params=params(40),
        cost_estimate=pl.CostEstimate(
            flops=2 * rows * D * D, bytes_accessed=8 << 20, transcendentals=0
        ),
        name="attention_out",
    )(scal, attn, x_all, vecs, w_up, w_out, *pieces)


def up_kernel(scal, y1_low, up_bias, w_up, w_out, *rest):
    pieces, (act, slope, held, sems) = rest[:10], rest[10:]
    pairs = up_pairs(scal, pieces, (w_up, w_out), 0, 512, held)
    groups = per_piece(pairs, up_owners(0, 512), sems)
    for group in groups:
        start_all(group)
    for m, group in enumerate(groups):
        wait_all(group)
        b = scal[0] ^ PIECES[m]
        bias = up_bias[pl.ds(b, 1), :]
        for r in (slice(0, 256), slice(256, 512)):
            u = contract(y1_low[r, :], held[m], 1, 0) + bias
            cdf = 0.5 * (1.0 + lax.erf(u * (1.0 / math.sqrt(2.0))))
            density = jnp.exp(-0.5 * u * u) * (1.0 / math.sqrt(2.0 * math.pi))
            slope[b, r, :] = (cdf + u * density).astype(BF)
            act[b, r, :] = (u * cdf).astype(BF)


def feed_up(scal, y1_low, up_bias, w_up, w_out, pieces):
    rows = y1_low.shape[0]
    return pl.pallas_call(
        up_kernel,
        out_shape=(struct((8, rows, 512), BF), struct((8, rows, 512), BF)),
        in_specs=[SMEM, VMEM, VMEM] + [ANY] * 12,
        out_specs=(VMEM, VMEM),
        scratch_shapes=[
            pltpu.VMEM((8, D, 512), BF),
            pltpu.SemaphoreType.DMA((len(up_owners(0, 512)),)),
        ],
        compiler_params=params(48),
        cost_estimate=pl.CostEstimate(
            flops=8 * rows * D * D, bytes_accessed=17 << 20, transcendentals=0
        ),
        name="feed_up",
    )(scal, y1_low, up_bias, w_up, w_out, *pieces)


def down_kernel(scal, act, y1, cot, vecs, *rest):
    pieces, (out2, dh2, dz2, sums, held, acc, sems) = rest[:10], rest[10:]
    pairs, owners = down_pairs(pieces, held)
    groups = per_piece(pairs, owners, sems)
    for group in groups:
        start_all(group)
    acc[...] = y1[...] + vecs[5:6]
    for m, group in enumerate(groups):
        wait_all(group)
        b = scal[0] ^ PIECES[m]
        for r in (slice(0, 256), slice(256, 512)):
            acc[r, :] += contract(act[b, r, :], held[m], 1, 0)
    out, normed, inverse = norm_forward(acc[...], vecs[6:7], vecs[7:8])
    out2[...] = out.astype(BF)
    c = cot[...].astype(F32)
    grad = norm_backward(c, normed, inverse, vecs[6:7])
    dh2[...] = grad
    low = grad.astype(BF)
    dz2[...] = low
    sums[0:1, :] = jnp.sum(c * normed, 0, keepdims=True)
    sums[1:2, :] = jnp.sum(c, 0, keepdims=True)
    sums[2:3, :] = jnp.sum(low.astype(F32), 0, keepdims=True)


DOWN_COPIES = 6 * 4 + 2 * 8


def feed_down(scal, act, y1, cot, vecs, pieces):
    rows = y1.shape[0]
    return pl.pallas_call(
        down_kernel,
        out_shape=(
            struct((rows, D), BF),
            struct((rows, D), F32),
            struct((rows, D), BF),
            struct((8, D), F32),
        ),
        in_specs=[SMEM] + [VMEM] * 4 + [ANY] * 10,
        out_specs=(VMEM,) * 4,
        scratch_shapes=[
            pltpu.VMEM((8, 512, D), BF),
            pltpu.VMEM((rows, D), F32),
            pltpu.SemaphoreType.DMA((DOWN_COPIES,)),
        ],
        compiler_params=params(48),
        cost_estimate=pl.CostEstimate(
            flops=8 * rows * D * D, bytes_accessed=20 << 20, transcendentals=0
        ),
        name="feed_down",
    )(scal, act, y1, cot, vecs, *pieces)


def feed_back_kernel(scal, dz2, dh2, slope, n1, r1, vecs, w_up, w_out, *rest):
    ups, downs = rest[:10], rest[10:20]
    du, dh1, dao, dattn, sums, up_sums, up_held, down_held, acc, sems = rest[20:]
    pairs, owners = down_pairs(downs, down_held)
    down_groups = per_piece(pairs, owners, sems)
    up_groups = per_piece(
        up_pairs(scal, ups, (w_up, w_out), 0, 640, up_held), up_owners(0, 640), sems, DOWN_COPIES
    )
    for down_group, up_group in zip(down_groups, up_groups):
        start_all(down_group)
        start_all(up_group)
    acc[...] = dh2[...]
    for m in range(8):
        wait_all(down_groups[m])
        wait_all(up_groups[m])
        b = scal[0] ^ PIECES[m]
        total = jnp.zeros((1, 512), F32)
        for r in (slice(0, 256), slice(256, 512)):
            low = (contract(dz2[r, :], down_held[m], 1, 1) * slope[b, r, :].astype(F32)).astype(BF)
            du[b, r, :] = low
            total = total + jnp.sum(low.astype(F32), 0, keepdims=True)
            acc[r, :] += contract(low, up_held[m, :, 0:512], 1, 1)
        up_sums[pl.ds(b, 1), :] = total
    dy1 = acc[...]
    normed = n1[...]
    grad = norm_backward(dy1, normed, r1[:, 0:1], vecs[3:4])
    dh1[...] = grad
    low = grad.astype(BF)
    dao[...] = low
    sums[0:1, :] = jnp.sum(dy1 * normed, 0, keepdims=True)
    sums[1:2, :] = jnp.sum(dy1, 0, keepdims=True)
    sums[2:3, :] = jnp.sum(low.astype(F32), 0, keepdims=True)
    acc[...] = jnp.zeros_like(acc)
    for m in range(8):
        columns = pl.ds(pl.multiple_of((scal[0] ^ PIECES[m]) * 128, 128), 128)
        acc[...] += contract(dao[:, columns], up_held[m, :, 512:640], 1, 1)
    for t in range(4):
        dattn[t] = acc[:, 256 * t : 256 * (t + 1)].astype(BF)


def feed_back(scal, dz2, dh2, slope, n1, r1, vecs, w_up, w_out, ups, downs):
    rows = dz2.shape[0]
    return pl.pallas_call(
        feed_back_kernel,
        out_shape=(
            struct((8, rows, 512), BF),
            struct((rows, D), F32),
            struct((rows, D), BF),
            struct((4, rows, 256), BF),
            struct((8, D), F32),
            struct((8, 512), F32),
        ),
        in_specs=[SMEM] + [VMEM] * 6 + [ANY] * 22,
        out_specs=(VMEM,) * 6,
        scratch_shapes=[
            pltpu.VMEM((8, D, 640), BF),
            pltpu.VMEM((8, 512, D), BF),
            pltpu.VMEM((rows, D), F32),
            pltpu.SemaphoreType.DMA((DOWN_COPIES + len(up_owners(0, 640)),)),
        ],
        compiler_params=params(58),
        cost_estimate=pl.CostEstimate(
            flops=18 * rows * D * D, bytes_accessed=40 << 20, transcendentals=0
        ),
        name="feed_back",
    )(scal, dz2, dh2, slope, n1, r1, vecs, w_up, w_out, *ups, *downs)


def other_core(index_map):
    return lambda n, s: index_map(n, s[0] ^ 1, s)


def own_core(index_map):
    return lambda n, s: index_map(n, s[0], s)


def split_write(n, block, a_keep, a_send, b_keep, b_send):
    half = a_keep.shape[1]
    top_rows, low_rows = block[:half], block[half:]
    for step in range(4):

        @pl.when(n == step)
        def _():
            (a_send if step in (1, 3) else a_keep)[0] = top_rows
            (b_send if step in (2, 3) else b_keep)[0] = low_rows


def split_specs(rows, columns):
    half = (1, rows // 2, columns)
    return (
        pl.BlockSpec(half, lambda n, s: (n // 2, 0, 0)),
        pl.BlockSpec(half, lambda n, s: (n // 2, 0, 0)),
        pl.BlockSpec(half, lambda n, s: (jnp.minimum(n, 1), 0, 0)),
        pl.BlockSpec(half, lambda n, s: (jnp.maximum(n - 2, 0), 0, 0)),
    )


def split_shapes(rows, columns):
    return (struct((2, rows // 2, columns), BF),) * 4


def down_block(act, dz2):
    return jnp.concatenate([contract(act[f], dz2[...], 0, 0) for f in range(4)], 0)


def down_grad_other_kernel(scal, act, dz2, out):
    out[0] = down_block(act, dz2).astype(BF)


def down_grad_own_kernel(scal, act, dz2, came, *outs):
    block = (down_block(act, dz2) + came[0].astype(F32)).astype(BF)
    split_write(pl.program_id(0), block, *outs)


def down_grad(scal, act, dz2, came=None):
    rows = dz2.shape[0]
    act_map = lambda n, core, s: (core, 0, s[1 + n])
    cost = pl.CostEstimate(flops=4 * rows * D * D, bytes_accessed=9 << 20, transcendentals=0)
    dz2_spec = pl.BlockSpec((rows, D), lambda n, s: (0, 0))
    act_block = (4, rows, 128)
    if came is None:
        return pl.pallas_call(
            down_grad_other_kernel,
            out_shape=struct((4, 512, D), BF),
            grid_spec=pltpu.PrefetchScalarGridSpec(
                num_scalar_prefetch=1,
                grid=(4,),
                in_specs=[pl.BlockSpec(act_block, other_core(act_map)), dz2_spec],
                out_specs=pl.BlockSpec((1, 512, D), lambda n, s: (n, 0, 0)),
            ),
            compiler_params=params(40),
            cost_estimate=cost,
            name="down_grad_other",
        )(scal, act, dz2)
    return pl.pallas_call(
        down_grad_own_kernel,
        out_shape=split_shapes(512, D),
        grid_spec=pltpu.PrefetchScalarGridSpec(
            num_scalar_prefetch=1,
            grid=(4,),
            in_specs=[
                pl.BlockSpec(act_block, own_core(act_map)),
                dz2_spec,
                pl.BlockSpec((1, 512, D), lambda n, s: (n, 0, 0)),
            ],
            out_specs=split_specs(512, D),
        ),
        compiler_params=params(40),
        cost_estimate=cost,
        name="down_grad_own",
    )(scal, act, dz2, came)


UP_WIDTH = 4096 + 1024 + 128


def up_block(y1_low, du, attn, dao, small):
    left = y1_low[...]
    parts = [contract(left, du[b], 0, 0) for b in range(8)]
    parts.append(contract(attn[0], dao[...], 0, 0))
    parts.append(small[0])
    return jnp.concatenate(parts, 1)


def up_grad_other_kernel(scal, y1_low, du, attn, dao, small, out):
    out[0] = up_block(y1_low, du, attn, dao, small).astype(BF)


def up_grad_own_kernel(scal, y1_low, du, attn, dao, small, came, *outs):
    block = (up_block(y1_low, du, attn, dao, small) + came[0].astype(F32)).astype(BF)
    split_write(pl.program_id(0), block, *outs)


def up_grad(scal, y1_low, du, attn, dao, small, came=None):
    rows = dao.shape[0]
    side = other_core if came is None else own_core
    in_specs = [
        pl.BlockSpec((rows, 128), side(lambda n, core, s: (0, 2 * s[1 + n] + core))),
        pl.BlockSpec((8, rows, 512), lambda n, s: (0, 0, 0)),
        pl.BlockSpec((1, rows, 128), side(lambda n, core, s: (s[1 + n], 0, core))),
        pl.BlockSpec((rows, D), lambda n, s: (0, 0)),
        pl.BlockSpec((1, 128, 128), side(lambda n, core, s: (2 * s[1 + n] + core, 0, 0))),
    ]
    cost = pl.CostEstimate(flops=5 * rows * D * D, bytes_accessed=12 << 20, transcendentals=0)
    if came is None:
        return pl.pallas_call(
            up_grad_other_kernel,
            out_shape=struct((4, 128, UP_WIDTH), BF),
            grid_spec=pltpu.PrefetchScalarGridSpec(
                num_scalar_prefetch=1,
                grid=(4,),
                in_specs=in_specs,
                out_specs=pl.BlockSpec((1, 128, UP_WIDTH), lambda n, s: (n, 0, 0)),
            ),
            compiler_params=params(48),
            cost_estimate=cost,
            name="up_grad_other",
        )(scal, y1_low, du, attn, dao, small)
    return pl.pallas_call(
        up_grad_own_kernel,
        out_shape=split_shapes(128, UP_WIDTH),
        grid_spec=pltpu.PrefetchScalarGridSpec(
            num_scalar_prefetch=1,
            grid=(4,),
            in_specs=in_specs
            + [pl.BlockSpec((1, 128, UP_WIDTH), lambda n, s: (n, 0, 0))],
            out_specs=split_specs(128, UP_WIDTH),
        ),
        compiler_params=params(48),
        cost_estimate=cost,
        name="up_grad_own",
    )(scal, y1_low, du, attn, dao, small, came)


def add_low(a, b):
    return (a.astype(F32) + b.astype(F32)).astype(BF)


def reduce_chips(a_keep, a_send, b_keep, b_send):
    a_came = hop(a_send, 2)
    b_came = hop(b_send, 4)
    a_next = hop(add_low(a_keep[1], a_came[1]), 4)
    b_next = hop(add_low(b_keep[1], b_came[1]), 2)
    a_all = a_keep[0].astype(F32) + a_came[0].astype(F32) + a_next.astype(F32)
    b_all = b_keep[0].astype(F32) + b_came[0].astype(F32) + b_next.astype(F32)
    both = jnp.concatenate([a_all, b_all], 0).astype(BF)
    return lax.psum_scatter(both, "fsdp", scatter_dimension=0, tiled=True).astype(F32)


def after(value, *others):
    return lax.optimization_barrier((value,) + others)[0]


def near_chips(own):
    return hop(own, 2), hop(own, 4)


def gather_chips(own, from_x, from_y):
    half = own.shape[1] // 2
    mine = [own, from_x, from_y, hop(from_y[:, :half], 2), hop(from_x[:, half:], 4)]
    return mine + [hop(piece, 1) for piece in mine]


def tiled_device(
    tokens, cotangent, lengths, order, w_qkv, w_out, w_up, w_down, q_bias, v_bias, out_bias,
    norm1_gain, norm1_bias, up_bias, down_bias, norm2_gain, norm2_bias,
):
    me = lax.axis_index("ctx")
    shard = lax.axis_index("fsdp")
    core, low, top = me % 2, me % 4, me // 4
    chunk = tokens.shape[2]
    half_groups = [[0, 1, 2, 3], [4, 5, 6, 7]]
    scal = jnp.stack(
        [me, low, top, shard] + [(shard + 4 - k) % 4 for k in (1, 2, 3)]
    ).astype(jnp.int32)
    chips = jnp.stack([core] + [(me // 2) ^ n for n in range(4)]).astype(jnp.int32)
    first_length = jnp.where(top == 0, lengths[0, 0, 0], lengths[1, 0, 0])
    places = jnp.stack([first_length, top] + [(me ^ k) * chunk for k in CHUNKS]).astype(jnp.int32)
    small = jnp.concatenate(
        [
            q_bias, v_bias, out_bias, norm1_gain, norm1_bias, down_bias, norm2_gain, norm2_bias,
            up_bias, jnp.zeros((12 * 768,), BF),
        ]
    ).reshape(16, 768)
    own_rows, other_rows, cot_own, cot_other, pack, up_slice, down_slice = carve(
        scal, tokens, cotangent, w_qkv, w_out, w_up, w_down, small
    )

    packed = lax.all_gather(pack, "fsdp", axis=0)
    held = [own_rows, hop(other_rows, 4), hop(own_rows, 2), hop(other_rows, 6)]
    held = held + [hop(piece, 1) for piece in held]
    foreign = jnp.stack(
        [
            lax.ppermute(up_slice, "fsdp", [(i, (i + k) % 4) for i in range(4)])
            for k in (1, 2, 3)
        ]
    )
    vectors = packed[:, 256:260].reshape(4, 3072).astype(F32)
    vecs = vectors[:, :2048].reshape(4, 8, 256).transpose(1, 0, 2).reshape(8, D)
    up_b = vectors[:, 2048:].reshape(4, 8, 128).transpose(1, 0, 2).reshape(8, 512)
    qkv, x_all = project(scal, vecs, packed, held)

    down_own = lax.all_gather(after(down_slice, packed), "fsdp", axis=0)
    up_x, up_y = near_chips(foreign)
    attn_send, attn_t, lse = attention_forward(places, after(qkv, foreign), chunk)
    attn = lax.all_to_all(
        attn_send.reshape(4, 2 * chunk, 256), "ctx", 0, 0, tiled=True,
        axis_index_groups=half_groups,
    )
    up_x, up_y = lax.optimization_barrier((up_x, up_y, attn_send))[:2]
    ups = gather_chips(foreign, up_x, up_y)
    down_own = after(down_own, attn_send)
    down_x, down_y = near_chips(down_own)

    order_row = jnp.where(top == 0, order[0, 0], order[1, 0])
    cot_held = jnp.concatenate([cot_own, hop(cot_other, 4)], 0)
    cot_all = lax.all_gather(
        after(cot_held, down_own), "ctx", axis=0, tiled=True, axis_index_groups=half_groups
    )
    cot_blocks = cot_all.reshape(16, BLK, D)
    blocks = jnp.arange(16, dtype=jnp.int32)

    def held_place(block):
        device = block // 2
        return (device % 4) * 4 + ((device // 4) ^ top) * 2 + block % 2

    cot_rows = []
    for k in (0, 4):
        for e in range(2):
            given = 2 * (me ^ k) + e
            dealt = jnp.sum(jnp.where(order_row == given, blocks, 0))
            cot_rows.append(
                lax.dynamic_index_in_dim(cot_blocks, held_place(dealt), 0, False)
            )
    cot_rows = jnp.concatenate(cot_rows, 0)

    y1, y1_low, n1, r1 = attention_out(scal, attn, x_all, vecs, w_up, w_out, ups)
    act, slope = feed_up(scal, y1_low, up_b, w_up, w_out, ups)
    downs = gather_chips(down_own, down_x, down_y)
    out2, dh2, dz2, sums2 = feed_down(scal, act, y1, cot_rows, vecs, downs)

    out_all = lax.all_gather(out2, "ctx", axis=0, tiled=True, axis_index_groups=half_groups)
    out_blocks = out_all.reshape(16, BLK, D)

    def dealt_rows(device):
        rows = []
        for e in range(2):
            given = jnp.sum(jnp.where(blocks == 2 * device + e, order_row, 0))
            rows.append(lax.dynamic_index_in_dim(out_blocks, held_place(given), 0, False))
        return jnp.concatenate(rows, 0)

    down_other = down_grad(chips, act, dz2)
    du, dh1, dao, dattn, sums1, up_sums = feed_back(
        scal, after(dz2, down_other), dh2, slope, n1, r1, vecs, w_up, w_out, ups, downs
    )
    dattn_send = dattn
    dattn = lax.all_to_all(
        dattn, "ctx", 0, 0, tiled=True, axis_index_groups=half_groups
    ).reshape(4, 2, chunk, 256)
    down_parts = down_grad(chips, after(act, dattn_send), dz2, hop(down_other, 1))

    def per_owner(vector):
        return vector.reshape(8, 4, 32)

    up_owner = up_sums.reshape(8, 4, 128).transpose(1, 0, 2).reshape(8, 4, 128)
    vec_block = jnp.concatenate(
        [per_owner(sums1[2]), per_owner(sums1[0]), per_owner(sums1[1]), per_owner(sums2[2]),
         per_owner(sums2[0]), per_owner(sums2[1]), up_owner, jnp.zeros((8, 4, 64), F32)], 2
    ).reshape(8, 4, 3, 128)
    vec_block = jnp.concatenate([vec_block, jnp.zeros((8, 4, 29, 128), F32)], 2).reshape(
        8, 128, 128
    )
    up_other = up_grad(chips, y1_low, after(du, down_parts[0]), attn, dao, vec_block)
    up_parts = up_grad(chips, y1_low, du, attn, dao, vec_block, hop(up_other, 1))

    dattn, out_blocks = lax.optimization_barrier((dattn, out_blocks, *up_parts))[:2]
    dqkv = attention_backward(places, qkv, dattn, attn_t, lse, chunk)
    down_rows = reduce_chips(*down_parts)
    up_rows = reduce_chips(*up_parts)

    mixed_own = dealt_rows(me)
    mixed_came = hop(dealt_rows(me ^ 4), 4)
    mixed = jnp.where(
        top == 0, jnp.stack([mixed_own, mixed_came]), jnp.stack([mixed_came, mixed_own])
    )[:, None]

    grad_qkv = contract(x_all, dqkv, 0, 0)
    column_sums = jnp.sum(dqkv.astype(F32), 0)
    spread = (jnp.arange(4) == low).astype(F32)[:, None]
    q_sum = (spread * column_sums[None, :256]).reshape(D, 1)
    v_sum = (spread * column_sums[None, 512:]).reshape(D, 1)
    grad_qkv = jnp.concatenate([grad_qkv, q_sum, v_sum, jnp.zeros((D, 126), F32)], 1).astype(BF)
    grad_qkv = grad_qkv.reshape(2, 4, 4, 32, 896).transpose(0, 2, 1, 3, 4)
    keep = lax.dynamic_index_in_dim(grad_qkv, top, 0, False)
    send = lax.dynamic_index_in_dim(grad_qkv, 1 - top, 0, False)
    pair = add_low(keep, hop(send, 4)).reshape(16 * 32, 896)
    mine = lax.psum_scatter(pair, "fsdp", scatter_dimension=0, tiled=True)
    mine = lax.all_to_all(
        mine.reshape(4, 32, 896), "ctx", 0, 0, tiled=True, axis_index_groups=half_groups
    ).astype(F32)
    w_qkv_grad = mine[:, :, :768].reshape(4, 32, 3, 256).transpose(1, 2, 0, 3).reshape(32, 3072)
    q_bias_grad = jnp.sum(mine[:, :, 768], 0)
    v_bias_grad = jnp.sum(mine[:, :, 769], 0)

    qkv_weight = packed[:, :256].reshape(D, 768)
    dx = contract(dqkv, qkv_weight, 1, 1).astype(BF).reshape(8, chunk, D)
    dx = add_low(dx[:4], hop(dx[4:], 1))
    dx = dx[:2].astype(F32) + hop(dx[2:], 2).astype(F32)
    dx = (dx.reshape(2 * chunk, D) + dh1).astype(BF)
    grad_own = dx[:chunk]
    grad_came = hop(dx[chunk:], 4)
    tokens_grad = jnp.where(
        top == 0, jnp.stack([grad_own, grad_came]), jnp.stack([grad_came, grad_own])
    )[:, None]

    w_up_grad = (
        up_rows[:, :4096].reshape(32, 8, 4, 128).transpose(0, 2, 1, 3).reshape(32, 4096)
    )
    w_out_grad = up_rows[:, 4096:5120]
    sums = up_rows[:3, 5120:].reshape(384)
    return (
        mixed, tokens_grad, w_qkv_grad, w_out_grad, w_up_grad, down_rows, q_bias_grad, v_bias_grad,
        sums[0:32], sums[32:64], sums[64:96], sums[192:320], sums[96:128], sums[128:160],
        sums[160:192],
    )


def pick_blocks(wanted, rows):
    shaped = rows.reshape(-1, BLK, rows.shape[-1])
    picked = [
        lax.dynamic_index_in_dim(shaped, wanted[e], 0, False) for e in range(wanted.shape[0])
    ]
    return jnp.concatenate(picked, 0)


def plain_device(
    tokens, cotangent, lengths, order, w_qkv, w_out, w_up, w_down, q_bias, v_bias, out_bias,
    norm1_gain, norm1_bias, up_bias, down_bias, norm2_gain, norm2_bias,
):
    shards = (
        w_qkv, w_out, w_up, w_down, q_bias, v_bias, out_bias, norm1_gain, norm1_bias, up_bias,
        down_bias, norm2_gain, norm2_bias,
    )
    me = lax.axis_index("ctx")
    count = lax.axis_size("ctx")
    rows = tokens.shape[2]
    per_device = rows // BLK
    whole_rows = rows * count
    scaling = 1.0 / math.sqrt(HD)
    (
        qkv_full, out_full, up_full, down_full, qbias_full, vbias_full, obias_full, gain_one,
        shift_one, ubias_full, dbias_full, gain_two, shift_two,
    ) = tuple(lax.all_gather(shard, "fsdp", axis=0, tiled=True) for shard in shards)
    full_bias = jnp.concatenate([qbias_full, jnp.zeros_like(qbias_full), vbias_full]).astype(F32)
    gain_one, shift_one, gain_two, shift_two = (
        vector.astype(F32) for vector in (gain_one, shift_one, gain_two, shift_two)
    )
    positions = jnp.arange(whole_rows, dtype=jnp.int32)
    mixed_list, grad_list, totals = [], [], None
    for micro in range(tokens.shape[0]):
        order_row = order[micro, 0]
        bound = lengths[micro, 0, 0]
        segment_all = (positions >= bound).astype(jnp.int32)
        segment_query = (me * rows + jnp.arange(rows, dtype=jnp.int32) >= bound).astype(jnp.int32)
        dealt = me * per_device + jnp.arange(per_device, dtype=jnp.int32)
        blocks = jnp.arange(order_row.shape[0], dtype=jnp.int32)
        inverse = jnp.sum(jnp.where(order_row[None, :] == dealt[:, None], blocks[None, :], 0), 1)
        forward = jnp.sum(jnp.where(blocks[None, :] == dealt[:, None], order_row[None, :], 0), 1)
        token_rows = tokens[micro, 0]
        cot_rows = pick_blocks(
            inverse, lax.all_gather(cotangent[micro, 0], "ctx", axis=0, tiled=True)
        ).astype(F32)
        qkv_rows = (jnp.dot(token_rows, qkv_full, preferred_element_type=F32) + full_bias).astype(BF)
        queries = qkv_rows[:, :D].reshape(rows, H, HD)
        keys_values = lax.all_gather(qkv_rows[:, D:], "ctx", axis=0, tiled=True)
        keys = keys_values[:, :D].reshape(whole_rows, H, HD)
        values = keys_values[:, D:].reshape(whole_rows, H, HD)
        allowed = (segment_query[:, None] == segment_all[None, :])[None]
        scores = jnp.einsum("rhd,khd->hrk", queries, keys, preferred_element_type=F32) * scaling
        scores = jnp.where(allowed, scores, NEGATIVE)
        expos = jnp.where(allowed, jnp.exp(scores - jnp.max(scores, -1, keepdims=True)), 0.0)
        probs = expos / jnp.sum(expos, -1, keepdims=True)
        probs_low = probs.astype(BF)
        attn_float = jnp.einsum("hrk,khd->rhd", probs_low, values, preferred_element_type=F32)
        attn_low = attn_float.reshape(rows, D).astype(BF)
        first_in = (
            token_rows.astype(F32)
            + jnp.dot(attn_low, out_full, preferred_element_type=F32)
            + obias_full.astype(F32)
        )
        first_out, normed_one, inverse_one = norm_forward(first_in, gain_one, shift_one)
        first_low = first_out.astype(BF)
        hidden_in = jnp.dot(first_low, up_full, preferred_element_type=F32) + ubias_full.astype(F32)
        activated, gelu_back = jax.vjp(partial(jax.nn.gelu, approximate=False), hidden_in)
        act_low = activated.astype(BF)
        second_in = (
            first_out
            + jnp.dot(act_low, down_full, preferred_element_type=F32)
            + dbias_full.astype(F32)
        )
        second_out, normed_two, inverse_two = norm_forward(second_in, gain_two, shift_two)
        out_all = lax.all_gather(second_out.astype(BF), "ctx", axis=0, tiled=True)
        mixed_list.append(pick_blocks(forward, out_all))

        grad_second = norm_backward(cot_rows, normed_two, inverse_two, gain_two)
        grad_down_low = grad_second.astype(BF)
        (grad_hidden,) = gelu_back(contract(grad_down_low, down_full, 1, 1))
        grad_hidden_low = grad_hidden.astype(BF)
        grad_first = grad_second + contract(grad_hidden_low, up_full, 1, 1)
        grad_first_in = norm_backward(grad_first, normed_one, inverse_one, gain_one)
        grad_branch = grad_first_in.astype(BF)
        grad_attn = contract(grad_branch, out_full, 1, 1).astype(BF).reshape(rows, H, HD)
        grad_probs = jnp.einsum("rhd,khd->hrk", grad_attn, values, preferred_element_type=F32)
        delta = jnp.sum(probs * grad_probs, -1, keepdims=True)
        grad_scores = (probs * (grad_probs - delta) * scaling).astype(BF)
        grad_query = jnp.einsum("hrk,khd->rhd", grad_scores, keys, preferred_element_type=F32)
        grad_keys = jnp.einsum("hrk,rhd->khd", grad_scores, queries, preferred_element_type=F32)
        grad_values = jnp.einsum("hrk,rhd->khd", probs_low, grad_attn, preferred_element_type=F32)
        both = jnp.concatenate(
            [grad_keys.reshape(whole_rows, D), grad_values.reshape(whole_rows, D)], 1
        )
        both = lax.psum_scatter(both, "ctx", scatter_dimension=0, tiled=True)
        grad_qkv = jnp.concatenate([grad_query.reshape(rows, D), both], 1).astype(BF)
        column_sums = jnp.sum(grad_qkv.astype(F32), 0)
        grad_list.append((grad_first_in + contract(grad_qkv, qkv_full, 1, 1)).astype(BF))
        parts = (
            contract(token_rows, grad_qkv, 0, 0),
            contract(attn_low, grad_branch, 0, 0),
            contract(first_low, grad_hidden_low, 0, 0),
            contract(act_low, grad_down_low, 0, 0),
            column_sums[:D],
            column_sums[2 * D :],
            jnp.sum(grad_branch.astype(F32), 0),
            jnp.sum(grad_first * normed_one, 0),
            jnp.sum(grad_first, 0),
            jnp.sum(grad_hidden_low.astype(F32), 0),
            jnp.sum(grad_down_low.astype(F32), 0),
            jnp.sum(cot_rows * normed_two, 0),
            jnp.sum(cot_rows, 0),
        )
        totals = parts if totals is None else tuple(a + b for a, b in zip(totals, parts))
    shares = tuple(
        lax.psum_scatter(part, ("ctx", "fsdp"), scatter_dimension=0, tiled=True) for part in totals
    )
    return (jnp.stack(mixed_list)[:, None], jnp.stack(grad_list)[:, None]) + shares


def solution(mesh):
    fits = mesh.shape["ctx"] == 8 and mesh.shape["fsdp"] == 4
    weights = (P("fsdp", None),) * 4 + (P("fsdp"),) * 9
    owners = (P(("ctx", "fsdp"), None),) * 4 + (P(("ctx", "fsdp")),) * 9
    rows = P(None, "fsdp", "ctx", None)
    return jax.shard_map(
        tiled_device if fits else plain_device,
        mesh=mesh,
        in_specs=(rows, rows, P(None, "fsdp", None), P(None, "fsdp", None)) + weights,
        out_specs=(rows, rows) + owners,
        check_vma=False,
    )
```

time: 2340 us -> 549 us (0.23)
  the two profiles are of different devices: /device:TPU:0 before, /device:TPU:8 now
where the time goes in v1:
time: 549 us; the launch traced here: 538 us
  waiting for transfers between devices  178 us (32%)
  Pallas kernels  174 us (32%)
  local copies, waits for them, and re-layouts  59.5 us (11%)
  starting transfers between devices  45.9 us (8%)
  between operations  37.5 us (7%)
  other arithmetic  35 us (6%)
  matrix products  8.76 us (2%)
    ppermute x41, waiting for transfers between devices, hop(): return lax.ppermute(value, 'ctx', [(i, i ^ mask) for i in range(count)])  127 us
    ppermute x3, waiting for transfers between devices, tiled_device(): lax.ppermute(up_slice, 'fsdp', [(i, (i + k) % 4) for i in range(4)])  49 us
    pallas_call x1, Pallas kernels, attention_backward(): pl.pallas_call(partial(attention_backward_kernel, heads=heads, chunk=chun...  43.1 us
    unnamed x114, local copies, waits for them, and re-layouts  35.4 us
    ppermute x41, starting transfers between devices, hop(): return lax.ppermute(value, 'ctx', [(i, i ^ mask) for i in range(count)])  31.3 us
    pallas_call x1, Pallas kernels, attention_forward(): pl.pallas_call(partial(attention_forward_kernel, heads=heads, chunk=chunk...  25 us
    pallas_call x1, Pallas kernels, feed_back(): pl.pallas_call(feed_back_kernel, out_shape=(struct((8, rows, 512), BF), s...  22.7 us
    pallas_call x1, Pallas kernels, feed_up(): pl.pallas_call(up_kernel, out_shape=(struct((8, rows, 512), BF), struct((...  14.7 us
  transfers between devices with their start and end apart: 54, of which 14 were waited for; matrix products, arithmetic and copies ran while one was open for 12% of the time, Pallas kernels for 27%

profile of v1, /device:TPU:8, one launch (start us, length us, event | category | flops | bytes accessed | tf_op | source)
XLA Modules:
  0.0 538.2 jit_solution(15417406063415404237)
XLA Ops:
  31.0 11.3 %collective-permute-done.7 = bf16[256,640]{1,0:T(8,128)(2,1)S(1)} collective-permute-done((bf16[256,640]{1,0:T(8,128)(2,1)S(1)}, bf16[256,640]{1,0:T(8,128)(2,1)S(1)}, u32[]{:S(2)}, u32[]{:S(2)}) %collective-permute-start.7) | collective-permute-done | bytes 327712 | tf_op jit(solution)/shard_map/ppermute | solution.py:843
  42.2 33.8 %collective-permute-done.8 = bf16[256,640]{1,0:T(8,128)(2,1)S(1)} collective-permute-done((bf16[256,640]{1,0:T(8,128)(2,1)S(1)}, bf16[256,640]{1,0:T(8,128)(2,1)S(1)}, u32[]{:S(2)}, u32[]{:S(2)}) %collective-permute-start.8) | collective-permute-done | bytes 327712 | tf_op jit(solution)/shard_map/ppermute | solution.py:843
  78.2 3.9 collective-permute-done.9
  90.4 7.2 %project.1 = (bf16[2048,768]{1,0:T(8,128)(2,1)S(1)}, bf16[2048,1024]{1,0:T(8,128)(2,1)S(1)}) custom-call(s32[7]{0:T(128)S(1)} %stack.120.scal, f32[8,1024]{1,0:T(8,128)S(1)} %bitcast.147, bf16[4,272,768]{2,1,0:T(8,128)(2,1)S(1)} %bitcast.146, bf16[256,1024]{1,0:T(8,128)(2,1)S(1)} %get-tuple-element.63.rest_0_, ...), custom_call_target="tpu_custom_call" | custom-call | flops 3221225472 | bytes 13631488 | tf_op jit(solution)/shard_map/project/pallas_call | solution.py:353
  101.3 25.0 %attention_forward.1 = (bf16[4,2,256,256]{3,2,1,0:T(8,128)(2,1)}, f32[256,2048]{1,0:T(8,128)}, f32[4,2048]{1,0:T(4,128)}) custom-call(s32[10]{0:T(128)} %stack.130.scal, bf16[2048,768]{1,0:T(8,128)(2,1)} %copy-done.35), custom_call_target="tpu_custom_call" | custom-call | flops 8589934592 | bytes 5242880 | tf_op jit(solution)/shard_map/attention_forward/pallas_call | solution.py:151
  130.4 33.2 %collective-permute-done.10.rest_1_ = bf16[3,256,640]{2,1,0:T(8,128)(2,1)S(1)} collective-permute-done((bf16[3,256,640]{2,1,0:T(8,128)(2,1)S(1)}, bf16[3,256,640]{2,1,0:T(8,128)(2,1)S(1)}, u32[]{:S(2)}, u32[]{:S(2)}) %collective-permute-start.10) | collective-permute-done | bytes 983072 | tf_op jit(solution)/shard_map/ppermute | solution.py:45
  165.0 2.4 collective-permute-start.12
  169.2 36.6 %collective-permute-done.12.rest_3_ = bf16[3,128,640]{2,1,0:T(8,128)(2,1)S(1)} collective-permute-done((bf16[3,128,640]{2,1,0:T(8,128)(2,1)S(1)}, bf16[3,128,640]{2,1,0:T(8,128)(2,1)S(1)}, u32[]{:S(2)}, u32[]{:S(2)}) %collective-permute-start.12) | collective-permute-done | bytes 491552 | tf_op jit(solution)/shard_map/ppermute | solution.py:45
  206.7 3.6 all-to-all-start
  232.9 9.7 %attention_out.1 = (f32[512,1024]{1,0:T(8,128)S(1)}, bf16[512,1024]{1,0:T(8,128)(2,1)S(1)}, f32[512,1024]{1,0:T(8,128)}, f32[512,128]{1,0:T(8,128)S(1)}) custom-call(s32[7]{0:T(128)S(1)} %copy-done.30, bf16[4,512,256]{2,1,0:T(8,128)(2,1)S(1)} %all-to-all-done.attn, bf16[2048,1024]{1,0:T(8,128)(2,1)} %copy-done.3, f32[8,1024]{1,0:T(8,128)S(1)} %bitcast.148, ...), custom_call_target="tpu_custom_call" | custom-call | flops 1073741824 | bytes 8388608 | tf_op jit(solution)/shard_map/attention_out/pallas_call | solution.py:457
  246.1 14.7 %feed_up.1 = (bf16[8,512,512]{2,1,0:T(8,128)(2,1)}, bf16[8,512,512]{2,1,0:T(8,128)(2,1)}) custom-call(s32[7]{0:T(128)S(1)} %copy-done.31, bf16[512,1024]{1,0:T(8,128)(2,1)} %copy-done.5, f32[8,512]{1,0:T(8,128)S(1)} %bitcast.151, bf16[256,4096]{1,0:T(8,128)(2,1)} %w_up.7, bf16[256,1024]{1,0:T(8,128)(2,1)S(1)} %copy-done.16, ...), custom_call_target="tpu_custom_call" | custom-call | flops 4294967296 | bytes 17825792 | tf_op jit(solution)/shard_map/feed_up/pallas_call | solution.py:501
  262.3 12.7 %feed_down.1 = (bf16[512,1024]{1,0:T(8,128)(2,1)}, f32[512,1024]{1,0:T(8,128)}, bf16[512,1024]{1,0:T(8,128)(2,1)S(1)}, f32[8,1024]{1,0:T(8,128)S(1)}) custom-call(s32[7]{0:T(128)S(1)} %copy-done.32, bf16[8,512,512]{2,1,0:T(8,128)(2,1)} %get-tuple-element.94.act, f32[512,1024]{1,0:T(8,128)} %copy-done.33, bf16[512,1024]{1,0:T(8,128)(2,1)S(1)} %pad_maximum_fusion.2.cot, ...), custom_call_target="tpu_custom_call" | custom-call | flops 4294967296 | bytes 20971520 | tf_op jit(solution)/shard_map/feed_down/pallas_call | solution.py:547
  275.0 13.6 %down_grad_other.1 = bf16[4,512,1024]{2,1,0:T(8,128)(2,1)} custom-call(s32[5]{0:T(128)S(1)} %copy-done.28, bf16[8,512,512]{2,1,0:T(8,128)(2,1)S(1)} %copy-done, bf16[512,1024]{1,0:T(8,128)(2,1)S(1)} %get-tuple-element.82.dz2), custom_call_target="tpu_custom_call" | custom-call | flops 2147483648 | bytes 9437184 | tf_op jit(solution)/shard_map/down_grad_other/pallas_call | solution.py:691
  289.1 22.7 %feed_back.1 = (bf16[8,512,512]{2,1,0:T(8,128)(2,1)}, f32[512,1024]{1,0:T(8,128)}, bf16[512,1024]{1,0:T(8,128)(2,1)}, bf16[4,512,256]{2,1,0:T(8,128)(2,1)}, f32[8,1024]{1,0:T(8,128)}, /*index=5*/f32[8,512]{1,0:T(8,128)}) custom-call(s32[7]{0:T(128)} %copy-done.29, bf16[512,1024]{1,0:T(8,128)(2,1)} %copy-done.9, f32[512,1024]{1,0:T(8,128)} %get-tuple-element.83.dh2, ...), custom_call_target="tpu_custom_call" | custom-call | flops 9663676416 | bytes 41943040 | tf_op jit(solution)/shard_map/feed_back/pallas_call | solution.py:612
  317.7 6.2 %down_grad_own.1 = (bf16[2,256,1024]{2,1,0:T(8,128)(2,1)S(1)}, bf16[2,256,1024]{2,1,0:T(8,128)(2,1)S(1)}, bf16[2,256,1024]{2,1,0:T(8,128)(2,1)S(1)}, bf16[2,256,1024]{2,1,0:T(8,128)(2,1)S(1)}) custom-call(s32[5]{0:T(128)S(1)} %copy-done.28, bf16[8,512,512]{2,1,0:T(8,128)(2,1)S(1)} %copy-done.1, bf16[512,1024]{1,0:T(8,128)(2,1)S(1)} %copy-done.10, ...), custom_call_target="tpu_custom_call" | custom-call | flops 2147483648 | bytes 9437184 | tf_op jit(solution)/shard_map/down_grad_own/pallas_call | solution.py:704
  323.9 7.8 %up_grad_other.1 = bf16[4,128,5248]{2,1,0:T(8,128)(2,1)} custom-call(s32[5]{0:T(128)S(1)} %copy-done.28, bf16[512,1024]{1,0:T(8,128)(2,1)S(1)} %copy-done.6, bf16[8,512,512]{2,1,0:T(8,128)(2,1)} %get-tuple-element.96.du, bf16[4,512,256]{2,1,0:T(8,128)(2,1)S(1)} %all-to-all-done.attn, bf16[512,1024]{1,0:T(8,128)(2,1)S(1)} %copy-done.7, ...), custom_call_target="tpu_custom_call" | custom-call | flops 2684354560 | bytes 12582912 | tf_op jit(solution)/shard_map/up_grad_other/pallas_call | solution.py:755
  332.1 25.1 %collective-permute-done.40 = bf16[2,256,1024]{2,1,0:T(8,128)(2,1)S(1)} collective-permute-done((bf16[2,256,1024]{2,1,0:T(8,128)(2,1)S(1)}, bf16[2,256,1024]{2,1,0:T(8,128)(2,1)S(1)}, u32[]{:S(2)}, u32[]{:S(2)}) %collective-permute-start.40) | collective-permute-done | bytes 1048608 | tf_op jit(solution)/shard_map/ppermute | solution.py:45
  360.4 2.7 slice.238
  363.1 4.2 all-to-all-start.1
  367.4 3.8 collective-permute-done.41
  377.9 9.4 %up_grad_own.1 = (bf16[2,64,5248]{2,1,0:T(8,128)(2,1)S(1)}, bf16[2,64,5248]{2,1,0:T(8,128)(2,1)}, bf16[2,64,5248]{2,1,0:T(8,128)(2,1)}, bf16[2,64,5248]{2,1,0:T(8,128)(2,1)}) custom-call(s32[5]{0:T(128)S(1)} %copy-done.28, bf16[512,1024]{1,0:T(8,128)(2,1)S(1)} %copy-done.6, bf16[8,512,512]{2,1,0:T(8,128)(2,1)} %get-tuple-element.96.du, ...), custom_call_target="tpu_custom_call" | custom-call | flops 2684354560 | bytes 12582912 | tf_op jit(solution)/shard_map/up_grad_own/pallas_call | solution.py:768
  390.4 43.1 %attention_backward.1 = bf16[2048,768]{1,0:T(8,128)(2,1)} custom-call(s32[10]{0:T(128)} %stack.130.scal, bf16[2048,768]{1,0:T(8,128)(2,1)} %copy-done.35, bf16[4,2,256,256]{3,2,1,0:T(8,128)(2,1)} %bitcast.39.grad, f32[256,2048]{1,0:T(8,128)} %get-tuple-element.103.out_t, f32[4,2048]{1,0:T(4,128)} %get-tuple-element.104.lse), custom_call_target="tpu_custom_call" | custom-call | flops 17179869184 | bytes 9437184 | tf_op jit(solution)/shard_map/attention_backward/pallas_call | solution.py:254
  433.5 2.6 convert_reduce_fusion
  436.3 4.7 convolution_convert_fusion.1
  444.8 4.1 convolution_convert_fusion
  448.9 2.5 fusion.20
  451.4 11.2 %collective-permute-done.35 = bf16[4,4,32,896]{3,2,1,0:T(8,128)(2,1)S(1)} collective-permute-done((bf16[4,4,32,896]{3,2,1,0:T(8,128)(2,1)S(1)}, bf16[4,4,32,896]{3,2,1,0:T(8,128)(2,1)S(1)}, u32[]{:S(2)}, u32[]{:S(2)}) %collective-permute-start.35) | collective-permute-done | bytes 917536 | tf_op jit(solution)/shard_map/ppermute | solution.py:45
  468.9 9.2 %collective-permute-done.37 = bf16[64,5248]{1,0:T(8,128)(2,1)S(1)} collective-permute-done((bf16[64,5248]{1,0:T(8,128)(2,1)S(1)}, bf16[64,5248]{1,0:T(8,128)(2,1)S(1)}, u32[]{:S(2)}, u32[]{:S(2)}) %collective-permute-start.37) | collective-permute-done | bytes 671776 | tf_op jit(solution)/shard_map/ppermute | solution.py:45
  483.9 3.3 fusion
  503.1 4.3 collective-permute-done.33
  512.6 3.4 all-to-all-start.2
  517.4 2.3 maximum_select_fusion
  (295 shorter events, 120.4 us)
Async XLA Ops:
  7.2 78.4 %all-gather.11.cloned.1.call-start = ((), (), s32[]{:S(2)}) async-start(), calls=%async_computation.11 | async-start | bytes 2088960 | tf_op jit(solution)/shard_map/all_gather | solution.py:838
  24.7 101.6 %all-gather.13.cloned.1.call-start = ((), (), s32[]{:S(2)}) async-start(), calls=%async_computation.12 | async-start | bytes 1310720 | tf_op jit(solution)/shard_map/all_gather | solution.py:852
  26.4 49.7 %collective-permute-start.8 = (bf16[256,640]{1,0:T(8,128)(2,1)S(1)}, bf16[256,640]{1,0:T(8,128)(2,1)S(1)}, u32[]{:S(2)}, u32[]{:S(2)}) collective-permute-start(bf16[256,640]{1,0:T(8,128)(2,1)S(1)} %get-tuple-element.66), channel_id=1, source_target_pairs={{0,2},{1,3},{2,0},{3,1},{4,6},{5,7},{6,4},{7,5},{8,10},{9,11},{10,... | collective-permute-start | bytes 983048 | tf_op jit(solution)/shard_map/ppermute | solution.py:843
  27.5 54.7 %collective-permute-start = (bf16[256,1024]{1,0:T(8,128)(2,1)S(1)}, bf16[256,1024]{1,0:T(8,128)(2,1)S(1)}, u32[]{:S(2)}, u32[]{:S(2)}) collective-permute-start(bf16[256,1024]{1,0:T(8,128)(2,1)S(1)} %get-tuple-element.64), channel_id=1, source_target_pairs={{0,16},{4,20},{8,24},{12,28},{16,0},{20,4},{24,8},{28,12},{1,17},{... | collective-permute-start | bytes 1572872 | tf_op jit(solution)/shard_map/ppermute | solution.py:45
  29.1 53.5 %collective-permute-start.1 = (bf16[256,1024]{1,0:T(8,128)(2,1)S(1)}, bf16[256,1024]{1,0:T(8,128)(2,1)}, u32[]{:S(2)}, u32[]{:S(2)}) collective-permute-start(bf16[256,1024]{1,0:T(8,128)(2,1)S(1)} %get-tuple-element.63.rest_0_), channel_id=1, source_target_pairs={{0,8},{4,12},{8,0},{12,4},{16,24},{20,28},{24,16},{28,20},{1,9},{5... | collective-permute-start | bytes 1572872 | tf_op jit(solution)/shard_map/ppermute | solution.py:45
  30.6 52.1 %collective-permute-start.2 = (bf16[256,1024]{1,0:T(8,128)(2,1)S(1)}, bf16[256,1024]{1,0:T(8,128)(2,1)}, u32[]{:S(2)}, u32[]{:S(2)}) collective-permute-start(bf16[256,1024]{1,0:T(8,128)(2,1)S(1)} %get-tuple-element.64), channel_id=1, source_target_pairs={{0,24},{4,28},{8,16},{12,20},{16,8},{20,12},{24,0},{28,4},{1,25},{... | collective-permute-start | bytes 1572872 | tf_op jit(solution)/shard_map/ppermute | solution.py:45
  42.2 39.9 %collective-permute-start.9 = (bf16[256,640]{1,0:T(8,128)(2,1)S(1)}, bf16[256,640]{1,0:T(8,128)(2,1)S(1)}, u32[]{:S(2)}, u32[]{:S(2)}) collective-permute-start(bf16[256,640]{1,0:T(8,128)(2,1)S(1)} %get-tuple-element.66), channel_id=1, source_target_pairs={{0,3},{1,0},{2,1},{3,2},{4,7},{5,4},{6,5},{7,6},{8,11},{9,8},{10,9... | collective-permute-start | bytes 983048 | tf_op jit(solution)/shard_map/ppermute | solution.py:843
  85.7 175.2 %all-gather.7.cloned.1.call-start = ((), (), s32[]{:S(2)}) async-start(), calls=%async_computation.6 | async-start | bytes 5242880 | tf_op jit(solution)/shard_map/all_gather | solution.py:866
  126.3 37.3 %collective-permute-start.10 = (bf16[3,256,640]{2,1,0:T(8,128)(2,1)S(1)}, bf16[3,256,640]{2,1,0:T(8,128)(2,1)S(1)}, u32[]{:S(2)}, u32[]{:S(2)}) collective-permute-start(bf16[3,256,640]{2,1,0:T(8,128)(2,1)S(1)} %pad_maximum_fusion.4.rest_0_), channel_id=1, source_target_pairs={{0,8},{4,12},{8,0},{12,4},{16,24},{20,28},{24,16},{28,20},{1,9},{5... | collective-permute-start | bytes 2949128 | tf_op jit(solution)/shard_map/ppermute | solution.py:45
  127.8 35.8 %collective-permute-start.11 = (bf16[3,256,640]{2,1,0:T(8,128)(2,1)S(1)}, bf16[3,256,640]{2,1,0:T(8,128)(2,1)}, u32[]{:S(2)}, u32[]{:S(2)}) collective-permute-start(bf16[3,256,640]{2,1,0:T(8,128)(2,1)S(1)} %pad_maximum_fusion.4.rest_0_), channel_id=1, source_target_pairs={{0,16},{4,20},{8,24},{12,28},{16,0},{20,4},{24,8},{28,12},{1,17},{... | collective-permute-start | bytes 2949128 | tf_op jit(solution)/shard_map/ppermute | solution.py:45
  129.4 76.9 %collective-permute-start.21 = (bf16[4,128,1024]{2,1,0:T(8,128)(2,1)}, bf16[4,128,1024]{2,1,0:T(8,128)(2,1)}, u32[]{:S(2)}, u32[]{:S(2)}) collective-permute-start(bf16[4,128,1024]{2,1,0:T(8,128)(2,1)} %bitcast.174), channel_id=1, source_target_pairs={{0,16},{4,20},{8,24},{12,28},{16,0},{20,4},{24,8},{28,12},{1,17},{... | collective-permute-start | bytes 3145736 | tf_op jit(solution)/shard_map/ppermute | solution.py:45
  129.9 76.4 %collective-permute-start.20 = (bf16[4,128,1024]{2,1,0:T(8,128)(2,1)}, bf16[4,128,1024]{2,1,0:T(8,128)(2,1)}, u32[]{:S(2)}, u32[]{:S(2)}) collective-permute-start(bf16[4,128,1024]{2,1,0:T(8,128)(2,1)} %bitcast.175), channel_id=1, source_target_pairs={{0,8},{4,12},{8,0},{12,4},{16,24},{20,28},{24,16},{28,20},{1,9},{5... | collective-permute-start | bytes 3145736 | tf_op jit(solution)/shard_map/ppermute | solution.py:45
  165.0 40.7 %collective-permute-start.12 = (bf16[3,128,640]{2,1,0:T(8,128)(2,1)S(1)}, bf16[3,128,640]{2,1,0:T(8,128)(2,1)S(1)}, u32[]{:S(2)}, u32[]{:S(2)}) collective-permute-start(bf16[3,128,640]{2,1,0:T(8,128)(2,1)S(1)} %slice.181), channel_id=1, source_target_pairs={{0,8},{4,12},{8,0},{12,4},{16,24},{20,28},{24,16},{28,20},{1,9},{5... | collective-permute-start | bytes 1474568 | tf_op jit(solution)/shard_map/ppermute | solution.py:45
  167.5 38.2 %collective-permute-start.13 = (bf16[3,128,640]{2,1,0:T(8,128)(2,1)S(1)}, bf16[3,128,640]{2,1,0:T(8,128)(2,1)}, u32[]{:S(2)}, u32[]{:S(2)}) collective-permute-start(bf16[3,128,640]{2,1,0:T(8,128)(2,1)S(1)} %slice.182), channel_id=1, source_target_pairs={{0,16},{4,20},{8,24},{12,28},{16,0},{20,4},{24,8},{28,12},{1,17},{... | collective-permute-start | bytes 1474568 | tf_op jit(solution)/shard_map/ppermute | solution.py:45
  169.1 45.4 %collective-permute-start.14 = (bf16[3,256,640]{2,1,0:T(8,128)(2,1)S(1)}, bf16[3,256,640]{2,1,0:T(8,128)(2,1)}, u32[]{:S(2)}, u32[]{:S(2)}) collective-permute-start(bf16[3,256,640]{2,1,0:T(8,128)(2,1)S(1)} %pad_maximum_fusion.4.rest_0_), channel_id=1, source_target_pairs={{0,4},{4,0},{8,12},{12,8},{16,20},{20,16},{24,28},{28,24},{1,5},{5... | collective-permute-start | bytes 2949128 | tf_op jit(solution)/shard_map/ppermute | solution.py:45
  210.4 180.0 %all-gather.9.cloned.1.call-start = ((), (), s32[]{:S(2)}) async-start(), calls=%async_computation.7 | async-start | bytes 5242880 | tf_op jit(solution)/shard_map/all_gather | solution.py:891
  214.5 31.1 %collective-permute-start.22 = (bf16[4,64,1024]{2,1,0:T(8,128)(2,1)}, bf16[4,64,1024]{2,1,0:T(8,128)(2,1)}, u32[]{:S(2)}, u32[]{:S(2)}) collective-permute-start(bf16[4,64,1024]{2,1,0:T(8,128)(2,1)} %slice.236), channel_id=1, source_target_pairs={{0,8},{4,12},{8,0},{12,4},{16,24},{20,28},{24,16},{28,20},{1,9},{5... | collective-permute-start | bytes 1572872 | tf_op jit(solution)/shard_map/ppermute | solution.py:45
  216.5 29.6 %collective-permute-start.23 = (bf16[4,64,1024]{2,1,0:T(8,128)(2,1)}, bf16[4,64,1024]{2,1,0:T(8,128)(2,1)}, u32[]{:S(2)}, u32[]{:S(2)}) collective-permute-start(bf16[4,64,1024]{2,1,0:T(8,128)(2,1)} %slice.237), channel_id=1, source_target_pairs={{0,16},{4,20},{8,24},{12,28},{16,0},{20,4},{24,8},{28,12},{1,17},{... | collective-permute-start | bytes 1572872 | tf_op jit(solution)/shard_map/ppermute | solution.py:45
  218.0 44.3 %collective-permute-start.24 = (bf16[4,128,1024]{2,1,0:T(8,128)(2,1)}, bf16[4,128,1024]{2,1,0:T(8,128)(2,1)}, u32[]{:S(2)}, u32[]{:S(2)}) collective-permute-start(bf16[4,128,1024]{2,1,0:T(8,128)(2,1)} %bitcast.176), channel_id=1, source_target_pairs={{0,4},{4,0},{8,12},{12,8},{16,20},{20,16},{24,28},{28,24},{1,5},{5... | collective-permute-start | bytes 3145736 | tf_op jit(solution)/shard_map/ppermute | solution.py:45
  218.0 44.3 %collective-permute-start.25 = (bf16[4,128,1024]{2,1,0:T(8,128)(2,1)}, bf16[4,128,1024]{2,1,0:T(8,128)(2,1)}, u32[]{:S(2)}, u32[]{:S(2)}) collective-permute-start(bf16[4,128,1024]{2,1,0:T(8,128)(2,1)} %collective-permute-done.20.rest_1_.rest_11_), channel_id=1, source_target_pairs={{0,4},{4,0},{8,12},{12,8},{16,20},{20,16},{24,28},{28,24},{1,5},{5... | collective-permute-start | bytes 3145736 | tf_op jit(solution)/shard_map/ppermute | solution.py:45
  218.5 43.8 %collective-permute-start.26 = (bf16[4,128,1024]{2,1,0:T(8,128)(2,1)}, bf16[4,128,1024]{2,1,0:T(8,128)(2,1)}, u32[]{:S(2)}, u32[]{:S(2)}) collective-permute-start(bf16[4,128,1024]{2,1,0:T(8,128)(2,1)} %collective-permute-done.21.rest_2_.rest_12_), channel_id=1, source_target_pairs={{0,4},{4,0},{8,12},{12,8},{16,20},{20,16},{24,28},{28,24},{1,5},{5... | collective-permute-start | bytes 3145736 | tf_op jit(solution)/shard_map/ppermute | solution.py:45
  288.6 25.6 %collective-permute-start.29 = (bf16[4,512,1024]{2,1,0:T(8,128)(2,1)}, bf16[4,512,1024]{2,1,0:T(8,128)(2,1)}, u32[]{:S(2)}, u32[]{:S(2)}) collective-permute-start(bf16[4,512,1024]{2,1,0:T(8,128)(2,1)} %down_grad_other.1), channel_id=1, source_target_pairs={{0,4},{4,0},{8,12},{12,8},{16,20},{20,16},{24,28},{28,24},{1,5},{5... | collective-permute-start | bytes 12582920 | tf_op jit(solution)/shard_map/ppermute | solution.py:45
  331.7 45.0 %collective-permute-start.30 = (bf16[4,128,5248]{2,1,0:T(8,128)(2,1)}, bf16[4,128,5248]{2,1,0:T(8,128)(2,1)}, u32[]{:S(2)}, u32[]{:S(2)}) collective-permute-start(bf16[4,128,5248]{2,1,0:T(8,128)(2,1)} %up_grad_other.1), channel_id=1, source_target_pairs={{0,4},{4,0},{8,12},{12,8},{16,20},{20,16},{24,28},{28,24},{1,5},{5... | collective-permute-start | bytes 16121864 | tf_op jit(solution)/shard_map/ppermute | solution.py:45
  331.7 25.6 %collective-permute-start.40 = (bf16[2,256,1024]{2,1,0:T(8,128)(2,1)S(1)}, bf16[2,256,1024]{2,1,0:T(8,128)(2,1)S(1)}, u32[]{:S(2)}, u32[]{:S(2)}) collective-permute-start(bf16[2,256,1024]{2,1,0:T(8,128)(2,1)S(1)} %get-tuple-element.106), channel_id=1, source_target_pairs={{0,8},{4,12},{8,0},{12,4},{16,24},{20,28},{24,16},{28,20},{1,9},{5... | collective-permute-start | bytes 3145736 | tf_op jit(solution)/shard_map/ppermute | solution.py:45
  331.7 26.2 %collective-permute-start.42 = (bf16[2,256,1024]{2,1,0:T(8,128)(2,1)S(1)}, bf16[2,256,1024]{2,1,0:T(8,128)(2,1)S(1)}, u32[]{:S(2)}, u32[]{:S(2)}) collective-permute-start(bf16[2,256,1024]{2,1,0:T(8,128)(2,1)S(1)} %get-tuple-element.108), channel_id=1, source_target_pairs={{0,16},{4,20},{8,24},{12,28},{16,0},{20,4},{24,8},{28,12},{1,17},{... | collective-permute-start | bytes 3145736 | tf_op jit(solution)/shard_map/ppermute | solution.py:45
  363.1 27.3 %all-to-all-start.1 = ((bf16[4,512,256]{2,1,0:T(8,128)(2,1)}), bf16[4,512,256]{2,1,0:T(8,128)(2,1)}, u32[]{:S(2)}, u32[]{:S(2)}) async-start(bf16[4,512,256]{2,1,0:T(8,128)(2,1)} %get-tuple-element.87), calls=%async_computation.1 | async-start | bytes 2097152 | tf_op jit(solution)/shard_map/all_to_all | solution.py:906
  367.3 143.4 %reduce-scatter.8.cloned.1.call-start = ((), (), s32[]{:S(2)}) async-start(), calls=%async_computation.10 | async-start | bytes 1310720 | tf_op jit(solution)/shard_map/reduce_scatter | solution.py:796
  376.6 135.9 %reduce-scatter.4.cloned.1.call-start = ((), (), s32[]{:S(2)}) async-start(), calls=%async_computation.8 | async-start | bytes 1146880 | tf_op jit(solution)/shard_map/reduce_scatter | solution.py:946
  388.4 75.4 %collective-permute-start.36 = (bf16[2,64,5248]{2,1,0:T(8,128)(2,1)}, bf16[2,64,5248]{2,1,0:T(8,128)(2,1)}, u32[]{:S(2)}, u32[]{:S(2)}) collective-permute-start(bf16[2,64,5248]{2,1,0:T(8,128)(2,1)} %get-tuple-element.98), channel_id=1, source_target_pairs={{0,8},{4,12},{8,0},{12,4},{16,24},{20,28},{24,16},{28,20},{1,9},{5... | collective-permute-start | bytes 4030472 | tf_op jit(solution)/shard_map/ppermute | solution.py:45
  389.5 76.7 %collective-permute-start.38 = (bf16[2,64,5248]{2,1,0:T(8,128)(2,1)}, bf16[2,64,5248]{2,1,0:T(8,128)(2,1)}, u32[]{:S(2)}, u32[]{:S(2)}) collective-permute-start(bf16[2,64,5248]{2,1,0:T(8,128)(2,1)} %get-tuple-element.100), channel_id=1, source_target_pairs={{0,16},{4,20},{8,24},{12,28},{16,0},{20,4},{24,8},{28,12},{1,17},{... | collective-permute-start | bytes 4030472 | tf_op jit(solution)/shard_map/ppermute | solution.py:45
  451.4 31.2 %collective-permute-start.32 = (bf16[4,256,1024]{2,1,0:T(8,128)(2,1)}, bf16[4,256,1024]{2,1,0:T(8,128)(2,1)S(1)}, u32[]{:S(2)}, u32[]{:S(2)}) collective-permute-start(bf16[4,256,1024]{2,1,0:T(8,128)(2,1)} %bitcast.53), channel_id=1, source_target_pairs={{0,4},{4,0},{8,12},{12,8},{16,20},{20,16},{24,28},{28,24},{1,5},{5... | collective-permute-start | bytes 6291464 | tf_op jit(solution)/shard_map/ppermute | solution.py:45
  463.8 61.2 %reduce-scatter.6.cloned.1.call-start = ((), (), s32[]{:S(2)}) async-start(), calls=%async_computation.9 | async-start | bytes 1679360 | tf_op jit(solution)/shard_map/reduce_scatter | solution.py:796
  (72 other events, 1161.8 us)
Sparse Core Ops, SparseCore 0:
  24.8 59.0 all-gather.10
  85.8 27.4 all-gather.12
  126.4 58.3 all-gather.6
  289.2 31.7 all-gather.8
  376.7 23.4 reduce-scatter.7
  463.9 21.4 reduce-scatter.3
  487.8 30.8 reduce-scatter.5

commit v2 on v1

v2 whole, which is shorter than its diff:
```python
from functools import partial
import math

import jax
import jax.numpy as jnp
from jax import lax
from jax.experimental import pallas as pl
from jax.experimental.pallas import tpu as pltpu
from jax.sharding import PartitionSpec as P

D = 1024
H = 16
HD = 64
BLK = 128
MB = 2

NEGATIVE = -1e30
EPSILON = 1e-05
BF = jnp.bfloat16
F32 = jnp.float32


def contract(a, b, ca, cb):
    return lax.dot_general(a, b, (((ca,), (cb,)), ((), ())), preferred_element_type=F32)


def norm_forward(values_in, gain_vec, shift_vec):
    center = values_in - jnp.mean(values_in, -1, keepdims=True)
    inverse = lax.rsqrt(jnp.mean(center * center, -1, keepdims=True) + EPSILON)
    normed = center * inverse
    return (normed * gain_vec + shift_vec, normed, inverse)


def norm_backward(grad_out, normed, inverse, gain_vec):
    grad_norm = grad_out * gain_vec
    return inverse * (
        grad_norm
        - jnp.mean(grad_norm, -1, keepdims=True)
        - normed * jnp.mean(grad_norm * normed, -1, keepdims=True)
    )


def hop(value, mask):
    count = lax.axis_size("ctx")
    return lax.ppermute(value, "ctx", [(i, i ^ mask) for i in range(count)])


VMEM = pl.BlockSpec(memory_space=pltpu.VMEM)
SMEM = pl.BlockSpec(memory_space=pltpu.SMEM)
HBM = pl.BlockSpec(memory_space=pltpu.HBM)


def takes(microseconds):
    return pl.CostEstimate(
        flops=int(microseconds * 1.15e9), bytes_accessed=1 << 20, transcendentals=0
    )


def params(mib):
    return pltpu.CompilerParams(vmem_limit_bytes=mib << 20)


def struct(shape, dtype):
    return jax.ShapeDtypeStruct(shape, dtype)


ME, LOW, TOP, SHARD, CORE, CHIP, SPLIT, ORDER, INVERSE = 0, 1, 2, 3, 7, 8, 9, 10, 26
CHUNKS = (0, 4, 2, 6, 1, 5, 3, 7)
ROWS = 512


def scalars(order, lengths):
    me = lax.axis_index("ctx")
    shard = lax.axis_index("fsdp")
    core, low, top = me % 2, me % 4, me // 4
    order_row = jnp.where(top == 0, order[0, 0], order[1, 0])
    first = jnp.where(top == 0, lengths[0, 0, 0], lengths[1, 0, 0])
    blocks = jnp.arange(16, dtype=jnp.int32)
    inverse = jnp.sum(jnp.where(order_row[None, :] == blocks[:, None], blocks[None, :], 0), 1)
    others = [(shard + 4 - k) % 4 for k in (1, 2, 3)]
    return jnp.concatenate(
        [jnp.stack([me, low, top, shard, *others, core, me // 2, first]), order_row, inverse]
    ).astype(jnp.int32)


def start_all(copies):
    for copy in copies:
        copy.start()


def wait_all(copies):
    for copy in copies:
        copy.wait()


def copies_of(pairs, sems, base=0):
    return [
        pltpu.make_async_copy(a, b, sems.at[base + i]) for i, (a, b) in enumerate(pairs)
    ]


def aligned(start, size):
    return pl.ds(pl.multiple_of(start, size), size)


def segment_lanes(first, rows, split, is_query):
    position = first + lax.broadcasted_iota(jnp.int32, (rows, HD), 0)
    lane = lax.broadcasted_iota(jnp.int32, (rows, HD), 1)
    second = (position >= split).astype(jnp.int32)
    if is_query:
        return jnp.where(lane == 1 - second, NEGATIVE, 0.0).astype(BF)
    return jnp.where(lane == second, 1.0, 0.0).astype(BF)


def key_range(q0, bq, split, bk, total):
    begin = jnp.where(q0 >= split, split // bk, 0)
    end = jnp.where(q0 + bq <= split, (split + bk - 1) // bk, total // bk)
    return begin, end


def widen(scal, qkv, qa, ka, begin, heads, chunk):
    total = qkv.shape[0]
    width = qkv.shape[1] // 3
    split = scal[SPLIT]
    for m in range(total // chunk):
        pos = pl.multiple_of((scal[ME] ^ CHUNKS[m]) * chunk, chunk)
        rows = slice(m * chunk, (m + 1) * chunk)
        qtail = segment_lanes(pos, chunk, split, True)
        ktail = segment_lanes(pos, chunk, split, False)
        for h in range(heads):
            at = begin + h * HD
            q = qkv[rows, at : at + HD]
            k = qkv[rows, width + at : width + at + HD]
            q = (q.astype(F32) * 0.125).astype(BF)
            qa[h, pl.ds(pos, chunk), :] = jnp.concatenate([q, qtail], 1)
            ka[h, pl.ds(pos, chunk), :] = jnp.concatenate([k, ktail], 1)


def attention_forward_kernel(
    scal, qkv, out0, out1, out2, out3, out_t, lse, qa, ka, vt, sc, out, *, heads, chunk, bq, bk
):
    total = qkv.shape[0]
    width = qkv.shape[1] // 3
    split = scal[SPLIT]
    widen(scal, qkv, qa, ka, 0, heads, chunk)
    for m in range(total // chunk):
        pos = pl.multiple_of((scal[ME] ^ CHUNKS[m]) * chunk, chunk)
        rows = slice(m * chunk, (m + 1) * chunk)
        vt[:, pl.ds(pos, chunk)] = qkv[rows, 2 * width :].T

    def q_step(qi, _):
        q0 = pl.multiple_of(qi * bq, bq)
        begin_k, end_k = key_range(q0, bq, split, bk, total)

        def max_step(ki, carry):
            k0 = pl.multiple_of(ki * bk, bk)
            result = []
            for h in range(heads):
                st = contract(ka[h, pl.ds(k0, bk), :], qa[h, pl.ds(q0, bq), :], 1, 1)
                sc[h, pl.ds(k0, bk), :] = st
                result.append(jnp.maximum(carry[h], jnp.max(st.reshape(bk // 8, 8, bq), 0)))
            return tuple(result)

        start = tuple(jnp.full((8, bq), NEGATIVE, F32) for _ in range(heads))
        peaks = lax.fori_loop(begin_k, end_k, max_step, start)
        peaks = [jnp.max(m, 0, keepdims=True) for m in peaks]

        def k_step(ki, carry):
            k0 = pl.multiple_of(ki * bk, bk)
            result = []
            for h in range(heads):
                total_p, acc = carry[2 * h : 2 * h + 2]
                p = jnp.exp(sc[h, pl.ds(k0, bk), :] - peaks[h])
                total_p = total_p + jnp.sum(p.reshape(bk // 8, 8, bq), 0)
                acc = acc + contract(
                    vt[h * HD : (h + 1) * HD, pl.ds(k0, bk)], p.astype(BF), 1, 0
                )
                result += [total_p, acc]
            return tuple(result)

        start = []
        for h in range(heads):
            start += [jnp.zeros((8, bq), F32), jnp.zeros((HD, bq), F32)]
        done = lax.fori_loop(begin_k, end_k, k_step, tuple(start))
        pieces = []
        for h in range(heads):
            denom = jnp.sum(done[2 * h], 0, keepdims=True)
            pieces.append(done[2 * h + 1] / denom)
            lse[h : h + 1, pl.ds(q0, bq)] = peaks[h] + jnp.log(denom)
        turned = jnp.concatenate(pieces, 0)
        out_t[:, pl.ds(q0, bq)] = turned
        low_rows = turned.T.astype(BF)
        for i in range(bq // BLK):
            place = scal[INVERSE + q0 // BLK + i]
            device = place // 2
            row = ((device // 4) ^ scal[TOP]) * 256 + (place % 2) * BLK
            out[(device % 4) ^ scal[LOW], aligned(row, BLK), :] = low_rows[
                i * BLK : (i + 1) * BLK
            ]
        return 0

    lax.fori_loop(0, total // bq, q_step, 0)
    for k, sent in enumerate((out0, out1, out2, out3)):
        sent[...] = out[k]


def attention_forward(scal, qkv, chunk, bq=512, bk=512):
    total = qkv.shape[0]
    width = qkv.shape[1] // 3
    heads = width // HD
    return pl.pallas_call(
        partial(attention_forward_kernel, heads=heads, chunk=chunk, bq=bq, bk=bk),
        out_shape=(struct((ROWS, width), BF),) * 4
        + (struct((width, total), F32), struct((heads, total), F32)),
        in_specs=[SMEM, VMEM],
        out_specs=(VMEM,) * 6,
        scratch_shapes=[
            pltpu.VMEM((heads, total, 128), BF),
            pltpu.VMEM((heads, total, 128), BF),
            pltpu.VMEM((width, total), BF),
            pltpu.VMEM((heads, total, bq), F32),
            pltpu.VMEM((4, ROWS, width), BF),
        ],
        compiler_params=params(60),
        cost_estimate=takes(23),
        name="attention_forward",
    )(scal, qkv)


def attention_backward_kernel(
    scal, qkv, grad0, grad1, grad2, grad3, out_t, lse, dqkv, qa, ka, kt, va, ga, gt, dkv, dq,
    *, first, heads, chunk, bq, bk
):
    total = qkv.shape[0]
    width = qkv.shape[1] // 3
    begin = first * HD
    end = begin + heads * HD
    split = scal[SPLIT]
    blank = jnp.zeros((chunk, HD), BF)
    short = jnp.zeros((BLK, HD), BF)
    widen(scal, qkv, qa, ka, begin, heads, chunk)
    for m in range(total // chunk):
        pos = pl.multiple_of((scal[ME] ^ CHUNKS[m]) * chunk, chunk)
        rows = slice(m * chunk, (m + 1) * chunk)
        for h in range(heads):
            at = 2 * width + begin + h * HD
            va[h, pl.ds(pos, chunk), :] = jnp.concatenate([qkv[rows, at : at + HD], blank], 1)
        kt[:, pl.ds(pos, chunk)] = qkv[rows, width + begin : width + end].T
    for k, grad in enumerate((grad0, grad1, grad2, grad3)):
        for e in range(4):
            device = (scal[LOW] ^ k) + 4 * ((e // 2) ^ scal[TOP])
            pos = pl.multiple_of(scal[ORDER + 2 * device + e % 2] * BLK, BLK)
            rows = slice(e * BLK, (e + 1) * BLK)
            for h in range(heads):
                g = grad[rows, begin + h * HD : begin + (h + 1) * HD]
                ga[h, pl.ds(pos, BLK), :] = jnp.concatenate([g, short], 1)
            gt[:, pl.ds(pos, BLK)] = grad[rows, begin:end].T
    dkv[...] = jnp.zeros_like(dkv)

    def q_step(qi, _):
        q0 = pl.multiple_of(qi * bq, bq)
        begin_k, end_k = key_range(q0, bq, split, bk, total)
        product = gt[:, pl.ds(q0, bq)].astype(F32) * out_t[begin:end, pl.ds(q0, bq)]
        delta = [jnp.sum(product[h * HD : (h + 1) * HD], 0, keepdims=True) for h in range(heads)]
        held_lse = lse[:, pl.ds(q0, bq)]
        totals = [held_lse[first + h : first + h + 1] for h in range(heads)]

        def k_step(ki, carry):
            k0 = pl.multiple_of(ki * bk, bk)
            result = []
            for h in range(heads):
                q = qa[h, pl.ds(q0, bq), :]
                g = ga[h, pl.ds(q0, bq), :]
                st = contract(ka[h, pl.ds(k0, bk), :], q, 1, 1)
                p = jnp.exp(st - totals[h])
                dp = contract(va[h, pl.ds(k0, bk), :], g, 1, 1)
                ds = (p * (dp - delta[h]) * 0.125).astype(BF)
                dkv[0, h, pl.ds(k0, bk), :] += contract(ds, q, 1, 0)
                dkv[1, h, pl.ds(k0, bk), :] += contract(p.astype(BF), g, 1, 0)
                result.append(
                    carry[h] + contract(kt[h * HD : (h + 1) * HD, pl.ds(k0, bk)], ds, 1, 0)
                )
            return tuple(result)

        start = tuple(jnp.zeros((HD, bq), F32) for _ in range(heads))
        turned = lax.fori_loop(begin_k, end_k, k_step, start)
        dq[pl.ds(q0, bq), :] = jnp.concatenate(turned, 0).T.astype(BF)
        return 0

    lax.fori_loop(0, total // bq, q_step, 0)
    for m in range(total // chunk):
        pos = pl.multiple_of((scal[ME] ^ CHUNKS[m]) * chunk, chunk)
        rows = slice(m * chunk, (m + 1) * chunk)
        dqkv[rows, 0 : heads * HD] = dq[pl.ds(pos, chunk), :]
        for h in range(0, heads, 2):
            for part, gain in ((0, 8.0), (1, 1.0)):
                pair = [dkv[part, h + e, pl.ds(pos, chunk), :][:, :HD] for e in range(2)]
                base = ((1 + part) * heads + h) * HD
                dqkv[rows, base : base + 2 * HD] = (jnp.concatenate(pair, 1) * gain).astype(BF)


def attention_backward(scal, qkv, grads, out_t, lse, chunk, first, heads, bq=512, bk=512):
    total = qkv.shape[0]
    width = heads * HD
    wide = pltpu.VMEM((heads, total, 128), BF)
    return pl.pallas_call(
        partial(
            attention_backward_kernel, first=first, heads=heads, chunk=chunk, bq=bq, bk=bk
        ),
        out_shape=struct((total, 3 * width), BF),
        in_specs=[SMEM] + [VMEM] * 7,
        out_specs=VMEM,
        scratch_shapes=[
            wide,
            wide,
            pltpu.VMEM((width, total), BF),
            wide,
            wide,
            pltpu.VMEM((width, total), BF),
            pltpu.VMEM((2, heads, total, 128), F32),
            pltpu.VMEM((total, width), BF),
        ],
        compiler_params=params(60),
        cost_estimate=takes(19),
        name="attention_backward",
    )(scal, qkv, *grads, out_t, lse)


def carve_kernel(
    tokens, cot, w_qkv, w_out, w_up, w_down, small,
    own, other, cot_own, cot_other, pack, pack_sent, up_slice, down_slice, sems,
):
    me = lax.axis_index("ctx")
    core, low, top, chip = me % 2, me % 4, me // 4, me // 2
    block = core * 4 + chip
    pairs = [(tokens.at[top, 0], own), (tokens.at[1 - top, 0], other)]
    half = aligned(top * 128, 128)
    for k in range(3):
        columns = aligned(k * D + low * 256, 256)
        target = slice(256 * k, 256 * (k + 1))
        pairs.append((w_qkv.at[:, columns], pack.at[:, target]))
        pairs.append((w_qkv.at[half, columns], pack_sent.at[0:128, target]))
    for k in range(4):
        columns = aligned(k * D + block * 128, 128)
        pairs.append((w_up.at[:, columns], up_slice.at[:, 128 * k : 128 * (k + 1)]))
    pairs.append((w_out.at[:, aligned(block * 128, 128)], up_slice.at[:, 512:640]))
    pairs.append((w_down.at[aligned(core * 512 + top * 128, 128), :], down_slice.at[0]))
    side = core * 512 + 256 + (chip % 2) * 128
    pairs.append((w_down.at[aligned(side, 128), :], down_slice.at[1]))
    pairs += [(cot.at[top, 0], cot_own), (cot.at[1 - top, 0], cot_other)]
    copies = copies_of(pairs, sems)
    start_all(copies)
    pack_sent[128:144, 0:256] = small[...]
    wait_all(copies)


def carve(tokens, cot, w_qkv, w_out, w_up, w_down, small):
    rows = tokens.shape[2]
    return pl.pallas_call(
        carve_kernel,
        out_shape=tuple(struct((rows, D), BF) for _ in range(4))
        + (
            struct((256, 768), BF),
            struct((144, 768), BF),
            struct((256, 640), BF),
            struct((2, 128, D), BF),
        ),
        in_specs=[HBM] * 6 + [VMEM],
        out_specs=(VMEM,) * 8,
        scratch_shapes=[pltpu.SemaphoreType.DMA((17,))],
        compiler_params=params(60),
        cost_estimate=takes(4),
        name="carve",
    )(tokens, cot, w_qkv, w_out, w_up, w_down, small)


def project_kernel(
    scal, pack, small, near, away, own, y, x, core_own, core_rest,
    qkv, x_all, weight, vecs, up_bias, qkv_held, x_held, rows_held, sems, out_sems,
):
    chunk = own.shape[0]
    own_f = scal[SHARD]
    pairs = [(pack, weight.at[aligned(own_f * 256, 256)]), (small, rows_held.at[own_f])]
    for k in range(3):
        f = scal[SHARD + 1 + k]
        mine = aligned(f * 256 + scal[TOP] * 128, 128)
        rest = aligned(f * 256 + (1 - scal[TOP]) * 128, 128)
        pairs.append((near.at[k, 0:128], weight.at[mine]))
        pairs.append((away.at[k, 0:128], weight.at[rest]))
        pairs.append((near.at[k, 128:144, 0:256], rows_held.at[f]))
    loads = len(pairs)
    sources = [own, y, x.at[0], x.at[1], core_own] + [core_rest.at[k] for k in range(3)]
    pairs += [
        (piece, x_held.at[m * chunk : (m + 1) * chunk]) for m, piece in enumerate(sources)
    ]
    copies = copies_of(pairs, sems)
    start_all(copies)
    wait_all(copies[:loads])
    for f in range(4):
        held = rows_held[f].astype(F32)
        vecs[:, 256 * f : 256 * (f + 1)] = held[0:8]
        for j in range(4):
            for e in range(2):
                up_bias[2 * j + e : 2 * j + e + 1, 128 * f : 128 * (f + 1)] = held[
                    8 + j : 9 + j, 128 * e : 128 * (e + 1)
                ]
    here = aligned(scal[LOW] * 256, 256)
    bias = jnp.concatenate([vecs[0:1, here], jnp.zeros((1, 256), F32), vecs[1:2, here]], 1)
    outs = []
    for m in range(8):
        copies[loads + m].wait()
        rows = slice(m * chunk, (m + 1) * chunk)
        qkv_held[rows, :] = (contract(x_held[rows, :], weight[...], 1, 0) + bias).astype(BF)
        sent = copies_of(
            [(x_held.at[rows], x_all.at[rows]), (qkv_held.at[rows], qkv.at[rows])], out_sems, 2 * m
        )
        start_all(sent)
        outs += sent
    wait_all(outs)


def project(scal, pack, small, near, away, pieces):
    chunk = pieces[0].shape[0]
    return pl.pallas_call(
        project_kernel,
        out_shape=(
            struct((8 * chunk, 768), BF),
            struct((8 * chunk, D), BF),
            struct((D, 768), BF),
            struct((8, D), F32),
            struct((8, 512), F32),
        ),
        in_specs=[SMEM] + [HBM] * 9,
        out_specs=(HBM, HBM, VMEM, VMEM, VMEM),
        scratch_shapes=[
            pltpu.VMEM((8 * chunk, 768), BF),
            pltpu.VMEM((8 * chunk, D), BF),
            pltpu.VMEM((4, 16, 256), BF),
            pltpu.SemaphoreType.DMA((19,)),
            pltpu.SemaphoreType.DMA((16,)),
        ],
        compiler_params=params(60),
        cost_estimate=takes(8),
        name="project",
    )(scal, pack, small, near, away, *pieces)


def out_pairs(scal, near, away, w_out, held):
    pairs = []
    for side, pieces in enumerate((near, away)):
        for m in range(4):
            block = 4 * (scal[CORE] ^ side) + (scal[CHIP] ^ m)
            for k in range(3):
                rows = aligned(scal[SHARD + 1 + k] * 256, 256)
                pairs.append((pieces.at[m, k], held.at[block, rows]))
            columns = aligned(block * 128, 128)
            rows = aligned(scal[SHARD] * 256, 256)
            pairs.append((w_out.at[:, columns], held.at[block, rows]))
    return pairs


def attention_out_kernel(
    scal, h0, h1, h2, h3, vecs, x_all, w_out, near, away, y1, y1_low, n1, r1, held, x, sems
):
    pairs = out_pairs(scal, near, away, w_out, held)
    for e in range(4):
        device = scal[ME] ^ (4 * (e // 2))
        given = scal[ORDER + 2 * device + e % 2]
        turn = scal[ME] ^ (given // 2)
        chunk = (turn % 2) * 4 + ((turn // 2) % 2) * 2 + turn // 4
        rows = aligned(chunk * 256 + (given % 2) * BLK, BLK)
        pairs.append((x_all.at[rows, :], x.at[e * BLK : (e + 1) * BLK]))
    copies = copies_of(pairs, sems)
    start_all(copies)
    wait_all(copies)
    columns = []
    for b in range(8):
        part = 0.0
        for k, heads in enumerate((h0, h1, h2, h3)):
            rows = aligned((scal[LOW] ^ k) * 256, 256)
            part = part + contract(heads[...], held[b, rows, :], 1, 0)
        columns.append(part)
    into = x[...].astype(F32) + jnp.concatenate(columns, 1) + vecs[2:3]
    out, normed, inverse = norm_forward(into, vecs[3:4], vecs[4:5])
    y1[...] = out
    y1_low[...] = out.astype(BF)
    n1[...] = normed
    r1[...] = jnp.broadcast_to(inverse, r1.shape)


def attention_out(scal, heads, vecs, x_all, w_out, near, away):
    return pl.pallas_call(
        attention_out_kernel,
        out_shape=(
            struct((ROWS, D), F32),
            struct((ROWS, D), BF),
            struct((ROWS, D), F32),
            struct((ROWS, 128), F32),
        ),
        in_specs=[SMEM] + [VMEM] * 5 + [HBM] * 4,
        out_specs=(VMEM,) * 4,
        scratch_shapes=[
            pltpu.VMEM((8, D, 128), BF),
            pltpu.VMEM((ROWS, D), BF),
            pltpu.SemaphoreType.DMA((36,)),
        ],
        compiler_params=params(60),
        cost_estimate=takes(9),
        name="attention_out",
    )(scal, *heads, vecs, x_all, w_out, near, away)


def up_pairs(scal, pieces, w_up, held):
    own, from_x, from_y, far_a, far_b = pieces
    groups = [[] for _ in range(4)]
    for k in range(3):
        base = scal[SHARD + 1 + k] * 256
        for m, piece in enumerate((own, from_x, from_y)):
            target = held.at[scal[CHIP] ^ m, aligned(base, 256)]
            groups[m].append((piece.at[k, :, 0:512], target))
        for half, piece in enumerate((far_a, far_b)):
            target = held.at[scal[CHIP] ^ 3, aligned(base + 128 * half, 128)]
            groups[3].append((piece.at[k, :, 0:512], target))
    rows = aligned(scal[SHARD] * 256, 256)
    for m in range(4):
        chip = scal[CHIP] ^ m
        for k in range(4):
            columns = aligned(k * D + (scal[CORE] * 4 + chip) * 128, 128)
            target = held.at[chip, rows, 128 * k : 128 * (k + 1)]
            groups[m].append((w_up.at[:, columns], target))
    return groups


UP_COPIES = 3 * 7 + 10


def grouped_copies(groups, sems, base=0):
    result = []
    for group in groups:
        result.append(copies_of(group, sems, base))
        base += len(group)
    return result


def down_pairs(scal, own, from_y, from_x, held):
    side = scal[CHIP] % 2
    pairs = []
    for f in range(4):
        rows = slice(128 * f, 128 * (f + 1))
        pairs.append((own.at[f, 0], held.at[scal[TOP], rows]))
        pairs.append((own.at[f, 1], held.at[2 + side, rows]))
        pairs.append((from_y.at[f], held.at[1 - scal[TOP], rows]))
        pairs.append((from_x.at[f], held.at[3 - side, rows]))
    return pairs


DOWN_COPIES = 16


def up_kernel(scal, y1_low, up_bias, w_up, *rest):
    pieces, (act, slope, held, act_held, slope_held, sems, out_sems) = rest[:5], rest[5:]
    groups = grouped_copies(up_pairs(scal, pieces, w_up, held), sems)
    for group in groups:
        start_all(group)
    outs = []
    for m, group in enumerate(groups):
        wait_all(group)
        q = scal[CHIP] ^ m
        bias = up_bias[pl.ds(scal[CORE] * 4 + q, 1), :]
        for r in (slice(0, 256), slice(256, 512)):
            u = contract(y1_low[r, :], held[q], 1, 0) + bias
            cdf = 0.5 * (1.0 + lax.erf(u * (1.0 / math.sqrt(2.0))))
            density = jnp.exp(-0.5 * u * u) * (1.0 / math.sqrt(2.0 * math.pi))
            slope_held[q, r, :] = (cdf + u * density).astype(BF)
            act_held[q, r, :] = (u * cdf).astype(BF)
        copies = copies_of(
            [(act_held.at[q], act.at[q]), (slope_held.at[q], slope.at[q])], out_sems, 2 * m
        )
        start_all(copies)
        outs += copies
    wait_all(outs)


def feed_up(scal, y1_low, up_bias, w_up, pieces):
    block = pltpu.VMEM((4, ROWS, 512), BF)
    return pl.pallas_call(
        up_kernel,
        out_shape=(struct((4, ROWS, 512), BF), struct((4, ROWS, 512), BF)),
        in_specs=[SMEM, VMEM, VMEM] + [HBM] * 6,
        out_specs=(HBM, HBM),
        scratch_shapes=[
            pltpu.VMEM((4, D, 512), BF),
            block,
            block,
            pltpu.SemaphoreType.DMA((UP_COPIES,)),
            pltpu.SemaphoreType.DMA((8,)),
        ],
        compiler_params=params(60),
        cost_estimate=takes(7),
        name="feed_up",
    )(scal, y1_low, up_bias, w_up, *pieces)


def down_kernel(scal, act, own, from_y, from_x, part, held, act_held, total, sems):
    pairs = down_pairs(scal, own, from_y, from_x, held)
    copies = copies_of(pairs, sems)
    acts = copies_of([(act.at[q], act_held.at[q]) for q in range(4)], sems, DOWN_COPIES)
    start_all(copies)
    start_all(acts)
    wait_all(copies)
    for q in range(4):
        acts[q].wait()
        moved = contract(act_held[q], held[q], 1, 0)
        if q == 0:
            total[...] = moved
        elif q < 3:
            total[...] += moved
        else:
            part[...] = (total[...] + moved).astype(part.dtype)


def feed_down(scal, act, pieces, dtype):
    return pl.pallas_call(
        down_kernel,
        out_shape=struct((ROWS, D), dtype),
        in_specs=[SMEM] + [HBM] * 4,
        out_specs=VMEM,
        scratch_shapes=[
            pltpu.VMEM((4, 512, D), BF),
            pltpu.VMEM((4, ROWS, 512), BF),
            pltpu.VMEM((ROWS, D), F32),
            pltpu.SemaphoreType.DMA((DOWN_COPIES + 4,)),
        ],
        compiler_params=params(60),
        cost_estimate=takes(5),
        name="feed_down",
    )(scal, act, *pieces)


def second_norm_kernel(y1, part, came, cot_own, cot_came, vecs, out_own, out_away, dh2, dz2, sums):
    n = pl.program_id(0)
    h2 = y1[...] + part[...] + came[...].astype(F32) + vecs[5:6]
    out, normed, inverse = norm_forward(h2, vecs[6:7], vecs[7:8])
    out = out.astype(BF)
    c = jnp.where(n < 2, cot_own[...], cot_came[...]).astype(F32)
    grad = norm_backward(c, normed, inverse, vecs[6:7])
    dh2[...] = grad
    low = grad.astype(BF)
    dz2[...] = low

    @pl.when(n == 0)
    def _():
        sums[...] = jnp.zeros_like(sums)

    for i, value in enumerate((c * normed, c, low.astype(F32))):
        sums[i : i + 1, :] += jnp.sum(value, 0, keepdims=True)

    @pl.when(n < 2)
    def _():
        out_own[...] = out

    @pl.when(n >= 2)
    def _():
        out_away[...] = out


def second_norm(y1, part, came, cot_own, cot_came, vecs):
    half = struct((ROWS // 2, D), BF)
    rows = pl.BlockSpec((128, D), lambda n: (n, 0))
    first = pl.BlockSpec((128, D), lambda n: (jnp.minimum(n, 1), 0))
    last = pl.BlockSpec((128, D), lambda n: (jnp.maximum(n - 2, 0), 0))
    whole = pl.BlockSpec((8, D), lambda n: (0, 0))
    return pl.pallas_call(
        second_norm_kernel,
        grid=(4,),
        out_shape=(half, half, struct((ROWS, D), F32), struct((ROWS, D), BF), struct((8, D), F32)),
        in_specs=[rows, rows, rows, first, last, whole],
        out_specs=(first, last, rows, rows, whole),
        compiler_params=params(60),
        cost_estimate=takes(4),
        name="second_norm",
    )(y1, part, came, cot_own, cot_came, vecs)


def back_kernel(scal, dz2_a, dz2_b, slope_a, slope_b, w_up, *rest):
    ups, downs, outs, scratch = rest[:5], rest[5:8], rest[8:13], rest[13:]
    du_a, du_b, part_a, part_b, up_sums = outs
    up_held, down_held, slopes, dus, acc_a, acc_b, sems, out_sems = scratch
    down_copies = copies_of(down_pairs(scal, *downs, down_held), sems)
    groups = grouped_copies(up_pairs(scal, ups, w_up, up_held), sems, DOWN_COPIES)
    loads = []
    for m in range(4):
        q = scal[CHIP] ^ m
        pairs = [(slope_b.at[q], slopes.at[1, q]), (slope_a.at[q], slopes.at[0, q])]
        loads.append(copies_of(pairs, sems, DOWN_COPIES + UP_COPIES + 2 * m))
    start_all(down_copies)
    for group, load in zip(groups, loads):
        start_all(load)
        start_all(group)
    wait_all(down_copies)
    sent = []
    for m in range(4):
        wait_all(loads[m])
        wait_all(groups[m])
        q = scal[CHIP] ^ m
        total = jnp.zeros((1, 512), F32)
        for side, (dz2, du, acc) in enumerate(((dz2_a, du_a, acc_a), (dz2_b, du_b, acc_b))):
            for r in (slice(0, 256), slice(256, 512)):
                low = contract(dz2[r, :], down_held[q], 1, 1) * slopes[side, q, r, :].astype(F32)
                low = low.astype(BF)
                dus[side, q, r, :] = low
                total = total + jnp.sum(low.astype(F32), 0, keepdims=True)
                moved = contract(low, up_held[q], 1, 1)
                if m == 0:
                    acc[r, :] = moved
                else:
                    acc[r, :] += moved
            copies = copies_of([(dus.at[side, q], du.at[q])], out_sems, 2 * m + side)
            start_all(copies)
            sent += copies
        up_sums[pl.ds(q, 1), :] = total
    part_a[...] = acc_a[...]
    part_b[...] = acc_b[...].astype(BF)
    wait_all(sent)


def feed_back(scal, dz2s, slopes, w_up, ups, downs):
    du = struct((4, ROWS, 512), BF)
    return pl.pallas_call(
        back_kernel,
        out_shape=(
            du, du, struct((ROWS, D), F32), struct((ROWS, D), BF), struct((8, 512), F32)
        ),
        in_specs=[SMEM, VMEM, VMEM] + [HBM] * 11,
        out_specs=(HBM, HBM, VMEM, VMEM, VMEM),
        scratch_shapes=[
            pltpu.VMEM((4, D, 512), BF),
            pltpu.VMEM((4, 512, D), BF),
            pltpu.VMEM((2, 4, ROWS, 512), BF),
            pltpu.VMEM((2, 4, ROWS, 512), BF),
            pltpu.VMEM((ROWS, D), F32),
            pltpu.VMEM((ROWS, D), F32),
            pltpu.SemaphoreType.DMA((DOWN_COPIES + UP_COPIES + 8,)),
            pltpu.SemaphoreType.DMA((8,)),
        ],
        compiler_params=params(60),
        cost_estimate=takes(22),
        name="feed_back",
    )(scal, *dz2s, *slopes, w_up, *ups, *downs)


def first_norm_kernel(
    scal, dh2, part, came, n1, r1, vecs, w_out, near, away, dao, g0, g1, g2, g3, sums, held, sems
):
    copies = copies_of(out_pairs(scal, near, away, w_out, held), sems)
    start_all(copies)
    dy1 = dh2[...] + part[...] + came[...].astype(F32)
    normed = n1[...]
    low = norm_backward(dy1, normed, r1[:, 0:1], vecs[3:4]).astype(BF)
    dao[...] = low
    sums[0:1, :] = jnp.sum(dy1 * normed, 0, keepdims=True)
    sums[1:2, :] = jnp.sum(dy1, 0, keepdims=True)
    sums[2:3, :] = jnp.sum(low.astype(F32), 0, keepdims=True)
    wait_all(copies)
    for k, out in enumerate((g0, g1, g2, g3)):
        rows = aligned((scal[LOW] ^ k) * 256, 256)
        total = 0.0
        for b in range(0, 8, 2):
            weight = jnp.concatenate([held[b, rows, :], held[b + 1, rows, :]], 1)
            total = total + contract(dao[:, b * 128 : (b + 2) * 128], weight, 1, 1)
        out[...] = total.astype(BF)


def first_norm(scal, dh2, part, came, n1, r1, vecs, w_out, near, away):
    return pl.pallas_call(
        first_norm_kernel,
        out_shape=(struct((ROWS, D), BF),) + (struct((ROWS, 256), BF),) * 4 + (struct((8, D), F32),),
        in_specs=[SMEM] + [VMEM] * 6 + [HBM] * 3,
        out_specs=(VMEM,) * 6,
        scratch_shapes=[pltpu.VMEM((8, D, 128), BF), pltpu.SemaphoreType.DMA((32,))],
        compiler_params=params(60),
        cost_estimate=takes(7),
        name="first_norm",
    )(scal, dh2, part, came, n1, r1, vecs, w_out, near, away)


def split_write(n, block, a_keep, a_send, b_keep, b_send):
    half = a_keep.shape[1]
    top_rows, low_rows = block[:half], block[half:]
    for step in range(4):

        @pl.when(n == step)
        def _():
            (a_send if step in (1, 3) else a_keep)[0] = top_rows
            (b_send if step in (2, 3) else b_keep)[0] = low_rows


def split_specs(rows, columns):
    half = (1, rows // 2, columns)
    return (
        pl.BlockSpec(half, lambda n, s: (n // 2, 0, 0)),
        pl.BlockSpec(half, lambda n, s: (n // 2, 0, 0)),
        pl.BlockSpec(half, lambda n, s: (jnp.minimum(n, 1), 0, 0)),
        pl.BlockSpec(half, lambda n, s: (jnp.maximum(n - 2, 0), 0, 0)),
    )


def split_shapes(rows, columns):
    return (struct((2, rows // 2, columns), BF),) * 4


def down_grad_kernel(scal, act_a, act_b, dz2_a, dz2_b, *outs):
    left = [jnp.concatenate([act[f] for f in range(4)], 1) for act in (act_a, act_b)]
    rows = contract(left[0], dz2_a[...], 0, 0) + contract(left[1], dz2_b[...], 0, 0)
    split_write(pl.program_id(0), rows.astype(BF), *outs)


def down_grad(scal, acts, dz2s):
    act_spec = pl.BlockSpec((4, ROWS, 128), lambda n, s: (0, 0, s[CHIP] ^ n))
    dz2_spec = pl.BlockSpec((ROWS, D), lambda n, s: (0, 0))
    return pl.pallas_call(
        down_grad_kernel,
        out_shape=split_shapes(512, D),
        grid_spec=pltpu.PrefetchScalarGridSpec(
            num_scalar_prefetch=1,
            grid=(4,),
            in_specs=[act_spec, act_spec, dz2_spec, dz2_spec],
            out_specs=split_specs(512, D),
        ),
        compiler_params=params(60),
        cost_estimate=takes(11),
        name="down_grad",
    )(scal, *acts, *dz2s)


OUT_WIDTH = 1024 + 128
UP_WIDTH = 4096 + 1024 + 128


def up_parts(y1_a, y1_b, du_a, du_b):
    return [
        contract(y1_a[...], du_a[q], 0, 0) + contract(y1_b[...], du_b[q], 0, 0) for q in range(4)
    ]


def up_grad_other_kernel(scal, y1_a, y1_b, du_a, du_b, out, left):
    @pl.when(pl.program_id(0) == 0)
    def _():
        for side, y1 in enumerate((y1_a, y1_b)):
            for n in range(4):
                row = 2 * (scal[CHIP] ^ n) + 1 - scal[CORE]
                left[side, :, 128 * n : 128 * (n + 1)] = y1[:, aligned(row * 128, 128)]

    rows = contract(left[0], du_a[0], 0, 0) + contract(left[1], du_b[0], 0, 0)
    for n in range(4):
        out[n] = rows[128 * n : 128 * (n + 1)].astype(BF)


def out_grad_other_kernel(scal, heads, dao, small, out):
    parts = [contract(heads[0], dao[...], 0, 0), small[0]]
    out[0] = jnp.concatenate(parts, 1).astype(BF)


def up_grad_own_kernel(scal, y1_a, y1_b, du_a, du_b, heads, dao, small, came, came_out, *rest):
    outs, block = rest[:4], rest[4]
    core = scal[CORE]
    own = jnp.concatenate(up_parts(y1_a, y1_b, du_a, du_b), 1).astype(BF)
    block[:, aligned(core * 2048, 2048)] = own
    block[:, aligned((1 - core) * 2048, 2048)] = came[0]
    out_rows = contract(heads[0], dao[...], 0, 0) + came_out[0, :, :1024].astype(F32)
    block[:, 4096:5120] = out_rows.astype(BF)
    block[:, 5120:] = (small[0] + came_out[0, :, 1024:].astype(F32)).astype(BF)
    split_write(pl.program_id(0), block, *outs)


def of_row(index, flip):
    return lambda n, s: index(s[CHIP] ^ n, s[CORE] ^ flip, s)


def up_specs(flip):
    y1_spec = pl.BlockSpec((ROWS, 128), of_row(lambda q, c, s: (0, 2 * q + c), flip))
    du_spec = pl.BlockSpec((4, ROWS, 512), lambda n, s: (0, 0, 0))
    return [y1_spec, y1_spec, du_spec, du_spec]


def out_specs(flip):
    return [
        pl.BlockSpec((1, ROWS, 128), of_row(lambda q, c, s: (q ^ s[LOW], 0, c), flip)),
        pl.BlockSpec((ROWS, D), lambda n, s: (0, 0)),
        pl.BlockSpec((1, 128, 128), of_row(lambda q, c, s: (2 * q + c, 0, 0), flip)),
    ]


UP_SENT = pl.BlockSpec((1, 128, 2048), lambda n, s: (n, 0, 0))
OUT_SENT = pl.BlockSpec((1, 128, OUT_WIDTH), lambda n, s: (n, 0, 0))


def up_grad_other(scal, y1s, dus):
    y1_spec = pl.BlockSpec((ROWS, D), lambda q, s: (0, 0))
    du_spec = pl.BlockSpec((1, ROWS, 512), lambda q, s: (q, 0, 0))
    return pl.pallas_call(
        up_grad_other_kernel,
        out_shape=struct((4, 128, 2048), BF),
        grid_spec=pltpu.PrefetchScalarGridSpec(
            num_scalar_prefetch=1,
            grid=(4,),
            in_specs=[y1_spec, y1_spec, du_spec, du_spec],
            out_specs=pl.BlockSpec((4, 128, 512), lambda q, s: (0, 0, q)),
            scratch_shapes=[pltpu.VMEM((2, ROWS, 512), BF)],
        ),
        compiler_params=params(60),
        cost_estimate=takes(6),
        name="up_grad_other",
    )(scal, *y1s, *dus)


def out_grad_other(scal, heads, dao, small):
    return pl.pallas_call(
        out_grad_other_kernel,
        out_shape=struct((4, 128, OUT_WIDTH), BF),
        grid_spec=pltpu.PrefetchScalarGridSpec(
            num_scalar_prefetch=1, grid=(4,), in_specs=out_specs(1), out_specs=OUT_SENT
        ),
        compiler_params=params(60),
        cost_estimate=takes(3),
        name="out_grad_other",
    )(scal, heads, dao, small)


def up_grad_own(scal, y1s, dus, heads, dao, small, came, came_out):
    return pl.pallas_call(
        up_grad_own_kernel,
        out_shape=split_shapes(128, UP_WIDTH),
        grid_spec=pltpu.PrefetchScalarGridSpec(
            num_scalar_prefetch=1,
            grid=(4,),
            in_specs=up_specs(0) + out_specs(0) + [UP_SENT, OUT_SENT],
            out_specs=split_specs(128, UP_WIDTH),
            scratch_shapes=[pltpu.VMEM((128, UP_WIDTH), BF)],
        ),
        compiler_params=params(60),
        cost_estimate=takes(10),
        name="up_grad_own",
    )(scal, *y1s, *dus, heads, dao, small, came, came_out)


def qkv_grad_kernel(scal, x, dqkv, out, acc, sums, *, half):
    n = pl.program_id(0)
    ones = jnp.ones((dqkv.shape[0], 128), BF)
    rows = contract(x[...], dqkv[...], 0, 0)
    q_sum = contract(dqkv[:, 0:128], ones, 0, 0)
    v_sum = contract(dqkv[:, 256:384], ones, 0, 0)

    @pl.when(n == 0)
    def _():
        acc[...] = rows
        sums[0] = q_sum
        sums[1] = v_sum

    @pl.when(n > 0)
    def _():
        acc[...] += rows
        sums[0] += q_sum
        sums[1] += v_sum

    @pl.when(n == 3)
    def _():
        lane = lax.broadcasted_iota(jnp.int32, (128, 128), 1)
        extra = jnp.where(lane == 0, sums[0], jnp.where(lane == 1, sums[1], 0.0))
        for r in range(8):
            here = jnp.where(2 * scal[LOW] + half == r, 1.0, 0.0)
            block = jnp.concatenate(
                [acc[128 * r : 128 * (r + 1), :], extra * here], 1
            ).astype(BF)
            for f in range(4):
                out[r // 4, f, r % 4] = block[32 * f : 32 * (f + 1), :]


def qkv_grad(scal, x_all, dqkv, half, cost):
    total = x_all.shape[0]
    part = total // 4
    return pl.pallas_call(
        partial(qkv_grad_kernel, half=half),
        out_shape=struct((2, 4, 4, 32, 512), BF),
        grid_spec=pltpu.PrefetchScalarGridSpec(
            num_scalar_prefetch=1,
            grid=(4,),
            in_specs=[
                pl.BlockSpec((part, D), lambda n, s: (n, 0)),
                pl.BlockSpec((part, 384), lambda n, s: (n, 0)),
            ],
            out_specs=pl.BlockSpec((2, 4, 4, 32, 512), lambda n, s: (0, 0, 0, 0, 0)),
            scratch_shapes=[pltpu.VMEM((D, 384), F32), pltpu.VMEM((2, 128, 128), F32)],
        ),
        compiler_params=params(60),
        cost_estimate=takes(cost),
        name="qkv_grad",
    )(scal, x_all, dqkv)


def input_grad_kernel(scal, dqkv_a, dqkv_b, weight, dao, away, near):
    n = pl.program_id(0)
    held = (n + 4) % 8
    joined = jnp.concatenate(
        [dqkv[:, 128 * k : 128 * (k + 1)] for k in range(3) for dqkv in (dqkv_a, dqkv_b)], 1
    )
    total = contract(joined, weight[...], 1, 1)
    turn = (held // 4) + 2 * ((held // 2) % 2) + 4 * (held % 2)
    parts = []
    for e in range(2):
        place = scal[INVERSE + 2 * (scal[ME] ^ turn) + e]
        other = (place // 2) ^ scal[ME]
        mine = jnp.where((other == 0) | (other == 4), 1.0, 0.0)
        source = aligned(((other // 4) % 2) * 256 + (place % 2) * BLK, BLK)
        rows = total[BLK * e : BLK * (e + 1)]
        parts.append((rows + dao[source, :].astype(F32) * mine).astype(BF))
    result = jnp.concatenate(parts, 0)

    @pl.when(n < 4)
    def _():
        away[0] = result

    @pl.when(n >= 4)
    def _():
        near[0] = result


def input_grad(scal, dqkv_a, dqkv_b, weight, dao):
    rows = pl.BlockSpec((256, 384), lambda n, s: ((n + 4) % 8, 0))
    return pl.pallas_call(
        input_grad_kernel,
        out_shape=(struct((4, 256, D), BF),) * 2,
        grid_spec=pltpu.PrefetchScalarGridSpec(
            num_scalar_prefetch=1,
            grid=(8,),
            in_specs=[
                rows,
                rows,
                pl.BlockSpec((D, 768), lambda n, s: (0, 0)),
                pl.BlockSpec((ROWS, D), lambda n, s: (0, 0)),
            ],
            out_specs=(
                pl.BlockSpec((1, 256, D), lambda n, s: (jnp.minimum(n, 3), 0, 0)),
                pl.BlockSpec((1, 256, D), lambda n, s: (jnp.maximum(n - 4, 0), 0, 0)),
            ),
        ),
        compiler_params=params(60),
        cost_estimate=takes(7),
        name="input_grad",
    )(scal, dqkv_a, dqkv_b, weight, dao)


def after(value, *others):
    return lax.optimization_barrier((value,) + others)[0]


def tied(*values):
    return lax.optimization_barrier(values)


def add_low(a, b):
    return (a.astype(F32) + b.astype(F32)).astype(BF)


def add_far(a_keep, b_keep, a_came, b_came):
    return hop(add_low(a_keep[1], a_came[1]), 4), hop(add_low(b_keep[1], b_came[1]), 2)


def own_rows_of(a_keep, b_keep, a_came, b_came, a_next, b_next):
    a_all = a_keep[0].astype(F32) + a_came[0].astype(F32) + a_next.astype(F32)
    b_all = b_keep[0].astype(F32) + b_came[0].astype(F32) + b_next.astype(F32)
    both = jnp.concatenate([a_all, b_all], 0).astype(BF)
    return lax.psum_scatter(both, "fsdp", scatter_dimension=0, tiled=True)


def tiled_device(
    tokens, cotangent, lengths, order, w_qkv, w_out, w_up, w_down, q_bias, v_bias, out_bias,
    norm1_gain, norm1_bias, up_bias, down_bias, norm2_gain, norm2_bias,
):
    me = lax.axis_index("ctx")
    core, low, top = me % 2, me % 4, me // 4
    chunk = tokens.shape[2]
    half_groups = [[0, 1, 2, 3], [4, 5, 6, 7]]
    scal = scalars(order, lengths)
    small = jnp.zeros((16, 256), BF)
    row = lax.broadcasted_iota(jnp.int32, (16, 256), 0)
    rows_of_small = [
        q_bias, v_bias, out_bias, norm1_gain, norm1_bias, down_bias, norm2_gain, norm2_bias,
    ] + [up_bias[256 * k : 256 * (k + 1)] for k in range(4)]
    for k, vector in enumerate(rows_of_small):
        small = jnp.where(row == k, vector[None, :], small)
    own_rows, other_rows, cot_own, cot_other, pack, pack_sent, up_slice, down_slice = carve(
        tokens, cotangent, w_qkv, w_out, w_up, w_down, small
    )

    def around(value):
        return [
            lax.ppermute(value, "fsdp", [(i, (i + k) % 4) for i in range(4)]) for k in (1, 2, 3)
        ]

    *pack_near, from_y = tied(*around(pack_sent), hop(other_rows, 4))
    pack_near = jnp.stack(pack_near)
    from_x, pack_away = tied(hop(jnp.stack([own_rows, from_y]), 2), hop(pack_near, 4))
    up_own = lax.all_gather(after(up_slice, from_y), "fsdp", axis=0)
    core_own = hop(own_rows, 1)
    core_rest = hop(jnp.concatenate([from_y[None], from_x], 0), 1)
    down_own = lax.all_gather(after(down_slice, from_x), "fsdp", axis=0)
    qkv, x_all, qkv_weight, vecs, up_b = project(
        scal, pack, small, pack_near, pack_away,
        (own_rows, from_y, from_x, core_own, core_rest),
    )
    up_own, qkv = tied(up_own, qkv)
    foreign = jnp.stack(
        [lax.dynamic_index_in_dim(up_own, scal[SHARD + k], 0, False) for k in (1, 2, 3)]
    )
    up_x, up_y = hop(foreign, 2), hop(foreign, 4)
    *sent, turned, lse = attention_forward(scal, after(qkv, foreign), chunk)
    up_x, up_y, *sent = tied(up_x, up_y, *sent)
    far_a, far_b, *far_heads = tied(
        hop(up_y[:, :128], 2), hop(up_x[:, 128:], 4), hop(sent[2], 2), hop(sent[3], 3)
    )
    heads = [sent[0], hop(sent[1], 1), *far_heads]
    ups = (foreign, up_x, up_y, far_a, far_b)
    near = jnp.stack(
        [piece[:, :, 512:] for piece in (foreign, up_x, up_y)]
        + [jnp.concatenate([far_a[:, :, 512:], far_b[:, :, 512:]], 1)]
    )
    away = hop(near, 1)
    down_own = after(down_own, far_a, far_b)
    down_y, down_x = hop(down_own[:, 0], 4), hop(down_own[:, 1], 2)

    y1, y1_low, n1, r1 = attention_out(scal, heads, vecs, x_all, w_out, near, away)

    y1_away = hop(y1_low, 1)
    act, slope = feed_up(scal, y1_low, up_b, w_up, ups)
    act, slope, y1_away = tied(act, slope, y1_away)
    act_away, slope_away = feed_up(scal, y1_away, up_b, w_up, ups)
    act_away, slope_away, down_x, down_y = tied(act_away, slope_away, down_x, down_y)
    downs = (down_own, down_y, down_x)
    part_away = hop(feed_down(scal, act_away, downs, BF), 1)
    cot_came = hop(after(cot_other, act_away), 4)
    part = feed_down(scal, act, downs, F32)
    part, part_away, cot_came = tied(part, part_away, cot_came)
    out_own, out_away, dh2, dz2, sums2 = second_norm(y1, part, part_away, cot_own, cot_came, vecs)
    dz2_away = hop(dz2, 1)
    mixed_came = hop(out_away, 4)
    mixed = jnp.where(
        top == 0, jnp.stack([out_own, mixed_came]), jnp.stack([mixed_came, out_own])
    )[:, None]

    dak, das, dbk, dbs = down_grad(scal, (act, act_away), (dz2, dz2_away))
    da_came, db_came = hop(das, 2), hop(dbs, 4)
    du, du_away, part, part_away, up_sums = feed_back(
        scal, (dz2, after(dz2_away, dak)), (slope, slope_away), w_up, ups, downs
    )
    part, du, du_away, up_sums, part_away, da_came, db_came = tied(
        part, du, du_away, up_sums, part_away, da_came, db_came
    )
    part_away = hop(part_away, 1)
    y1s, dus = (y1_low, y1_away), (du, du_away)
    up_other = up_grad_other(scal, y1s, dus)
    up_other, part_away = tied(up_other, part_away)
    dao, *dattn, sums1 = first_norm(
        scal, dh2, part, part_away, n1, r1, vecs, w_out, near, away
    )
    dattn = [dattn[0]] + [hop(dattn[k], k) for k in (1, 2, 3)]
    up_came = hop(up_other, 1)

    def per_owner(vector):
        return vector.reshape(8, 4, 32)

    unit_sums = up_sums[:4].reshape(4, 4, 128).transpose(1, 0, 2)
    mine = (jnp.arange(2) == core)[None, :, None, None]
    up_owner = jnp.where(mine, unit_sums[:, None], 0.0).reshape(8, 4, 128)
    vec_block = jnp.concatenate(
        [per_owner(sums1[2]), per_owner(sums1[0]), per_owner(sums1[1]), per_owner(sums2[2]),
         per_owner(sums2[0]), per_owner(sums2[1]), up_owner, jnp.zeros((8, 4, 64), F32)], 2
    ).reshape(8, 4, 3, 128)
    vec_block = jnp.concatenate([vec_block, jnp.zeros((8, 4, 29, 128), F32)], 2).reshape(
        8, 128, 128
    )
    all_heads = jnp.stack(heads)
    out_other = out_grad_other(scal, all_heads, dao, vec_block)
    uak, uas, ubk, ubs = up_grad_own(
        scal, y1s, dus, all_heads, dao, vec_block, up_came, hop(out_other, 1)
    )
    uak, uas, ubk, ubs, *dattn = tied(uak, uas, ubk, ubs, *dattn)
    ua_came, ub_came = hop(uas, 2), hop(ubs, 4)
    da_next, db_next = add_far(dak, dbk, da_came, db_came)
    dqkv_a = attention_backward(
        scal, after(qkv, uak), dattn, turned, lse, chunk, 0, 2
    )
    da_next, db_next, dqkv_a = tied(da_next, db_next, dqkv_a)
    down_rows = own_rows_of(dak, dbk, da_came, db_came, da_next, db_next)
    grad_a = qkv_grad(scal, x_all, dqkv_a, 0, 0.05)
    ua_came, ub_came, grad_a = tied(ua_came, ub_came, grad_a)
    ua_next, ub_next = add_far(uak, ubk, ua_came, ub_came)

    def to_owners(grad):
        groups = [[4 * ctx + f for ctx in (k, k + 4) for f in range(4)] for k in range(4)]
        return lax.all_to_all(
            grad.reshape(8, 4, 32, 512), ("ctx", "fsdp"), 0, 0, tiled=True,
            axis_index_groups=groups,
        )

    grad_a = to_owners(grad_a)
    dqkv_b = attention_backward(
        scal, after(qkv, dqkv_a, ua_came), dattn, turned, lse, chunk, 2, 2
    )
    ua_next, ub_next, grad_a, dqkv_b = tied(ua_next, ub_next, grad_a, dqkv_b)
    up_rows = own_rows_of(uak, ubk, ua_came, ub_came, ua_next, ub_next).astype(F32)

    dx_away, dx = input_grad(scal, dqkv_a, dqkv_b, qkv_weight, dao)
    grad_b = qkv_grad(scal, x_all, after(dqkv_b, dx_away), 1, 6)
    grad_b, dx_came = tied(grad_b, hop(dx_away, 1))
    dx = add_low(dx, dx_came)
    far_rows, own_rows = hop(dx[3], 2), hop(dx[2], 2)
    grad_b = to_owners(grad_b)
    grad_far = add_low(dx[1], far_rows)
    grad_came = hop(grad_far, 4)
    grad_b = after(grad_b, grad_far)
    grad_own = add_low(dx[0], after(own_rows, grad_far))
    tokens_grad = jnp.where(
        top == 0, jnp.stack([grad_own, grad_came]), jnp.stack([grad_came, grad_own])
    )[:, None]
    mine = [jnp.sum(parts.astype(F32), 0).astype(BF) for parts in (grad_a, grad_b)]
    mine = lax.all_to_all(
        jnp.concatenate(mine, 2), "ctx", 0, 0, tiled=True, axis_index_groups=half_groups
    ).astype(F32)
    mine = mine.reshape(4, 32, 2, 4, 128)
    w_qkv_grad = mine[:, :, :, :3].transpose(1, 3, 0, 2, 4).reshape(32, 3072)
    q_bias_grad = jnp.sum(mine[:, :, :, 3, 0], (0, 2))
    v_bias_grad = jnp.sum(mine[:, :, :, 3, 1], (0, 2))

    w_up_grad = (
        up_rows[:, :4096].reshape(32, 8, 4, 128).transpose(0, 2, 1, 3).reshape(32, 4096)
    )
    w_out_grad = up_rows[:, 4096:5120]
    sums = up_rows[:3, 5120:].reshape(384)
    return (
        mixed, tokens_grad, w_qkv_grad, w_out_grad, w_up_grad, down_rows.astype(F32), q_bias_grad, v_bias_grad,
        sums[0:32], sums[32:64], sums[64:96], sums[192:320], sums[96:128], sums[128:160],
        sums[160:192],
    )


def pick_blocks(wanted, rows):
    shaped = rows.reshape(-1, BLK, rows.shape[-1])
    picked = [
        lax.dynamic_index_in_dim(shaped, wanted[e], 0, False) for e in range(wanted.shape[0])
    ]
    return jnp.concatenate(picked, 0)


def plain_device(
    tokens, cotangent, lengths, order, w_qkv, w_out, w_up, w_down, q_bias, v_bias, out_bias,
    norm1_gain, norm1_bias, up_bias, down_bias, norm2_gain, norm2_bias,
):
    shards = (
        w_qkv, w_out, w_up, w_down, q_bias, v_bias, out_bias, norm1_gain, norm1_bias, up_bias,
        down_bias, norm2_gain, norm2_bias,
    )
    me = lax.axis_index("ctx")
    count = lax.axis_size("ctx")
    rows = tokens.shape[2]
    per_device = rows // BLK
    whole_rows = rows * count
    scaling = 1.0 / math.sqrt(HD)
    (
        qkv_full, out_full, up_full, down_full, qbias_full, vbias_full, obias_full, gain_one,
        shift_one, ubias_full, dbias_full, gain_two, shift_two,
    ) = tuple(lax.all_gather(shard, "fsdp", axis=0, tiled=True) for shard in shards)
    full_bias = jnp.concatenate([qbias_full, jnp.zeros_like(qbias_full), vbias_full]).astype(F32)
    gain_one, shift_one, gain_two, shift_two = (
        vector.astype(F32) for vector in (gain_one, shift_one, gain_two, shift_two)
    )
    positions = jnp.arange(whole_rows, dtype=jnp.int32)
    mixed_list, grad_list, totals = [], [], None
    for micro in range(tokens.shape[0]):
        order_row = order[micro, 0]
        bound = lengths[micro, 0, 0]
        segment_all = (positions >= bound).astype(jnp.int32)
        segment_query = (me * rows + jnp.arange(rows, dtype=jnp.int32) >= bound).astype(jnp.int32)
        dealt = me * per_device + jnp.arange(per_device, dtype=jnp.int32)
        blocks = jnp.arange(order_row.shape[0], dtype=jnp.int32)
        inverse = jnp.sum(jnp.where(order_row[None, :] == dealt[:, None], blocks[None, :], 0), 1)
        forward = jnp.sum(jnp.where(blocks[None, :] == dealt[:, None], order_row[None, :], 0), 1)
        token_rows = tokens[micro, 0]
        cot_rows = pick_blocks(
            inverse, lax.all_gather(cotangent[micro, 0], "ctx", axis=0, tiled=True)
        ).astype(F32)
        qkv_rows = (jnp.dot(token_rows, qkv_full, preferred_element_type=F32) + full_bias).astype(BF)
        queries = qkv_rows[:, :D].reshape(rows, H, HD)
        keys_values = lax.all_gather(qkv_rows[:, D:], "ctx", axis=0, tiled=True)
        keys = keys_values[:, :D].reshape(whole_rows, H, HD)
        values = keys_values[:, D:].reshape(whole_rows, H, HD)
        allowed = (segment_query[:, None] == segment_all[None, :])[None]
        scores = jnp.einsum("rhd,khd->hrk", queries, keys, preferred_element_type=F32) * scaling
        scores = jnp.where(allowed, scores, NEGATIVE)
        expos = jnp.where(allowed, jnp.exp(scores - jnp.max(scores, -1, keepdims=True)), 0.0)
        probs = expos / jnp.sum(expos, -1, keepdims=True)
        probs_low = probs.astype(BF)
        attn_float = jnp.einsum("hrk,khd->rhd", probs_low, values, preferred_element_type=F32)
        attn_low = attn_float.reshape(rows, D).astype(BF)
        first_in = (
            token_rows.astype(F32)
            + jnp.dot(attn_low, out_full, preferred_element_type=F32)
            + obias_full.astype(F32)
        )
        first_out, normed_one, inverse_one = norm_forward(first_in, gain_one, shift_one)
        first_low = first_out.astype(BF)
        hidden_in = jnp.dot(first_low, up_full, preferred_element_type=F32) + ubias_full.astype(F32)
        activated, gelu_back = jax.vjp(partial(jax.nn.gelu, approximate=False), hidden_in)
        act_low = activated.astype(BF)
        second_in = (
            first_out
            + jnp.dot(act_low, down_full, preferred_element_type=F32)
            + dbias_full.astype(F32)
        )
        second_out, normed_two, inverse_two = norm_forward(second_in, gain_two, shift_two)
        out_all = lax.all_gather(second_out.astype(BF), "ctx", axis=0, tiled=True)
        mixed_list.append(pick_blocks(forward, out_all))

        grad_second = norm_backward(cot_rows, normed_two, inverse_two, gain_two)
        grad_down_low = grad_second.astype(BF)
        (grad_hidden,) = gelu_back(contract(grad_down_low, down_full, 1, 1))
        grad_hidden_low = grad_hidden.astype(BF)
        grad_first = grad_second + contract(grad_hidden_low, up_full, 1, 1)
        grad_first_in = norm_backward(grad_first, normed_one, inverse_one, gain_one)
        grad_branch = grad_first_in.astype(BF)
        grad_attn = contract(grad_branch, out_full, 1, 1).astype(BF).reshape(rows, H, HD)
        grad_probs = jnp.einsum("rhd,khd->hrk", grad_attn, values, preferred_element_type=F32)
        delta = jnp.sum(probs * grad_probs, -1, keepdims=True)
        grad_scores = (probs * (grad_probs - delta) * scaling).astype(BF)
        grad_query = jnp.einsum("hrk,khd->rhd", grad_scores, keys, preferred_element_type=F32)
        grad_keys = jnp.einsum("hrk,rhd->khd", grad_scores, queries, preferred_element_type=F32)
        grad_values = jnp.einsum("hrk,rhd->khd", probs_low, grad_attn, preferred_element_type=F32)
        both = jnp.concatenate(
            [grad_keys.reshape(whole_rows, D), grad_values.reshape(whole_rows, D)], 1
        )
        both = lax.psum_scatter(both, "ctx", scatter_dimension=0, tiled=True)
        grad_qkv = jnp.concatenate([grad_query.reshape(rows, D), both], 1).astype(BF)
        column_sums = jnp.sum(grad_qkv.astype(F32), 0)
        grad_list.append((grad_first_in + contract(grad_qkv, qkv_full, 1, 1)).astype(BF))
        parts = (
            contract(token_rows, grad_qkv, 0, 0),
            contract(attn_low, grad_branch, 0, 0),
            contract(first_low, grad_hidden_low, 0, 0),
            contract(act_low, grad_down_low, 0, 0),
            column_sums[:D],
            column_sums[2 * D :],
            jnp.sum(grad_branch.astype(F32), 0),
            jnp.sum(grad_first * normed_one, 0),
            jnp.sum(grad_first, 0),
            jnp.sum(grad_hidden_low.astype(F32), 0),
            jnp.sum(grad_down_low.astype(F32), 0),
            jnp.sum(cot_rows * normed_two, 0),
            jnp.sum(cot_rows, 0),
        )
        totals = parts if totals is None else tuple(a + b for a, b in zip(totals, parts))
    shares = tuple(
        lax.psum_scatter(part, ("ctx", "fsdp"), scatter_dimension=0, tiled=True) for part in totals
    )
    return (jnp.stack(mixed_list)[:, None], jnp.stack(grad_list)[:, None]) + shares


def solution(mesh):
    fits = mesh.shape["ctx"] == 8 and mesh.shape["fsdp"] == 4
    weights = (P("fsdp", None),) * 4 + (P("fsdp"),) * 9
    owners = (P(("ctx", "fsdp"), None),) * 4 + (P(("ctx", "fsdp")),) * 9
    rows = P(None, "fsdp", "ctx", None)
    return jax.shard_map(
        tiled_device if fits else plain_device,
        mesh=mesh,
        in_specs=(rows, rows, P(None, "fsdp", None), P(None, "fsdp", None)) + weights,
        out_specs=(rows, rows) + owners,
        check_vma=False,
    )
```

time: 549 us -> 471 us (0.86)
  the two profiles are of different devices: /device:TPU:8 before, /device:TPU:0 now
where the time goes in v2:
time: 471 us; the launch traced here: 462 us
  Pallas kernels  208 us (44%)
  waiting for transfers between devices  115 us (24%)
  starting transfers between devices  64.3 us (14%)
  other arithmetic  38.2 us (8%)
  local copies, waits for them, and re-layouts  20.8 us (4%)
  between operations  16 us (3%)
    ppermute x38, waiting for transfers between devices, hop(): return lax.ppermute(value, 'ctx', [(i, i ^ mask) for i in range(count)])  86.5 us
    ppermute x38, starting transfers between devices, hop(): return lax.ppermute(value, 'ctx', [(i, i ^ mask) for i in range(count)])  42.8 us
    pallas_call x2, Pallas kernels, attention_backward(): pl.pallas_call(partial(attention_backward_kernel, first=first, heads=head...  42.1 us
    pallas_call x1, Pallas kernels, attention_forward(): pl.pallas_call(partial(attention_forward_kernel, heads=heads, chunk=chunk...  22 us
    pallas_call x1, Pallas kernels, feed_back(): pl.pallas_call(back_kernel, out_shape=(du, du, struct((ROWS, D), F32), st...  17.8 us
    pallas_call x2, Pallas kernels, feed_up(): pl.pallas_call(up_kernel, out_shape=(struct((4, ROWS, 512), BF), struct((...  16.2 us
    pallas_call x2, Pallas kernels, qkv_grad(): pl.pallas_call(partial(qkv_grad_kernel, half=half), out_shape=struct((2,...  14.8 us
    all_to_all x2, waiting for transfers between devices, to_owners(): lax.all_to_all(grad.reshape(8, 4, 32, 512), ('ctx', 'fsdp'), 0, 0, tiled=...  14.7 us
  transfers between devices with their start and end apart: 48, of which 23 were waited for; matrix products, arithmetic and copies ran while one was open for 10% of the time, Pallas kernels for 37%

profile of v2, /device:TPU:0, one launch (start us, length us, event | category | flops | bytes accessed | tf_op | source)
XLA Modules:
  0.0 462.3 jit_solution(8089801122763963787)
XLA Ops:
  9.6 4.6 carve.1
  22.8 5.0 %collective-permute-done = bf16[144,768]{1,0:T(8,128)(2,1)S(1)} collective-permute-done((bf16[144,768]{1,0:T(8,128)(2,1)}, bf16[144,768]{1,0:T(8,128)(2,1)S(1)}, u32[]{:S(2)}, u32[]{:S(2)}) %collective-permute-start) | collective-permute-done | bytes 221216 | tf_op jit(solution)/shard_map/ppermute | solution.py:1098
  27.7 8.1 %collective-permute-done.1 = bf16[144,768]{1,0:T(8,128)(2,1)S(1)} collective-permute-done((bf16[144,768]{1,0:T(8,128)(2,1)}, bf16[144,768]{1,0:T(8,128)(2,1)S(1)}, u32[]{:S(2)}, u32[]{:S(2)}) %collective-permute-start.1) | collective-permute-done | bytes 221216 | tf_op jit(solution)/shard_map/ppermute | solution.py:1098
  40.2 16.2 %collective-permute-done.5.away = bf16[3,144,768]{2,1,0:T(8,128)(2,1)} collective-permute-done((bf16[3,144,768]{2,1,0:T(8,128)(2,1)}, bf16[3,144,768]{2,1,0:T(8,128)(2,1)}, u32[]{:S(2)}, u32[]{:S(2)}) %collective-permute-start.5) | collective-permute-done | bytes 663584 | tf_op jit(solution)/shard_map/ppermute | solution.py:45
  56.4 5.8 %collective-permute-done.4.x = bf16[2,256,1024]{2,1,0:T(8,128)(2,1)S(1)} collective-permute-done((bf16[2,256,1024]{2,1,0:T(8,128)(2,1)S(1)}, bf16[2,256,1024]{2,1,0:T(8,128)(2,1)S(1)}, u32[]{:S(2)}, u32[]{:S(2)}) %collective-permute-start.4) | collective-permute-done | bytes 1048608 | tf_op jit(solution)/shard_map/ppermute | solution.py:45
  66.7 10.3 %project.1 = (bf16[2048,768]{1,0:T(8,128)(2,1)}, bf16[2048,1024]{1,0:T(8,128)(2,1)}, bf16[1024,768]{1,0:T(8,128)(2,1)}, f32[8,1024]{1,0:T(8,128)}, f32[8,512]{1,0:T(8,128)}) custom-call(s32[42]{0:T(128)} %concatenate.54.scal, bf16[256,768]{1,0:T(8,128)(2,1)} %get-tuple-element.141.pack, bf16[16,256]{1,0:T(8,128)(2,1)} %select_select_fusion.small, ...), custom_call_target="tpu_custom_call" | custom-call | flops 9200000000 | bytes 1048576 | tf_op jit(solution)/shard_map/project/pallas_call | solution.py:424
  80.5 22.0 %attention_forward.1 = (bf16[512,256]{1,0:T(8,128)(2,1)}, bf16[512,256]{1,0:T(8,128)(2,1)}, bf16[512,256]{1,0:T(8,128)(2,1)}, bf16[512,256]{1,0:T(8,128)(2,1)}, f32[256,2048]{1,0:T(8,128)}, /*index=5*/f32[4,2048]{1,0:T(4,128)}) custom-call(s32[42]{0:T(128)} %concatenate.54.scal, bf16[2048,768]{1,0:T(8,128)(2,1)} %get-tuple-element.242.qkv), custom_call_target="tpu_custom_call" | custom-call | flops 26449999872 | bytes 1048576 | tf_op jit(solution)/shard_map/attention_forward/pallas_call | solution.py:211
  109.7 13.8 %collective-permute-done.13.h2 = bf16[512,256]{1,0:T(8,128)(2,1)S(1)} collective-permute-done((bf16[512,256]{1,0:T(8,128)(2,1)S(1)}, bf16[512,256]{1,0:T(8,128)(2,1)S(1)}, u32[]{:S(2)}, u32[]{:S(2)}) %collective-permute-start.13) | collective-permute-done | bytes 262176 | tf_op jit(solution)/shard_map/ppermute | solution.py:45
  131.6 9.2 %attention_out.1 = (f32[512,1024]{1,0:T(8,128)}, bf16[512,1024]{1,0:T(8,128)(2,1)}, f32[512,1024]{1,0:T(8,128)}, f32[512,128]{1,0:T(8,128)}) custom-call(s32[42]{0:T(128)} %concatenate.54.scal, bf16[512,256]{1,0:T(8,128)(2,1)} %get-tuple-element.156.h0, bf16[512,256]{1,0:T(8,128)(2,1)} %copy-done.19, bf16[512,256]{1,0:T(8,128)(2,1)} %copy-done.15, ...), custom_call_target="tpu_custom_call" | custom-call | flops 10350000128 | bytes 1048576 | tf_op jit(solution)/shard_map/attention_out/pallas_call | solution.py:492
  147.0 8.1 %feed_up.2 = (bf16[4,512,512]{2,1,0:T(8,128)(2,1)}, bf16[4,512,512]{2,1,0:T(8,128)(2,1)}) custom-call(s32[42]{0:T(128)} %concatenate.54.scal, bf16[512,1024]{1,0:T(8,128)(2,1)} %get-tuple-element.169.y1_low.y1_a, f32[8,512]{1,0:T(8,128)} %get-tuple-element.170.up_bias, bf16[256,4096]{1,0:T(8,128)(2,1)} %w_up.7, bf16[3,256,640]{2,1,0:T(8,128)(2,1)} %copy-done.3, ...), custom_call_target="tpu_custom_call" | custom-call | flops 8049999872 | bytes 1048576 | tf_op jit(solution)/shard_map/feed_up/pallas_call | solution.py:586
  155.1 8.1 %feed_up.3 = (bf16[4,512,512]{2,1,0:T(8,128)(2,1)}, bf16[4,512,512]{2,1,0:T(8,128)(2,1)}) custom-call(s32[42]{0:T(128)} %concatenate.54.scal, bf16[512,1024]{1,0:T(8,128)(2,1)} %collective-permute-done.16.y1_low.y1_b, f32[8,512]{1,0:T(8,128)} %get-tuple-element.170.up_bias, bf16[256,4096]{1,0:T(8,128)(2,1)} %w_up.7, bf16[3,256,640]{2,1,0:T(8,128)(2,1)} %copy-done.3, ...), custom_call_target="tpu_custom_call" | custom-call | flops 8049999872 | bytes 1048576 | tf_op jit(solution)/shard_map/feed_up/pallas_call | solution.py:586
  171.2 7.1 %feed_down.3 = bf16[512,1024]{1,0:T(8,128)(2,1)} custom-call(s32[42]{0:T(128)} %concatenate.54.scal, bf16[4,512,512]{2,1,0:T(8,128)(2,1)} %get-tuple-element.182.act.act_b, bf16[4,2,128,1024]{3,2,1,0:T(8,128)(2,1)} %bitcast.97, bf16[4,128,1024]{2,1,0:T(8,128)(2,1)} %copy-done.27, bf16[4,128,1024]{2,1,0:T(8,128)(2,1)} %copy-done.26), custom_call_target="tpu_custom_call" | custom-call | flops 5750000128 | bytes 1048576 | tf_op jit(solution)/shard_map/feed_down/pallas_call | solution.py:623
  180.5 7.0 %feed_down.2.part = f32[512,1024]{1,0:T(8,128)} custom-call(s32[42]{0:T(128)} %concatenate.54.scal, bf16[4,512,512]{2,1,0:T(8,128)(2,1)} %get-tuple-element.173.act.act_a, bf16[4,2,128,1024]{3,2,1,0:T(8,128)(2,1)} %bitcast.98, bf16[4,128,1024]{2,1,0:T(8,128)(2,1)} %copy-done.27, bf16[4,128,1024]{2,1,0:T(8,128)(2,1)} %copy-done.26), custom_call_target="tpu_custom_call" | custom-call | flops 5750000128 | bytes 1048576 | tf_op jit(solution)/shard_map/feed_down/pallas_call | solution.py:623
  187.5 5.5 %collective-permute-done.20.cot_came = bf16[256,1024]{1,0:T(8,128)(2,1)S(1)} collective-permute-done((bf16[256,1024]{1,0:T(8,128)(2,1)S(1)}, bf16[256,1024]{1,0:T(8,128)(2,1)S(1)}, u32[]{:S(2)}, u32[]{:S(2)}) %collective-permute-start.20) | collective-permute-done | bytes 524320 | tf_op jit(solution)/shard_map/ppermute | solution.py:45
  194.2 6.7 %second_norm.1 = (bf16[256,1024]{1,0:T(8,128)(2,1)}, bf16[256,1024]{1,0:T(8,128)(2,1)}, f32[512,1024]{1,0:T(8,128)}, bf16[512,1024]{1,0:T(8,128)(2,1)}, f32[8,1024]{1,0:T(8,128)}) custom-call(f32[512,1024]{1,0:T(8,128)} %get-tuple-element.168.y1, f32[512,1024]{1,0:T(8,128)} %feed_down.2.part, bf16[512,1024]{1,0:T(8,128)(2,1)} %copy-done.30, ...), custom_call_target="tpu_custom_call" | custom-call | flops 4600000000 | bytes 1048576 | tf_op jit(solution)/shard_map/second_norm/pallas_call | solution.py:673
  204.8 9.8 %down_grad.1 = (bf16[2,256,1024]{2,1,0:T(8,128)(2,1)}, bf16[2,256,1024]{2,1,0:T(8,128)(2,1)}, bf16[2,256,1024]{2,1,0:T(8,128)(2,1)}, bf16[2,256,1024]{2,1,0:T(8,128)(2,1)}) custom-call(s32[42]{0:T(128)} %concatenate.54.scal, bf16[4,512,512]{2,1,0:T(8,128)(2,1)} %get-tuple-element.173.act.act_a, bf16[4,512,512]{2,1,0:T(8,128)(2,1)} %get-tuple-element.182.act.act_b, ...), custom_call_target="tpu_custom_call" | custom-call | flops 12650000384 | bytes 1048576 | tf_op jit(solution)/shard_map/down_grad/pallas_call | solution.py:821
  217.6 17.8 %feed_back.1 = (bf16[4,512,512]{2,1,0:T(8,128)(2,1)}, bf16[4,512,512]{2,1,0:T(8,128)(2,1)}, f32[512,1024]{1,0:T(8,128)}, bf16[512,1024]{1,0:T(8,128)(2,1)}, f32[8,512]{1,0:T(8,128)}) custom-call(s32[42]{0:T(128)} %concatenate.54.scal, bf16[512,1024]{1,0:T(8,128)(2,1)} %get-tuple-element.191.dz2_a, bf16[512,1024]{1,0:T(8,128)(2,1)} %copy-done.29, ...), custom_call_target="tpu_custom_call" | custom-call | flops 25300000768 | bytes 1048576 | tf_op jit(solution)/shard_map/feed_back/pallas_call | solution.py:729
  243.5 7.5 %up_grad_other.1 = bf16[4,128,2048]{2,1,0:T(8,128)(2,1)} custom-call(s32[42]{0:T(128)} %concatenate.54.scal, bf16[512,1024]{1,0:T(8,128)(2,1)} %get-tuple-element.169.y1_low.y1_a, bf16[512,1024]{1,0:T(8,128)(2,1)} %collective-permute-done.16.y1_low.y1_b, bf16[4,512,512]{2,1,0:T(8,128)(2,1)} %get-tuple-element.206.du_a, ...), custom_call_target="tpu_custom_call" | custom-call | flops 6899999744 | bytes 1048576 | tf_op jit(solution)/shard_map/up_grad_other/pallas_call | solution.py:901
  252.0 7.1 %first_norm.1 = (bf16[512,1024]{1,0:T(8,128)(2,1)}, bf16[512,256]{1,0:T(8,128)(2,1)}, bf16[512,256]{1,0:T(8,128)(2,1)}, bf16[512,256]{1,0:T(8,128)(2,1)}, bf16[512,256]{1,0:T(8,128)(2,1)}, /*index=5*/f32[8,1024]{1,0:T(8,128)}) custom-call(s32[42]{0:T(128)} %concatenate.54.scal, f32[512,1024]{1,0:T(8,128)} %get-tuple-element.208.dh2, ...), custom_call_target="tpu_custom_call" | custom-call | flops 8049999872 | bytes 1048576 | tf_op jit(solution)/shard_map/first_norm/pallas_call | solution.py:775
  261.3 5.2 %out_grad_other.1 = bf16[4,128,1152]{2,1,0:T(8,128)(2,1)} custom-call(s32[42]{0:T(128)} %concatenate.54.scal, bf16[4,512,256]{2,1,0:T(8,128)(2,1)} %pad_maximum_fusion.3.heads, bf16[512,1024]{1,0:T(8,128)(2,1)} %get-tuple-element.214.dao, f32[8,128,128]{2,1,0:T(8,128)} %bitcast.109), custom_call_target="tpu_custom_call" | custom-call | flops 3449999872 | bytes 1048576 | tf_op jit(solution)/shard_map/out_grad_other/pallas_call | solution.py:918
  273.7 10.3 %up_grad_own.1 = (bf16[2,64,5248]{2,1,0:T(8,128)(2,1)}, bf16[2,64,5248]{2,1,0:T(8,128)(2,1)}, bf16[2,64,5248]{2,1,0:T(8,128)(2,1)}, bf16[2,64,5248]{2,1,0:T(8,128)(2,1)}) custom-call(s32[42]{0:T(128)} %concatenate.54.scal, bf16[512,1024]{1,0:T(8,128)(2,1)} %get-tuple-element.169.y1_low.y1_a, bf16[512,1024]{1,0:T(8,128)(2,1)} %collective-permute-done.16.y1_low.y1_b, ...), custom_call_target="tpu_custom_call" | custom-call | flops 11500000256 | bytes 1048576 | tf_op jit(solution)/shard_map/up_grad_own/pallas_call | solution.py:931
  284.0 4.7 %collective-permute-done.31.grad2 = bf16[512,256]{1,0:T(8,128)(2,1)} collective-permute-done((bf16[512,256]{1,0:T(8,128)(2,1)}, bf16[512,256]{1,0:T(8,128)(2,1)}, u32[]{:S(2)}, u32[]{:S(2)}) %collective-permute-start.31) | collective-permute-done | bytes 262176 | tf_op jit(solution)/shard_map/ppermute | solution.py:45
  295.3 21.0 %attention_backward.2.dqkv.dqkv_a = bf16[2048,384]{1,0:T(8,128)(2,1)} custom-call(s32[42]{0:T(128)} %concatenate.54.scal, bf16[2048,768]{1,0:T(8,128)(2,1)} %get-tuple-element.242.qkv, bf16[512,256]{1,0:T(8,128)(2,1)} %get-tuple-element.229.grad0, bf16[512,256]{1,0:T(8,128)(2,1)} %copy-done.34, bf16[512,256]{1,0:T(8,128)(2,1)} %collective-permute-done.31.grad2, ...), custom_call_target="tpu_custom_call" | custom-call | flops 21849999360 | bytes 1048576 | tf_op jit(solution)/shard_map/attention_backward/pallas_call | solution.py:306
  320.1 7.5 %qkv_grad.2 = bf16[2,4,4,32,512]{4,3,2,1,0:T(8,128)(2,1)} custom-call(s32[42]{0:T(128)} %concatenate.54.scal, bf16[2048,1024]{1,0:T(8,128)(2,1)} %get-tuple-element.165.x_all.x, bf16[2048,384]{1,0:T(8,128)(2,1)} %attention_backward.2.dqkv.dqkv_a), custom_call_target="tpu_custom_call" | custom-call | flops 57500000 | bytes 1048576 | tf_op jit(solution)/shard_map/qkv_grad/pallas_call | solution.py:982
  336.3 8.0 %all-to-all-start = ((bf16[8,4,32,512]{3,2,1,0:T(8,128)(2,1)}), bf16[8,4,32,512]{3,2,1,0:T(8,128)(2,1)S(1)}, u32[]{:S(2)}, u32[]{:S(2)}) async-start(bf16[8,4,32,512]{3,2,1,0:T(8,128)(2,1)} %bitcast.39), calls=%async_computation | async-start | bytes 2097152 | tf_op jit(solution)/shard_map/all_to_all | solution.py:1201
  344.5 21.1 %attention_backward.3.dqkv_b.dqkv = bf16[2048,384]{1,0:T(8,128)(2,1)} custom-call(s32[42]{0:T(128)} %concatenate.54.scal, bf16[2048,768]{1,0:T(8,128)(2,1)} %get-tuple-element.242.qkv, bf16[512,256]{1,0:T(8,128)(2,1)} %get-tuple-element.229.grad0, bf16[512,256]{1,0:T(8,128)(2,1)} %copy-done.34, bf16[512,256]{1,0:T(8,128)(2,1)} %collective-permute-done.31.grad2, ...), custom_call_target="tpu_custom_call" | custom-call | flops 21849999360 | bytes 1048576 | tf_op jit(solution)/shard_map/attention_backward/pallas_call | solution.py:306
  366.5 7.7 %all-to-all-done = bf16[8,4,32,512]{3,2,1,0:T(8,128)(2,1)S(1)} async-done(((bf16[8,4,32,512]{3,2,1,0:T(8,128)(2,1)}), bf16[8,4,32,512]{3,2,1,0:T(8,128)(2,1)S(1)}, u32[]{:S(2)}, u32[]{:S(2)}) %all-to-all-start) | async-done | bytes 1048608 | tf_op jit(solution)/shard_map/all_to_all | solution.py:1201
  375.9 10.6 %input_grad.1 = (bf16[4,256,1024]{2,1,0:T(8,128)(2,1)}, bf16[4,256,1024]{2,1,0:T(8,128)(2,1)}) custom-call(s32[42]{0:T(128)} %concatenate.54.scal, bf16[2048,384]{1,0:T(8,128)(2,1)} %attention_backward.2.dqkv.dqkv_a, bf16[2048,384]{1,0:T(8,128)(2,1)} %attention_backward.3.dqkv_b.dqkv, bf16[1024,768]{1,0:T(8,128)(2,1)} %get-tuple-element.244.weight, ...), custom_call_target="tpu_custom_call" | custom-call | flops 8049999872 | bytes 1048576 | tf_op jit(solution)/shard_map/input_grad/pallas_call | solution.py:1030
  389.9 7.3 %qkv_grad.3 = bf16[2,4,4,32,512]{4,3,2,1,0:T(8,128)(2,1)} custom-call(s32[42]{0:T(128)} %concatenate.54.scal, bf16[2048,1024]{1,0:T(8,128)(2,1)} %get-tuple-element.165.x_all.x, bf16[2048,384]{1,0:T(8,128)(2,1)} %attention_backward.3.dqkv_b.dqkv), custom_call_target="tpu_custom_call" | custom-call | flops 6899999744 | bytes 1048576 | tf_op jit(solution)/shard_map/qkv_grad/pallas_call | solution.py:982
  412.2 8.7 %collective-permute-done.39 = bf16[256,1024]{1,0:T(8,128)(2,1)} collective-permute-done((bf16[256,1024]{1,0:T(8,128)(2,1)}, bf16[256,1024]{1,0:T(8,128)(2,1)}, u32[]{:S(2)}, u32[]{:S(2)}) %collective-permute-start.39) | collective-permute-done | bytes 524320 | tf_op jit(solution)/shard_map/ppermute | solution.py:45
  424.9 6.5 %collective-permute-done.38 = bf16[256,1024]{1,0:T(8,128)(2,1)} collective-permute-done((bf16[256,1024]{1,0:T(8,128)(2,1)}, bf16[256,1024]{1,0:T(8,128)(2,1)}, u32[]{:S(2)}, u32[]{:S(2)}) %collective-permute-start.38) | collective-permute-done | bytes 524320 | tf_op jit(solution)/shard_map/ppermute | solution.py:45
  433.8 7.0 %all-to-all-done.1 = bf16[8,4,32,512]{3,2,1,0:T(8,128)(2,1)} async-done(((bf16[8,4,32,512]{3,2,1,0:T(8,128)(2,1)}), bf16[8,4,32,512]{3,2,1,0:T(8,128)(2,1)}, u32[]{:S(2)}, u32[]{:S(2)}) %all-to-all-start.1) | async-done | bytes 1048608 | tf_op jit(solution)/shard_map/all_to_all | solution.py:1201
  (252 shorter events, 141.0 us)
Async XLA Ops:
  7.2 69.8 %all-gather.5.cloned.1.call-start = ((), (), s32[]{:S(2)}) async-start(), calls=%async_computation.7 | async-start | bytes 1638400 | tf_op jit(solution)/shard_map/all_gather | solution.py:1104
  14.2 21.6 %collective-permute-start.3 = (bf16[256,1024]{1,0:T(8,128)(2,1)}, bf16[256,1024]{1,0:T(8,128)(2,1)S(1)}, u32[]{:S(2)}, u32[]{:S(2)}) collective-permute-start(bf16[256,1024]{1,0:T(8,128)(2,1)} %get-tuple-element.138), channel_id=1, source_target_pairs={{0,16},{4,20},{8,24},{12,28},{16,0},{20,4},{24,8},{28,12},{1,17},{... | collective-permute-start | bytes 1572872 | tf_op jit(solution)/shard_map/ppermute | solution.py:45
  18.8 17.0 %collective-permute-start.1 = (bf16[144,768]{1,0:T(8,128)(2,1)}, bf16[144,768]{1,0:T(8,128)(2,1)S(1)}, u32[]{:S(2)}, u32[]{:S(2)}) collective-permute-start(bf16[144,768]{1,0:T(8,128)(2,1)} %get-tuple-element.137), channel_id=1, source_target_pairs={{0,2},{1,3},{2,0},{3,1},{4,6},{5,7},{6,4},{7,5},{8,10},{9,11},{10,... | collective-permute-start | bytes 663560 | tf_op jit(solution)/shard_map/ppermute | solution.py:1098
  37.1 25.1 %collective-permute-start.4 = (bf16[2,256,1024]{2,1,0:T(8,128)(2,1)S(1)}, bf16[2,256,1024]{2,1,0:T(8,128)(2,1)S(1)}, u32[]{:S(2)}, u32[]{:S(2)}) collective-permute-start(bf16[2,256,1024]{2,1,0:T(8,128)(2,1)S(1)} %pad_maximum_fusion.2), channel_id=1, source_target_pairs={{0,8},{4,12},{8,0},{12,4},{16,24},{20,28},{24,16},{28,20},{1,9},{5... | collective-permute-start | bytes 3145736 | tf_op jit(solution)/shard_map/ppermute | solution.py:45
  39.6 16.8 %collective-permute-start.5 = (bf16[3,144,768]{2,1,0:T(8,128)(2,1)}, bf16[3,144,768]{2,1,0:T(8,128)(2,1)}, u32[]{:S(2)}, u32[]{:S(2)}) collective-permute-start(bf16[3,144,768]{2,1,0:T(8,128)(2,1)} %pad_maximum_fusion.7.near), channel_id=1, source_target_pairs={{0,16},{4,20},{8,24},{12,28},{16,0},{20,4},{24,8},{28,12},{1,17},{... | collective-permute-start | bytes 1990664 | tf_op jit(solution)/shard_map/ppermute | solution.py:45
  40.2 88.2 %all-gather.7.cloned.1.call-start = ((), (), s32[]{:S(2)}) async-start(), calls=%async_computation.8 | async-start | bytes 2621440 | tf_op jit(solution)/shard_map/all_gather | solution.py:1107
  65.9 344.3 %reduce-scatter.5.cloned.1.call-start = ((), (), s32[]{:S(2)}) async-start(), calls=%async_computation.6 | async-start | bytes 1310720 | tf_op jit(solution)/shard_map/reduce_scatter | solution.py:1073
  78.4 24.0 %collective-permute-start.8 = (bf16[3,256,640]{2,1,0:T(8,128)(2,1)S(1)}, bf16[3,256,640]{2,1,0:T(8,128)(2,1)S(1)}, u32[]{:S(2)}, u32[]{:S(2)}) collective-permute-start(bf16[3,256,640]{2,1,0:T(8,128)(2,1)S(1)} %pad_maximum_fusion.5.rest_0_), channel_id=1, source_target_pairs={{0,8},{4,12},{8,0},{12,4},{16,24},{20,28},{24,16},{28,20},{1,9},{5... | collective-permute-start | bytes 2949128 | tf_op jit(solution)/shard_map/ppermute | solution.py:45
  80.0 23.6 %collective-permute-start.9 = (bf16[3,256,640]{2,1,0:T(8,128)(2,1)S(1)}, bf16[3,256,640]{2,1,0:T(8,128)(2,1)S(1)}, u32[]{:S(2)}, u32[]{:S(2)}) collective-permute-start(bf16[3,256,640]{2,1,0:T(8,128)(2,1)S(1)} %pad_maximum_fusion.5.rest_0_), channel_id=1, source_target_pairs={{0,16},{4,20},{8,24},{12,28},{16,0},{20,4},{24,8},{28,12},{1,17},{... | collective-permute-start | bytes 2949128 | tf_op jit(solution)/shard_map/ppermute | solution.py:45
  103.6 21.7 %collective-permute-start.11 = (bf16[3,128,640]{2,1,0:T(8,128)(2,1)S(1)}, bf16[3,128,640]{2,1,0:T(8,128)(2,1)S(1)}, u32[]{:S(2)}, u32[]{:S(2)}) collective-permute-start(bf16[3,128,640]{2,1,0:T(8,128)(2,1)S(1)} %slice.179), channel_id=1, source_target_pairs={{0,8},{4,12},{8,0},{12,4},{16,24},{20,28},{24,16},{28,20},{1,9},{5... | collective-permute-start | bytes 1474568 | tf_op jit(solution)/shard_map/ppermute | solution.py:45
  104.3 21.1 %collective-permute-start.12 = (bf16[3,128,640]{2,1,0:T(8,128)(2,1)S(1)}, bf16[3,128,640]{2,1,0:T(8,128)(2,1)S(1)}, u32[]{:S(2)}, u32[]{:S(2)}) collective-permute-start(bf16[3,128,640]{2,1,0:T(8,128)(2,1)S(1)} %slice.180), channel_id=1, source_target_pairs={{0,16},{4,20},{8,24},{12,28},{16,0},{20,4},{24,8},{28,12},{1,17},{... | collective-permute-start | bytes 1474568 | tf_op jit(solution)/shard_map/ppermute | solution.py:45
  108.0 15.4 %collective-permute-start.13 = (bf16[512,256]{1,0:T(8,128)(2,1)S(1)}, bf16[512,256]{1,0:T(8,128)(2,1)S(1)}, u32[]{:S(2)}, u32[]{:S(2)}) collective-permute-start(bf16[512,256]{1,0:T(8,128)(2,1)S(1)} %copy-done.37), channel_id=1, source_target_pairs={{0,8},{4,12},{8,0},{12,4},{16,24},{20,28},{24,16},{28,20},{1,9},{5... | collective-permute-start | bytes 786440 | tf_op jit(solution)/shard_map/ppermute | solution.py:45
  109.6 15.7 %collective-permute-start.14 = (bf16[512,256]{1,0:T(8,128)(2,1)S(1)}, bf16[512,256]{1,0:T(8,128)(2,1)S(1)}, u32[]{:S(2)}, u32[]{:S(2)}) collective-permute-start(bf16[512,256]{1,0:T(8,128)(2,1)S(1)} %copy-done.36), channel_id=1, source_target_pairs={{0,12},{4,8},{8,4},{12,0},{16,28},{20,24},{24,20},{28,16},{1,13},{... | collective-permute-start | bytes 786440 | tf_op jit(solution)/shard_map/ppermute | solution.py:45
  142.4 25.4 %collective-permute-start.17 = (bf16[4,128,1024]{2,1,0:T(8,128)(2,1)}, bf16[4,128,1024]{2,1,0:T(8,128)(2,1)S(1)}, u32[]{:S(2)}, u32[]{:S(2)}) collective-permute-start(bf16[4,128,1024]{2,1,0:T(8,128)(2,1)} %get-tuple-element.268), channel_id=1, source_target_pairs={{0,8},{4,12},{8,0},{12,4},{16,24},{20,28},{24,16},{28,20},{1,9},{5... | collective-permute-start | bytes 3145736 | tf_op jit(solution)/shard_map/ppermute | solution.py:45
  143.0 27.2 %collective-permute-start.18 = (bf16[4,128,1024]{2,1,0:T(8,128)(2,1)S(1)}, bf16[4,128,1024]{2,1,0:T(8,128)(2,1)S(1)}, u32[]{:S(2)}, u32[]{:S(2)}) collective-permute-start(bf16[4,128,1024]{2,1,0:T(8,128)(2,1)S(1)} %get-tuple-element.267), channel_id=1, source_target_pairs={{0,16},{4,20},{8,24},{12,28},{16,0},{20,4},{24,8},{28,12},{1,17},{... | collective-permute-start | bytes 3145736 | tf_op jit(solution)/shard_map/ppermute | solution.py:45
  214.6 25.4 %collective-permute-start.23 = (bf16[2,256,1024]{2,1,0:T(8,128)(2,1)}, bf16[2,256,1024]{2,1,0:T(8,128)(2,1)S(1)}, u32[]{:S(2)}, u32[]{:S(2)}) collective-permute-start(bf16[2,256,1024]{2,1,0:T(8,128)(2,1)} %get-tuple-element.201), channel_id=1, source_target_pairs={{0,8},{4,12},{8,0},{12,4},{16,24},{20,28},{24,16},{28,20},{1,9},{5... | collective-permute-start | bytes 3145736 | tf_op jit(solution)/shard_map/ppermute | solution.py:45
  215.8 25.3 %collective-permute-start.24 = (bf16[2,256,1024]{2,1,0:T(8,128)(2,1)}, bf16[2,256,1024]{2,1,0:T(8,128)(2,1)}, u32[]{:S(2)}, u32[]{:S(2)}) collective-permute-start(bf16[2,256,1024]{2,1,0:T(8,128)(2,1)} %get-tuple-element.202), channel_id=1, source_target_pairs={{0,16},{4,20},{8,24},{12,28},{16,0},{20,4},{24,8},{28,12},{1,17},{... | collective-permute-start | bytes 3145736 | tf_op jit(solution)/shard_map/ppermute | solution.py:45
  251.0 22.0 %collective-permute-start.28 = (bf16[4,128,2048]{2,1,0:T(8,128)(2,1)}, bf16[4,128,2048]{2,1,0:T(8,128)(2,1)}, u32[]{:S(2)}, u32[]{:S(2)}) collective-permute-start(bf16[4,128,2048]{2,1,0:T(8,128)(2,1)} %up_grad_other.1), channel_id=1, source_target_pairs={{0,4},{4,0},{8,12},{12,8},{16,20},{20,16},{24,28},{28,24},{1,5},{5... | collective-permute-start | bytes 6291464 | tf_op jit(solution)/shard_map/ppermute | solution.py:45
  268.2 48.1 %collective-permute-start.26 = (bf16[256,1024]{1,0:T(8,128)(2,1)S(1)}, bf16[256,1024]{1,0:T(8,128)(2,1)}, u32[]{:S(2)}, u32[]{:S(2)}) collective-permute-start(bf16[256,1024]{1,0:T(8,128)(2,1)S(1)} %fusion.9), channel_id=1, source_target_pairs={{0,8},{4,12},{8,0},{12,4},{16,24},{20,28},{24,16},{28,20},{1,9},{5... | collective-permute-start | bytes 1572872 | tf_op jit(solution)/shard_map/ppermute | solution.py:45
  270.1 46.2 %collective-permute-start.25 = (bf16[256,1024]{1,0:T(8,128)(2,1)}, bf16[256,1024]{1,0:T(8,128)(2,1)}, u32[]{:S(2)}, u32[]{:S(2)}) collective-permute-start(bf16[256,1024]{1,0:T(8,128)(2,1)} %fusion.8), channel_id=1, source_target_pairs={{0,16},{4,20},{8,24},{12,28},{16,0},{20,4},{24,8},{28,12},{1,17},{... | collective-permute-start | bytes 1572872 | tf_op jit(solution)/shard_map/ppermute | solution.py:45
  271.8 16.9 %collective-permute-start.31 = (bf16[512,256]{1,0:T(8,128)(2,1)}, bf16[512,256]{1,0:T(8,128)(2,1)}, u32[]{:S(2)}, u32[]{:S(2)}) collective-permute-start(bf16[512,256]{1,0:T(8,128)(2,1)} %get-tuple-element.225), channel_id=1, source_target_pairs={{0,8},{4,12},{8,0},{12,4},{16,24},{20,28},{24,16},{28,20},{1,9},{5... | collective-permute-start | bytes 786440 | tf_op jit(solution)/shard_map/ppermute | solution.py:45
  273.0 19.7 %collective-permute-start.32 = (bf16[512,256]{1,0:T(8,128)(2,1)}, bf16[512,256]{1,0:T(8,128)(2,1)}, u32[]{:S(2)}, u32[]{:S(2)}) collective-permute-start(bf16[512,256]{1,0:T(8,128)(2,1)} %get-tuple-element.226), channel_id=1, source_target_pairs={{0,12},{4,8},{8,4},{12,0},{16,28},{20,24},{24,20},{28,16},{1,13},{... | collective-permute-start | bytes 786440 | tf_op jit(solution)/shard_map/ppermute | solution.py:45
  292.7 34.9 %collective-permute-start.33 = (bf16[2,64,5248]{2,1,0:T(8,128)(2,1)}, bf16[2,64,5248]{2,1,0:T(8,128)(2,1)}, u32[]{:S(2)}, u32[]{:S(2)}) collective-permute-start(bf16[2,64,5248]{2,1,0:T(8,128)(2,1)} %get-tuple-element.236), channel_id=1, source_target_pairs={{0,8},{4,12},{8,0},{12,4},{16,24},{20,28},{24,16},{28,20},{1,9},{5... | collective-permute-start | bytes 4030472 | tf_op jit(solution)/shard_map/ppermute | solution.py:45
  293.5 34.1 %collective-permute-start.34 = (bf16[2,64,5248]{2,1,0:T(8,128)(2,1)}, bf16[2,64,5248]{2,1,0:T(8,128)(2,1)}, u32[]{:S(2)}, u32[]{:S(2)}) collective-permute-start(bf16[2,64,5248]{2,1,0:T(8,128)(2,1)} %get-tuple-element.237), channel_id=1, source_target_pairs={{0,16},{4,20},{8,24},{12,28},{16,0},{20,4},{24,8},{28,12},{1,17},{... | collective-permute-start | bytes 4030472 | tf_op jit(solution)/shard_map/ppermute | solution.py:45
  331.9 33.7 %collective-permute-start.36 = (bf16[64,5248]{1,0:T(8,128)(2,1)}, bf16[64,5248]{1,0:T(8,128)(2,1)S(1)}, u32[]{:S(2)}, u32[]{:S(2)}) collective-permute-start(bf16[64,5248]{1,0:T(8,128)(2,1)} %fusion.7), channel_id=1, source_target_pairs={{0,8},{4,12},{8,0},{12,4},{16,24},{20,28},{24,16},{28,20},{1,9},{5... | collective-permute-start | bytes 2015240 | tf_op jit(solution)/shard_map/ppermute | solution.py:45
  333.1 32.5 %collective-permute-start.35 = (bf16[64,5248]{1,0:T(8,128)(2,1)}, bf16[64,5248]{1,0:T(8,128)(2,1)}, u32[]{:S(2)}, u32[]{:S(2)}) collective-permute-start(bf16[64,5248]{1,0:T(8,128)(2,1)} %fusion.6), channel_id=1, source_target_pairs={{0,16},{4,20},{8,24},{12,28},{16,0},{20,4},{24,8},{28,12},{1,17},{... | collective-permute-start | bytes 2015240 | tf_op jit(solution)/shard_map/ppermute | solution.py:45
  336.3 37.9 %all-to-all-start = ((bf16[8,4,32,512]{3,2,1,0:T(8,128)(2,1)}), bf16[8,4,32,512]{3,2,1,0:T(8,128)(2,1)S(1)}, u32[]{:S(2)}, u32[]{:S(2)}) async-start(bf16[8,4,32,512]{3,2,1,0:T(8,128)(2,1)} %bitcast.39), calls=%async_computation | async-start | bytes 2097152 | tf_op jit(solution)/shard_map/all_to_all | solution.py:1201
  344.2 88.5 %reduce-scatter.3.cloned.1.call-start = ((), (), s32[]{:S(2)}) async-start(), calls=%async_computation.5 | async-start | bytes 1679360 | tf_op jit(solution)/shard_map/reduce_scatter | solution.py:1073
  389.3 18.6 %collective-permute-start.21 = (bf16[256,1024]{1,0:T(8,128)(2,1)}, bf16[256,1024]{1,0:T(8,128)(2,1)}, u32[]{:S(2)}, u32[]{:S(2)}) collective-permute-start(bf16[256,1024]{1,0:T(8,128)(2,1)} %get-tuple-element.190), channel_id=1, source_target_pairs={{0,16},{4,20},{8,24},{12,28},{16,0},{20,4},{24,8},{28,12},{1,17},{... | collective-permute-start | bytes 1572872 | tf_op jit(solution)/shard_map/ppermute | solution.py:45
  397.2 43.6 %all-to-all-start.1 = ((bf16[8,4,32,512]{3,2,1,0:T(8,128)(2,1)}), bf16[8,4,32,512]{3,2,1,0:T(8,128)(2,1)}, u32[]{:S(2)}, u32[]{:S(2)}) async-start(bf16[8,4,32,512]{3,2,1,0:T(8,128)(2,1)} %bitcast.105), calls=%async_computation.1 | async-start | bytes 2097152 | tf_op jit(solution)/shard_map/all_to_all | solution.py:1201
  407.3 24.2 %collective-permute-start.38 = (bf16[256,1024]{1,0:T(8,128)(2,1)}, bf16[256,1024]{1,0:T(8,128)(2,1)}, u32[]{:S(2)}, u32[]{:S(2)}) collective-permute-start(bf16[256,1024]{1,0:T(8,128)(2,1)} %get-tuple-element.265), channel_id=1, source_target_pairs={{0,8},{4,12},{8,0},{12,4},{16,24},{20,28},{24,16},{28,20},{1,9},{5... | collective-permute-start | bytes 1572872 | tf_op jit(solution)/shard_map/ppermute | solution.py:45
  423.0 26.8 %collective-permute-start.40 = (bf16[256,1024]{1,0:T(8,128)(2,1)}, bf16[256,1024]{1,0:T(8,128)(2,1)}, u32[]{:S(2)}, u32[]{:S(2)}) collective-permute-start(bf16[256,1024]{1,0:T(8,128)(2,1)} %fusion.2), channel_id=1, source_target_pairs={{0,16},{4,20},{8,24},{12,28},{16,0},{20,4},{24,8},{28,12},{1,17},{... | collective-permute-start | bytes 1572872 | tf_op jit(solution)/shard_map/ppermute | solution.py:45
  (54 other events, 492.9 us)
Sparse Core Ops, SparseCore 0:
  40.3 35.6 all-gather.4
  77.5 44.9 all-gather.6
  320.2 34.1 reduce-scatter.4
  389.4 40.0 reduce-scatter.2

commit v3 on v2

--- a/solution.py
+++ b/solution.py
@@ -321,7 +321,7 @@
             pltpu.VMEM((total, width), BF),
         ],
         compiler_params=params(60),
-        cost_estimate=takes(19),
+        cost_estimate=takes(40),
         name="attention_backward",
     )(scal, qkv, *grads, out_t, lse)
 
@@ -944,110 +944,68 @@
     )(scal, *y1s, *dus, heads, dao, small, came, came_out)
 
 
-def qkv_grad_kernel(scal, x, dqkv, out, acc, sums, *, half):
-    n = pl.program_id(0)
+def qkv_grad_kernel(scal, x, dqkv, send, keep):
     ones = jnp.ones((dqkv.shape[0], 128), BF)
-    rows = contract(x[...], dqkv[...], 0, 0)
-    q_sum = contract(dqkv[:, 0:128], ones, 0, 0)
-    v_sum = contract(dqkv[:, 256:384], ones, 0, 0)
-
-    @pl.when(n == 0)
-    def _():
-        acc[...] = rows
-        sums[0] = q_sum
-        sums[1] = v_sum
-
-    @pl.when(n > 0)
-    def _():
-        acc[...] += rows
-        sums[0] += q_sum
-        sums[1] += v_sum
-
-    @pl.when(n == 3)
-    def _():
-        lane = lax.broadcasted_iota(jnp.int32, (128, 128), 1)
-        extra = jnp.where(lane == 0, sums[0], jnp.where(lane == 1, sums[1], 0.0))
-        for r in range(8):
-            here = jnp.where(2 * scal[LOW] + half == r, 1.0, 0.0)
-            block = jnp.concatenate(
-                [acc[128 * r : 128 * (r + 1), :], extra * here], 1
-            ).astype(BF)
-            for f in range(4):
-                out[r // 4, f, r % 4] = block[32 * f : 32 * (f + 1), :]
-
-
-def qkv_grad(scal, x_all, dqkv, half, cost):
-    total = x_all.shape[0]
-    part = total // 4
-    return pl.pallas_call(
-        partial(qkv_grad_kernel, half=half),
-        out_shape=struct((2, 4, 4, 32, 512), BF),
-        grid_spec=pltpu.PrefetchScalarGridSpec(
-            num_scalar_prefetch=1,
-            grid=(4,),
-            in_specs=[
-                pl.BlockSpec((part, D), lambda n, s: (n, 0)),
-                pl.BlockSpec((part, 384), lambda n, s: (n, 0)),
-            ],
-            out_specs=pl.BlockSpec((2, 4, 4, 32, 512), lambda n, s: (0, 0, 0, 0, 0)),
-            scratch_shapes=[pltpu.VMEM((D, 384), F32), pltpu.VMEM((2, 128, 128), F32)],
-        ),
-        compiler_params=params(60),
-        cost_estimate=takes(cost),
+    lane = lax.broadcasted_iota(jnp.int32, (256, 128), 1)
+    q_sum = contract(dqkv[:, 0:256], ones, 0, 0)
+    v_sum = contract(dqkv[:, 512:768], ones, 0, 0)
+    extra = jnp.where(lane == 0, q_sum, jnp.where(lane == 1, v_sum, 0.0))
+    for y, out in ((1 - scal[TOP], send), (scal[TOP], keep)):
+        for r in range(2):
+            group = 2 * y + r
+            rows = contract(x[:, aligned(256 * group, 256)], dqkv[...], 0, 0)
+            here = jnp.where(scal[LOW] == group, 1.0, 0.0)
+            block = jnp.concatenate([rows, extra * here], 1).astype(BF)
+            for e in range(2):
+                for f in range(4):
+                    at = 128 * e + 32 * f
+                    out[f, 2 * r + e] = block[at : at + 32, :]
+
+
+def qkv_grad(scal, x_all, dqkv):
+    return pl.pallas_call(
+        qkv_grad_kernel,
+        out_shape=(struct((4, 4, 32, 896), BF),) * 2,
+        in_specs=[SMEM, VMEM, VMEM],
+        out_specs=(VMEM, VMEM),
+        compiler_params=params(60),
+        cost_estimate=takes(8),
         name="qkv_grad",
     )(scal, x_all, dqkv)
 
 
-def input_grad_kernel(scal, dqkv_a, dqkv_b, weight, dao, away, near):
-    n = pl.program_id(0)
-    held = (n + 4) % 8
-    joined = jnp.concatenate(
-        [dqkv[:, 128 * k : 128 * (k + 1)] for k in range(3) for dqkv in (dqkv_a, dqkv_b)], 1
-    )
-    total = contract(joined, weight[...], 1, 1)
+def input_grad_kernel(scal, dqkv, weight, dao, out, *, first):
+    held = pl.program_id(0) + first
+    total = contract(dqkv[...], weight[...], 1, 1)
     turn = (held // 4) + 2 * ((held // 2) % 2) + 4 * (held % 2)
-    parts = []
     for e in range(2):
         place = scal[INVERSE + 2 * (scal[ME] ^ turn) + e]
         other = (place // 2) ^ scal[ME]
         mine = jnp.where((other == 0) | (other == 4), 1.0, 0.0)
         source = aligned(((other // 4) % 2) * 256 + (place % 2) * BLK, BLK)
         rows = total[BLK * e : BLK * (e + 1)]
-        parts.append((rows + dao[source, :].astype(F32) * mine).astype(BF))
-    result = jnp.concatenate(parts, 0)
-
-    @pl.when(n < 4)
-    def _():
-        away[0] = result
-
-    @pl.when(n >= 4)
-    def _():
-        near[0] = result
-
-
-def input_grad(scal, dqkv_a, dqkv_b, weight, dao):
-    rows = pl.BlockSpec((256, 384), lambda n, s: ((n + 4) % 8, 0))
-    return pl.pallas_call(
-        input_grad_kernel,
-        out_shape=(struct((4, 256, D), BF),) * 2,
+        out[0, BLK * e : BLK * (e + 1), :] = (rows + dao[source, :].astype(F32) * mine).astype(BF)
+
+
+def input_grad(scal, dqkv, weight, dao, first):
+    rows = pl.BlockSpec((256, 768), lambda n, s: (n + first, 0))
+    return pl.pallas_call(
+        partial(input_grad_kernel, first=first),
+        out_shape=struct((4, 256, D), BF),
         grid_spec=pltpu.PrefetchScalarGridSpec(
             num_scalar_prefetch=1,
-            grid=(8,),
+            grid=(4,),
             in_specs=[
-                rows,
                 rows,
                 pl.BlockSpec((D, 768), lambda n, s: (0, 0)),
                 pl.BlockSpec((ROWS, D), lambda n, s: (0, 0)),
             ],
-            out_specs=(
-                pl.BlockSpec((1, 256, D), lambda n, s: (jnp.minimum(n, 3), 0, 0)),
-                pl.BlockSpec((1, 256, D), lambda n, s: (jnp.maximum(n - 4, 0), 0, 0)),
-            ),
+            out_specs=pl.BlockSpec((1, 256, D), lambda n, s: (n, 0, 0)),
         ),
         compiler_params=params(60),
-        cost_estimate=takes(7),
+        cost_estimate=takes(5),
         name="input_grad",
-    )(scal, dqkv_a, dqkv_b, weight, dao)
+    )(scal, dqkv, weight, dao)
 
 
 def after(value, *others):
@@ -1066,11 +1024,14 @@
     return hop(add_low(a_keep[1], a_came[1]), 4), hop(add_low(b_keep[1], b_came[1]), 2)
 
 
-def own_rows_of(a_keep, b_keep, a_came, b_came, a_next, b_next):
+def sum_chips(a_keep, b_keep, a_came, b_came, a_next, b_next):
     a_all = a_keep[0].astype(F32) + a_came[0].astype(F32) + a_next.astype(F32)
     b_all = b_keep[0].astype(F32) + b_came[0].astype(F32) + b_next.astype(F32)
-    both = jnp.concatenate([a_all, b_all], 0).astype(BF)
-    return lax.psum_scatter(both, "fsdp", scatter_dimension=0, tiled=True)
+    return jnp.concatenate([a_all, b_all], 0).astype(BF)
+
+
+def sum_shards(rows):
+    return lax.psum_scatter(rows, "fsdp", scatter_dimension=0, tiled=True)
 
 
 def tiled_device(
@@ -1114,23 +1075,20 @@
         [lax.dynamic_index_in_dim(up_own, scal[SHARD + k], 0, False) for k in (1, 2, 3)]
     )
     up_x, up_y = hop(foreign, 2), hop(foreign, 4)
+    out_far = hop(foreign[:, :, 512:], 6)
     *sent, turned, lse = attention_forward(scal, after(qkv, foreign), chunk)
-    up_x, up_y, *sent = tied(up_x, up_y, *sent)
-    far_a, far_b, *far_heads = tied(
-        hop(up_y[:, :128], 2), hop(up_x[:, 128:], 4), hop(sent[2], 2), hop(sent[3], 3)
-    )
-    heads = [sent[0], hop(sent[1], 1), *far_heads]
+    up_x, up_y, out_far, *sent = tied(up_x, up_y, out_far, *sent)
+    near = jnp.stack([piece[:, :, 512:] for piece in (foreign, up_x, up_y)] + [out_far])
+    away, *came_heads = tied(hop(near, 1), *[hop(sent[k], k) for k in (1, 2, 3)])
+    heads = [sent[0], *came_heads]
+    far_a, far_b = hop(after(up_y, away)[:, :128], 2), hop(after(up_x, away)[:, 128:], 4)
     ups = (foreign, up_x, up_y, far_a, far_b)
-    near = jnp.stack(
-        [piece[:, :, 512:] for piece in (foreign, up_x, up_y)]
-        + [jnp.concatenate([far_a[:, :, 512:], far_b[:, :, 512:]], 1)]
-    )
-    away = hop(near, 1)
+    y1, y1_low, n1, r1 = attention_out(scal, heads, vecs, x_all, w_out, near, away)
+    y1, y1_low, n1, r1, far_a, far_b = tied(y1, y1_low, n1, r1, far_a, far_b)
+    ups = (foreign, up_x, up_y, far_a, far_b)
+
     down_own = after(down_own, far_a, far_b)
     down_y, down_x = hop(down_own[:, 0], 4), hop(down_own[:, 1], 2)
-
-    y1, y1_low, n1, r1 = attention_out(scal, heads, vecs, x_all, w_out, near, away)
-
     y1_away = hop(y1_low, 1)
     act, slope = feed_up(scal, y1_low, up_b, w_up, ups)
     act, slope, y1_away = tied(act, slope, y1_away)
@@ -1143,12 +1101,11 @@
     part, part_away, cot_came = tied(part, part_away, cot_came)
     out_own, out_away, dh2, dz2, sums2 = second_norm(y1, part, part_away, cot_own, cot_came, vecs)
     dz2_away = hop(dz2, 1)
-    mixed_came = hop(out_away, 4)
+    dak, das, dbk, dbs = down_grad(scal, (act, act_away), (dz2, dz2_away))
+    dak, das, dbk, dbs, mixed_came = tied(dak, das, dbk, dbs, hop(out_away, 4))
     mixed = jnp.where(
         top == 0, jnp.stack([out_own, mixed_came]), jnp.stack([mixed_came, out_own])
     )[:, None]
-
-    dak, das, dbk, dbs = down_grad(scal, (act, act_away), (dz2, dz2_away))
     da_came, db_came = hop(das, 2), hop(dbs, 4)
     du, du_away, part, part_away, up_sums = feed_back(
         scal, (dz2, after(dz2_away, dak)), (slope, slope_away), w_up, ups, downs
@@ -1185,52 +1142,44 @@
         scal, y1s, dus, all_heads, dao, vec_block, up_came, hop(out_other, 1)
     )
     uak, uas, ubk, ubs, *dattn = tied(uak, uas, ubk, ubs, *dattn)
+    da_next, db_next = add_far(dak, dbk, da_came, db_came)
     ua_came, ub_came = hop(uas, 2), hop(ubs, 4)
-    da_next, db_next = add_far(dak, dbk, da_came, db_came)
-    dqkv_a = attention_backward(
-        scal, after(qkv, uak), dattn, turned, lse, chunk, 0, 2
-    )
-    da_next, db_next, dqkv_a = tied(da_next, db_next, dqkv_a)
-    down_rows = own_rows_of(dak, dbk, da_came, db_came, da_next, db_next)
-    grad_a = qkv_grad(scal, x_all, dqkv_a, 0, 0.05)
-    ua_came, ub_came, grad_a = tied(ua_came, ub_came, grad_a)
-    ua_next, ub_next = add_far(uak, ubk, ua_came, ub_came)
-
-    def to_owners(grad):
-        groups = [[4 * ctx + f for ctx in (k, k + 4) for f in range(4)] for k in range(4)]
-        return lax.all_to_all(
-            grad.reshape(8, 4, 32, 512), ("ctx", "fsdp"), 0, 0, tiled=True,
-            axis_index_groups=groups,
-        )
-
-    grad_a = to_owners(grad_a)
-    dqkv_b = attention_backward(
-        scal, after(qkv, dqkv_a, ua_came), dattn, turned, lse, chunk, 2, 2
-    )
-    ua_next, ub_next, grad_a, dqkv_b = tied(ua_next, ub_next, grad_a, dqkv_b)
-    up_rows = own_rows_of(uak, ubk, ua_came, ub_came, ua_next, ub_next).astype(F32)
-
-    dx_away, dx = input_grad(scal, dqkv_a, dqkv_b, qkv_weight, dao)
-    grad_b = qkv_grad(scal, x_all, after(dqkv_b, dx_away), 1, 6)
-    grad_b, dx_came = tied(grad_b, hop(dx_away, 1))
-    dx = add_low(dx, dx_came)
-    far_rows, own_rows = hop(dx[3], 2), hop(dx[2], 2)
-    grad_b = to_owners(grad_b)
-    grad_far = add_low(dx[1], far_rows)
-    grad_came = hop(grad_far, 4)
-    grad_b = after(grad_b, grad_far)
-    grad_own = add_low(dx[0], after(own_rows, grad_far))
+    dqkv = attention_backward(scal, after(qkv, uak), dattn, turned, lse, chunk, 0, 4)
+    da_next, db_next, ua_came, ub_came, dqkv = tied(da_next, db_next, ua_came, ub_came, dqkv)
+
+    ua_sent, ub_sent = add_low(uak[1], ua_came[1]), add_low(ubk[1], ub_came[1])
+    ua_next, ub_next = hop(ua_sent, 4), hop(ub_sent, 2)
+    down_sum = sum_chips(dak, dbk, da_came, db_came, after(da_next, ua_sent, ub_sent), db_next)
+    down_rows = sum_shards(down_sum)
+    grad_send, grad_keep = qkv_grad(scal, x_all, dqkv)
+    grad_send, grad_keep, ua_next, ub_next = tied(grad_send, grad_keep, ua_next, ub_next)
+    grad_came = hop(grad_send, 4)
+    up_sum = sum_chips(uak, ubk, ua_came, ub_came, ua_next, ub_next)
+    up_rows = sum_shards(up_sum).astype(F32)
+    dx_away = input_grad(scal, after(dqkv, grad_keep, up_sum), qkv_weight, dao, 4)
+    dx = input_grad(scal, dqkv, qkv_weight, after(dao, dx_away), 0)
+    dx_came, dx, grad_came = tied(hop(dx_away, 1), dx, grad_came)
+    grad_parts = lax.all_to_all(
+        add_low(grad_keep, grad_came), "fsdp", 0, 0, tiled=True
+    )
+    sent_rows = add_low(dx[2:], dx_came[2:])
+    far_rows = hop(sent_rows[1], 2)
+    kept_rows = add_low(dx[:2], after(dx_came, sent_rows)[:2])
+    far_rows, kept_rows = tied(far_rows, kept_rows)
+    own_rows = hop(after(sent_rows[0], far_rows), 2)
+    home_rows = hop(add_low(kept_rows[1], far_rows), 4)
+    grad_parts, own_rows, home_rows = tied(grad_parts, own_rows, home_rows)
+    grad_own = add_low(kept_rows[0], own_rows)
     tokens_grad = jnp.where(
-        top == 0, jnp.stack([grad_own, grad_came]), jnp.stack([grad_came, grad_own])
+        top == 0, jnp.stack([grad_own, home_rows]), jnp.stack([home_rows, grad_own])
     )[:, None]
-    mine = [jnp.sum(parts.astype(F32), 0).astype(BF) for parts in (grad_a, grad_b)]
     mine = lax.all_to_all(
-        jnp.concatenate(mine, 2), "ctx", 0, 0, tiled=True, axis_index_groups=half_groups
+        jnp.sum(grad_parts.astype(F32), 0).astype(BF), "ctx", 0, 0, tiled=True,
+        axis_index_groups=half_groups,
     ).astype(F32)
-    mine = mine.reshape(4, 32, 2, 4, 128)
-    w_qkv_grad = mine[:, :, :, :3].transpose(1, 3, 0, 2, 4).reshape(32, 3072)
-    q_bias_grad = jnp.sum(mine[:, :, :, 3, 0], (0, 2))
-    v_bias_grad = jnp.sum(mine[:, :, :, 3, 1], (0, 2))
+    w_qkv_grad = mine[:, :, :768].reshape(4, 32, 3, 256).transpose(1, 2, 0, 3).reshape(32, 3072)
+    q_bias_grad = jnp.sum(mine[:, :, 768], 0)
+    v_bias_grad = jnp.sum(mine[:, :, 769], 0)
 
     w_up_grad = (
         up_rows[:, :4096].reshape(32, 8, 4, 128).transpose(0, 2, 1, 3).reshape(32, 4096)

time: 471 us -> 451 us (0.958)
  Pallas kernels: 208 us -> 199 us
  starting transfers between devices: 64.3 us -> 55.5 us
  other arithmetic: 38.2 us -> 33 us
    ppermute x38 -> x40, waiting for transfers between devices: 86.5 us -> 99.1 us  [hop(): return lax.ppermute(value, 'ctx', [(i, i ^ mask) for i in range(count)])]
    all_to_all x3 -> x2, waiting for transfers between devices: 15 us -> 5.63 us  [the longest x1 3.58 us: tiled_device(): lax.all_to_all(add_low(grad_keep, grad_came), 'fsdp', 0, 0, tiled=True)]
    all_to_all x3 -> x2, starting transfers between devices: 15.6 us -> 10.9 us  [the longest x1 7.49 us: tiled_device(): lax.all_to_all(add_low(grad_keep, grad_came), 'fsdp', 0, 0, tiled=True)]
    pallas_call x2 -> x1, Pallas kernels: 42.1 us -> 37.6 us  [attention_backward(): pl.pallas_call(partial(attention_backward_kernel, first=first, heads=head...]
    ppermute x38 -> x40, starting transfers between devices: 42.8 us -> 39 us  [hop(): return lax.ppermute(value, 'ctx', [(i, i ^ mask) for i in range(count)])]
    convert_element_type x6 -> x8, other arithmetic: 11.9 us -> 11.5 us  [add_low(): return (a.astype(F32) + b.astype(F32)).astype(BF)]
  transfers between devices with their start and end apart: 48 -> 49, of which waited for: 23 -> 30; matrix products, arithmetic and copies ran while one was open for 10% -> 9% of each run, Pallas kernels for 37% -> 41%
where the time goes in v3:
time: 451 us; the launch traced here: 442 us
  Pallas kernels  199 us (44%)
  waiting for transfers between devices  118 us (26%)
  starting transfers between devices  55.5 us (12%)
  other arithmetic  33 us (7%)
  local copies, waits for them, and re-layouts  20.4 us (5%)
  between operations  16 us (4%)
    ppermute x40, waiting for transfers between devices, hop(): return lax.ppermute(value, 'ctx', [(i, i ^ mask) for i in range(count)])  99.1 us
    ppermute x40, starting transfers between devices, hop(): return lax.ppermute(value, 'ctx', [(i, i ^ mask) for i in range(count)])  39 us
    pallas_call x1, Pallas kernels, attention_backward(): pl.pallas_call(partial(attention_backward_kernel, first=first, heads=head...  37.6 us
    pallas_call x1, Pallas kernels, attention_forward(): pl.pallas_call(partial(attention_forward_kernel, heads=heads, chunk=chunk...  22.2 us
    pallas_call x1, Pallas kernels, feed_back(): pl.pallas_call(back_kernel, out_shape=(du, du, struct((ROWS, D), F32), st...  17.7 us
    pallas_call x2, Pallas kernels, feed_up(): pl.pallas_call(up_kernel, out_shape=(struct((4, ROWS, 512), BF), struct((...  16.1 us
    pallas_call x2, Pallas kernels, feed_down(): pl.pallas_call(down_kernel, out_shape=struct((ROWS, D), dtype), in_specs=...  14.2 us
    ppermute x3, waiting for transfers between devices, around(): lax.ppermute(value, 'fsdp', [(i, (i + k) % 4) for i in range(4)])  13 us
  transfers between devices with their start and end apart: 49, of which 30 were waited for; matrix products, arithmetic and copies ran while one was open for 9% of the time, Pallas kernels for 41%

profile of v3, /device:TPU:0, one launch (start us, length us, event | category | flops | bytes accessed | tf_op | source)
XLA Modules:
  0.0 442.0 jit_solution(10560263037830501277)
XLA Ops:
  9.6 4.6 %carve.1 = (bf16[256,1024]{1,0:T(8,128)(2,1)}, bf16[256,1024]{1,0:T(8,128)(2,1)}, bf16[256,1024]{1,0:T(8,128)(2,1)}, bf16[256,1024]{1,0:T(8,128)(2,1)}, bf16[256...) custom-call(bf16[2,1,256,1024]{3,2,1,0:T(8,128)(2,1)} %tokens.1, ...), custom_call_target="tpu_custom_call" | custom-call | flops 4600000000 | bytes 1048576 | tf_op jit(solution)/shard_map/carve/pallas_call | solution.py:359
  22.8 5.0 %collective-permute-done = bf16[144,768]{1,0:T(8,128)(2,1)S(1)} collective-permute-done((bf16[144,768]{1,0:T(8,128)(2,1)}, bf16[144,768]{1,0:T(8,128)(2,1)S(1)}, u32[]{:S(2)}, u32[]{:S(2)}) %collective-permute-start) | collective-permute-done | bytes 221216 | tf_op jit(solution)/shard_map/ppermute | solution.py:1059
  27.8 8.1 %collective-permute-done.1 = bf16[144,768]{1,0:T(8,128)(2,1)S(1)} collective-permute-done((bf16[144,768]{1,0:T(8,128)(2,1)}, bf16[144,768]{1,0:T(8,128)(2,1)S(1)}, u32[]{:S(2)}, u32[]{:S(2)}) %collective-permute-start.1) | collective-permute-done | bytes 221216 | tf_op jit(solution)/shard_map/ppermute | solution.py:1059
  40.2 16.2 %collective-permute-done.5.away = bf16[3,144,768]{2,1,0:T(8,128)(2,1)} collective-permute-done((bf16[3,144,768]{2,1,0:T(8,128)(2,1)}, bf16[3,144,768]{2,1,0:T(8,128)(2,1)}, u32[]{:S(2)}, u32[]{:S(2)}) %collective-permute-start.5) | collective-permute-done | bytes 663584 | tf_op jit(solution)/shard_map/ppermute | solution.py:45
  56.4 5.8 %collective-permute-done.4.x = bf16[2,256,1024]{2,1,0:T(8,128)(2,1)S(1)} collective-permute-done((bf16[2,256,1024]{2,1,0:T(8,128)(2,1)S(1)}, bf16[2,256,1024]{2,1,0:T(8,128)(2,1)S(1)}, u32[]{:S(2)}, u32[]{:S(2)}) %collective-permute-start.4) | collective-permute-done | bytes 1048608 | tf_op jit(solution)/shard_map/ppermute | solution.py:45
  66.7 10.2 %project.1 = (bf16[2048,768]{1,0:T(8,128)(2,1)}, bf16[2048,1024]{1,0:T(8,128)(2,1)}, bf16[1024,768]{1,0:T(8,128)(2,1)}, f32[8,1024]{1,0:T(8,128)}, f32[8,512]{1,0:T(8,128)}) custom-call(s32[42]{0:T(128)} %concatenate.48.scal, bf16[256,768]{1,0:T(8,128)(2,1)} %get-tuple-element.161.pack, bf16[16,256]{1,0:T(8,128)(2,1)} %select_select_fusion.small, ...), custom_call_target="tpu_custom_call" | custom-call | flops 9200000000 | bytes 1048576 | tf_op jit(solution)/shard_map/project/pallas_call | solution.py:424
  82.1 22.2 %attention_forward.1 = (bf16[512,256]{1,0:T(8,128)(2,1)}, bf16[512,256]{1,0:T(8,128)(2,1)}, bf16[512,256]{1,0:T(8,128)(2,1)}, bf16[512,256]{1,0:T(8,128)(2,1)}, f32[256,2048]{1,0:T(8,128)}, /*index=5*/f32[4,2048]{1,0:T(4,128)}) custom-call(s32[42]{0:T(128)} %concatenate.48.scal, bf16[2048,768]{1,0:T(8,128)(2,1)} %get-tuple-element.264.qkv), custom_call_target="tpu_custom_call" | custom-call | flops 26449999872 | bytes 1048576 | tf_op jit(solution)/shard_map/attention_forward/pallas_call | solution.py:211
  111.7 7.0 %collective-permute-done.13.h2 = bf16[512,256]{1,0:T(8,128)(2,1)S(1)} collective-permute-done((bf16[512,256]{1,0:T(8,128)(2,1)S(1)}, bf16[512,256]{1,0:T(8,128)(2,1)S(1)}, u32[]{:S(2)}, u32[]{:S(2)}) %collective-permute-start.13) | collective-permute-done | bytes 262176 | tf_op jit(solution)/shard_map/ppermute | solution.py:45
  125.8 9.0 %attention_out.1 = (f32[512,1024]{1,0:T(8,128)}, bf16[512,1024]{1,0:T(8,128)(2,1)}, f32[512,1024]{1,0:T(8,128)}, f32[512,128]{1,0:T(8,128)}) custom-call(s32[42]{0:T(128)} %concatenate.48.scal, bf16[512,256]{1,0:T(8,128)(2,1)} %get-tuple-element.176.h0, bf16[512,256]{1,0:T(8,128)(2,1)} %copy-done.22, bf16[512,256]{1,0:T(8,128)(2,1)} %copy-done.24, ...), custom_call_target="tpu_custom_call" | custom-call | flops 10350000128 | bytes 1048576 | tf_op jit(solution)/shard_map/attention_out/pallas_call | solution.py:492
  142.0 8.0 %feed_up.2 = (bf16[4,512,512]{2,1,0:T(8,128)(2,1)}, bf16[4,512,512]{2,1,0:T(8,128)(2,1)}) custom-call(s32[42]{0:T(128)} %concatenate.48.scal, bf16[512,1024]{1,0:T(8,128)(2,1)} %get-tuple-element.196.y1_low.y1_a, f32[8,512]{1,0:T(8,128)} %get-tuple-element.197.up_bias, bf16[256,4096]{1,0:T(8,128)(2,1)} %w_up.7, bf16[3,256,640]{2,1,0:T(8,128)(2,1)} %copy-done.3, ...), custom_call_target="tpu_custom_call" | custom-call | flops 8049999872 | bytes 1048576 | tf_op jit(solution)/shard_map/feed_up/pallas_call | solution.py:586
  151.0 8.0 %feed_up.3 = (bf16[4,512,512]{2,1,0:T(8,128)(2,1)}, bf16[4,512,512]{2,1,0:T(8,128)(2,1)}) custom-call(s32[42]{0:T(128)} %concatenate.48.scal, bf16[512,1024]{1,0:T(8,128)(2,1)} %copy-done.31, f32[8,512]{1,0:T(8,128)} %get-tuple-element.197.up_bias, bf16[256,4096]{1,0:T(8,128)(2,1)} %w_up.7, bf16[3,256,640]{2,1,0:T(8,128)(2,1)} %copy-done.3, ...), custom_call_target="tpu_custom_call" | custom-call | flops 8049999872 | bytes 1048576 | tf_op jit(solution)/shard_map/feed_up/pallas_call | solution.py:586
  159.1 6.6 %collective-permute-done.18.from_x.rest_7_ = bf16[4,128,1024]{2,1,0:T(8,128)(2,1)} collective-permute-done((bf16[4,128,1024]{2,1,0:T(8,128)(2,1)S(1)}, bf16[4,128,1024]{2,1,0:T(8,128)(2,1)}, u32[]{:S(2)}, u32[]{:S(2)}) %collective-permute-start.18) | collective-permute-done | bytes 1048608 | tf_op jit(solution)/shard_map/ppermute | solution.py:45
  166.8 7.2 %feed_down.3 = bf16[512,1024]{1,0:T(8,128)(2,1)} custom-call(s32[42]{0:T(128)} %concatenate.48.scal, bf16[4,512,512]{2,1,0:T(8,128)(2,1)} %get-tuple-element.211.act.act_b, bf16[4,2,128,1024]{3,2,1,0:T(8,128)(2,1)} %bitcast.91, bf16[4,128,1024]{2,1,0:T(8,128)(2,1)} %collective-permute-done.19.from_y.rest_6_, ...), custom_call_target="tpu_custom_call" | custom-call | flops 5750000128 | bytes 1048576 | tf_op jit(solution)/shard_map/feed_down/pallas_call | solution.py:623
  174.7 7.0 %feed_down.2.part = f32[512,1024]{1,0:T(8,128)} custom-call(s32[42]{0:T(128)} %concatenate.48.scal, bf16[4,512,512]{2,1,0:T(8,128)(2,1)} %get-tuple-element.202.act.act_a, bf16[4,2,128,1024]{3,2,1,0:T(8,128)(2,1)} %bitcast.92, bf16[4,128,1024]{2,1,0:T(8,128)(2,1)} %collective-permute-done.19.from_y.rest_6_, ...), custom_call_target="tpu_custom_call" | custom-call | flops 5750000128 | bytes 1048576 | tf_op jit(solution)/shard_map/feed_down/pallas_call | solution.py:623
  181.7 6.7 %collective-permute-done.21.cot_came = bf16[256,1024]{1,0:T(8,128)(2,1)S(1)} collective-permute-done((bf16[256,1024]{1,0:T(8,128)(2,1)S(1)}, bf16[256,1024]{1,0:T(8,128)(2,1)S(1)}, u32[]{:S(2)}, u32[]{:S(2)}) %collective-permute-start.21) | collective-permute-done | bytes 524320 | tf_op jit(solution)/shard_map/ppermute | solution.py:45
  189.6 6.6 %second_norm.1 = (bf16[256,1024]{1,0:T(8,128)(2,1)}, bf16[256,1024]{1,0:T(8,128)(2,1)}, f32[512,1024]{1,0:T(8,128)}, bf16[512,1024]{1,0:T(8,128)(2,1)}, f32[8,1024]{1,0:T(8,128)}) custom-call(f32[512,1024]{1,0:T(8,128)} %get-tuple-element.195.y1, f32[512,1024]{1,0:T(8,128)} %feed_down.2.part, bf16[512,1024]{1,0:T(8,128)(2,1)} %copy-done.33, ...), custom_call_target="tpu_custom_call" | custom-call | flops 4600000000 | bytes 1048576 | tf_op jit(solution)/shard_map/second_norm/pallas_call | solution.py:673
  200.1 9.8 %down_grad.1 = (bf16[2,256,1024]{2,1,0:T(8,128)(2,1)}, bf16[2,256,1024]{2,1,0:T(8,128)(2,1)}, bf16[2,256,1024]{2,1,0:T(8,128)(2,1)}, bf16[2,256,1024]{2,1,0:T(8,128)(2,1)}) custom-call(s32[42]{0:T(128)} %concatenate.48.scal, bf16[4,512,512]{2,1,0:T(8,128)(2,1)} %get-tuple-element.202.act.act_a, bf16[4,512,512]{2,1,0:T(8,128)(2,1)} %get-tuple-element.211.act.act_b, ...), custom_call_target="tpu_custom_call" | custom-call | flops 12650000384 | bytes 1048576 | tf_op jit(solution)/shard_map/down_grad/pallas_call | solution.py:821
  212.9 17.7 %feed_back.1 = (bf16[4,512,512]{2,1,0:T(8,128)(2,1)}, bf16[4,512,512]{2,1,0:T(8,128)(2,1)}, f32[512,1024]{1,0:T(8,128)}, bf16[512,1024]{1,0:T(8,128)(2,1)}, f32[8,512]{1,0:T(8,128)}) custom-call(s32[42]{0:T(128)} %concatenate.48.scal, bf16[512,1024]{1,0:T(8,128)(2,1)} %get-tuple-element.219.dz2_a, bf16[512,1024]{1,0:T(8,128)(2,1)} %copy-done.32, ...), custom_call_target="tpu_custom_call" | custom-call | flops 25300000768 | bytes 1048576 | tf_op jit(solution)/shard_map/feed_back/pallas_call | solution.py:729
  230.6 5.4 %collective-permute-done.24 = bf16[2,256,1024]{2,1,0:T(8,128)(2,1)S(1)} collective-permute-done((bf16[2,256,1024]{2,1,0:T(8,128)(2,1)}, bf16[2,256,1024]{2,1,0:T(8,128)(2,1)S(1)}, u32[]{:S(2)}, u32[]{:S(2)}) %collective-permute-start.24) | collective-permute-done | bytes 1048608 | tf_op jit(solution)/shard_map/ppermute | solution.py:45
  238.8 7.5 %up_grad_other.1 = bf16[4,128,2048]{2,1,0:T(8,128)(2,1)} custom-call(s32[42]{0:T(128)} %concatenate.48.scal, bf16[512,1024]{1,0:T(8,128)(2,1)} %get-tuple-element.196.y1_low.y1_a, bf16[512,1024]{1,0:T(8,128)(2,1)} %copy-done.31, bf16[4,512,512]{2,1,0:T(8,128)(2,1)} %get-tuple-element.240.du_a, bf16[4,512,512]{2,1,0:T(8,128)(2,1)} %get-tuple-element.241.du_b), custom_call_target="tpu_custom_call" | custom-call | flops 6899999744 | bytes 1048576 | tf_op jit(solution)/shard_map/up_grad_other/pallas_call | solution.py:901
  246.8 7.1 %first_norm.1 = (bf16[512,1024]{1,0:T(8,128)(2,1)}, bf16[512,256]{1,0:T(8,128)(2,1)}, bf16[512,256]{1,0:T(8,128)(2,1)}, bf16[512,256]{1,0:T(8,128)(2,1)}, bf16[512,256]{1,0:T(8,128)(2,1)}, /*index=5*/f32[8,1024]{1,0:T(8,128)}) custom-call(s32[42]{0:T(128)} %concatenate.48.scal, f32[512,1024]{1,0:T(8,128)} %get-tuple-element.242.dh2, ...), custom_call_target="tpu_custom_call" | custom-call | flops 8049999872 | bytes 1048576 | tf_op jit(solution)/shard_map/first_norm/pallas_call | solution.py:775
  256.1 5.2 %out_grad_other.1 = bf16[4,128,1152]{2,1,0:T(8,128)(2,1)} custom-call(s32[42]{0:T(128)} %concatenate.48.scal, bf16[4,512,256]{2,1,0:T(8,128)(2,1)} %pad_maximum_fusion.3.heads, bf16[512,1024]{1,0:T(8,128)(2,1)} %get-tuple-element.282.dao, f32[8,128,128]{2,1,0:T(8,128)} %bitcast.102), custom_call_target="tpu_custom_call" | custom-call | flops 3449999872 | bytes 1048576 | tf_op jit(solution)/shard_map/out_grad_other/pallas_call | solution.py:918
  266.0 10.4 %up_grad_own.1 = (bf16[2,64,5248]{2,1,0:T(8,128)(2,1)}, bf16[2,64,5248]{2,1,0:T(8,128)(2,1)}, bf16[2,64,5248]{2,1,0:T(8,128)(2,1)}, bf16[2,64,5248]{2,1,0:T(8,128)(2,1)}) custom-call(s32[42]{0:T(128)} %concatenate.48.scal, bf16[512,1024]{1,0:T(8,128)(2,1)} %get-tuple-element.196.y1_low.y1_a, bf16[512,1024]{1,0:T(8,128)(2,1)} %copy-done.31, ...), custom_call_target="tpu_custom_call" | custom-call | flops 11500000256 | bytes 1048576 | tf_op jit(solution)/shard_map/up_grad_own/pallas_call | solution.py:931
  276.4 5.6 %collective-permute-done.32.grad2 = bf16[512,256]{1,0:T(8,128)(2,1)S(1)} collective-permute-done((bf16[512,256]{1,0:T(8,128)(2,1)}, bf16[512,256]{1,0:T(8,128)(2,1)S(1)}, u32[]{:S(2)}, u32[]{:S(2)}) %collective-permute-start.32) | collective-permute-done | bytes 262176 | tf_op jit(solution)/shard_map/ppermute | solution.py:45
  282.1 4.5 %collective-permute-done.33.grad3 = bf16[512,256]{1,0:T(8,128)(2,1)S(1)} collective-permute-done((bf16[512,256]{1,0:T(8,128)(2,1)S(1)}, bf16[512,256]{1,0:T(8,128)(2,1)S(1)}, u32[]{:S(2)}, u32[]{:S(2)}) %collective-permute-start.33) | collective-permute-done | bytes 262176 | tf_op jit(solution)/shard_map/ppermute | solution.py:45
  288.6 37.6 %attention_backward.1.dqkv = bf16[2048,768]{1,0:T(8,128)(2,1)} custom-call(s32[42]{0:T(128)} %concatenate.48.scal, bf16[2048,768]{1,0:T(8,128)(2,1)} %get-tuple-element.264.qkv, bf16[512,256]{1,0:T(8,128)(2,1)} %get-tuple-element.265.grad0, bf16[512,256]{1,0:T(8,128)(2,1)} %copy-done.37, bf16[512,256]{1,0:T(8,128)(2,1)} %copy-done.38, ...), custom_call_target="tpu_custom_call" | custom-call | flops 46000001024 | bytes 1048576 | tf_op jit(solution)/shard_map/attention_backward/pallas_call | solution.py:306
  332.1 6.1 %collective-permute-start.36 = (bf16[64,5248]{1,0:T(8,128)(2,1)}, bf16[64,5248]{1,0:T(8,128)(2,1)}, u32[]{:S(2)}, u32[]{:S(2)}) collective-permute-start(bf16[64,5248]{1,0:T(8,128)(2,1)} %fusion.6), channel_id=1, source_target_pairs={{0,16},{4,20},{8,24},{12,28},{16,0},{20,4},{24,8},{28,12},{1,17},{... | collective-permute-start | bytes 2015240 | tf_op jit(solution)/shard_map/ppermute | solution.py:45
  342.0 8.2 %qkv_grad.1 = (bf16[4,4,32,896]{3,2,1,0:T(8,128)(2,1)}, bf16[4,4,32,896]{3,2,1,0:T(8,128)(2,1)}) custom-call(s32[42]{0:T(128)} %concatenate.48.scal, bf16[2048,1024]{1,0:T(8,128)(2,1)} %get-tuple-element.187.x_all.x, bf16[2048,768]{1,0:T(8,128)(2,1)} %attention_backward.1.dqkv), custom_call_target="tpu_custom_call" | custom-call | flops 9200000000 | bytes 1048576 | tf_op jit(solution)/shard_map/qkv_grad/pallas_call | solution.py:966
  357.5 6.4 %input_grad.2 = bf16[4,256,1024]{2,1,0:T(8,128)(2,1)} custom-call(s32[42]{0:T(128)} %concatenate.48.scal, bf16[2048,768]{1,0:T(8,128)(2,1)} %attention_backward.1.dqkv, bf16[1024,768]{1,0:T(8,128)(2,1)} %get-tuple-element.281.weight, bf16[512,1024]{1,0:T(8,128)(2,1)} %get-tuple-element.282.dao), custom_call_target="tpu_custom_call" | custom-call | flops 5750000128 | bytes 1048576 | tf_op jit(solution)/shard_map/input_grad/pallas_call | solution.py:992
  365.7 6.4 %input_grad.3 = bf16[4,256,1024]{2,1,0:T(8,128)(2,1)} custom-call(s32[42]{0:T(128)} %concatenate.48.scal, bf16[2048,768]{1,0:T(8,128)(2,1)} %attention_backward.1.dqkv, bf16[1024,768]{1,0:T(8,128)(2,1)} %get-tuple-element.281.weight, bf16[512,1024]{1,0:T(8,128)(2,1)} %get-tuple-element.282.dao), custom_call_target="tpu_custom_call" | custom-call | flops 5750000128 | bytes 1048576 | tf_op jit(solution)/shard_map/input_grad/pallas_call | solution.py:992
  372.1 14.8 %collective-permute-done.39 = bf16[4,4,32,896]{3,2,1,0:T(8,128)(2,1)S(1)} collective-permute-done((bf16[4,4,32,896]{3,2,1,0:T(8,128)(2,1)}, bf16[4,4,32,896]{3,2,1,0:T(8,128)(2,1)S(1)}, u32[]{:S(2)}, u32[]{:S(2)}) %collective-permute-start.39) | collective-permute-done | bytes 917536 | tf_op jit(solution)/shard_map/ppermute | solution.py:45
  392.8 7.5 %all-to-all-start = ((bf16[4,4,32,896]{3,2,1,0:T(8,128)(2,1)}), bf16[4,4,32,896]{3,2,1,0:T(8,128)(2,1)S(1)}, u32[]{:S(2)}, u32[]{:S(2)}) async-start(bf16[4,4,32,896]{3,2,1,0:T(8,128)(2,1)} %add_convert_fusion.2), calls=%async_computation | async-start | bytes 1835008 | tf_op jit(solution)/shard_map/all_to_all | solution.py:1162
  (261 shorter events, 127.6 us)
Async XLA Ops:
  7.2 69.8 %all-gather.5.cloned.1.call-start = ((), (), s32[]{:S(2)}) async-start(), calls=%async_computation.6 | async-start | bytes 1638400 | tf_op jit(solution)/shard_map/all_gather | solution.py:1065
  14.2 21.6 %collective-permute-start.3 = (bf16[256,1024]{1,0:T(8,128)(2,1)}, bf16[256,1024]{1,0:T(8,128)(2,1)S(1)}, u32[]{:S(2)}, u32[]{:S(2)}) collective-permute-start(bf16[256,1024]{1,0:T(8,128)(2,1)} %get-tuple-element.158), channel_id=1, source_target_pairs={{0,16},{4,20},{8,24},{12,28},{16,0},{20,4},{24,8},{28,12},{1,17},{... | collective-permute-start | bytes 1572872 | tf_op jit(solution)/shard_map/ppermute | solution.py:45
  18.9 17.0 %collective-permute-start.1 = (bf16[144,768]{1,0:T(8,128)(2,1)}, bf16[144,768]{1,0:T(8,128)(2,1)S(1)}, u32[]{:S(2)}, u32[]{:S(2)}) collective-permute-start(bf16[144,768]{1,0:T(8,128)(2,1)} %get-tuple-element.157), channel_id=1, source_target_pairs={{0,2},{1,3},{2,0},{3,1},{4,6},{5,7},{6,4},{7,5},{8,10},{9,11},{10,... | collective-permute-start | bytes 663560 | tf_op jit(solution)/shard_map/ppermute | solution.py:1059
  21.4 14.4 %collective-permute-start.2 = (bf16[144,768]{1,0:T(8,128)(2,1)}, bf16[144,768]{1,0:T(8,128)(2,1)S(1)}, u32[]{:S(2)}, u32[]{:S(2)}) collective-permute-start(bf16[144,768]{1,0:T(8,128)(2,1)} %get-tuple-element.157), channel_id=1, source_target_pairs={{0,3},{1,0},{2,1},{3,2},{4,7},{5,4},{6,5},{7,6},{8,11},{9,8},{10,9... | collective-permute-start | bytes 663560 | tf_op jit(solution)/shard_map/ppermute | solution.py:1059
  37.2 25.1 %collective-permute-start.4 = (bf16[2,256,1024]{2,1,0:T(8,128)(2,1)S(1)}, bf16[2,256,1024]{2,1,0:T(8,128)(2,1)S(1)}, u32[]{:S(2)}, u32[]{:S(2)}) collective-permute-start(bf16[2,256,1024]{2,1,0:T(8,128)(2,1)S(1)} %pad_maximum_fusion.2), channel_id=1, source_target_pairs={{0,8},{4,12},{8,0},{12,4},{16,24},{20,28},{24,16},{28,20},{1,9},{5... | collective-permute-start | bytes 3145736 | tf_op jit(solution)/shard_map/ppermute | solution.py:45
  39.6 16.8 %collective-permute-start.5 = (bf16[3,144,768]{2,1,0:T(8,128)(2,1)}, bf16[3,144,768]{2,1,0:T(8,128)(2,1)}, u32[]{:S(2)}, u32[]{:S(2)}) collective-permute-start(bf16[3,144,768]{2,1,0:T(8,128)(2,1)} %pad_maximum_fusion.7.near), channel_id=1, source_target_pairs={{0,16},{4,20},{8,24},{12,28},{16,0},{20,4},{24,8},{28,12},{1,17},{... | collective-permute-start | bytes 1990664 | tf_op jit(solution)/shard_map/ppermute | solution.py:45
  40.2 98.0 %all-gather.7.cloned.1.call-start = ((), (), s32[]{:S(2)}) async-start(), calls=%async_computation.7 | async-start | bytes 2621440 | tf_op jit(solution)/shard_map/all_gather | solution.py:1068
  65.5 343.7 %reduce-scatter.5.cloned.1.call-start = ((), (), s32[]{:S(2)}) async-start(), calls=%async_computation.5 | async-start | bytes 1310720 | tf_op jit(solution)/shard_map/reduce_scatter | solution.py:1034
  78.4 28.2 %collective-permute-start.8 = (bf16[3,256,640]{2,1,0:T(8,128)(2,1)S(1)}, bf16[3,256,640]{2,1,0:T(8,128)(2,1)S(1)}, u32[]{:S(2)}, u32[]{:S(2)}) collective-permute-start(bf16[3,256,640]{2,1,0:T(8,128)(2,1)S(1)} %pad_maximum_fusion.5.rest_0_), channel_id=1, source_target_pairs={{0,8},{4,12},{8,0},{12,4},{16,24},{20,28},{24,16},{28,20},{1,9},{5... | collective-permute-start | bytes 2949128 | tf_op jit(solution)/shard_map/ppermute | solution.py:45
  80.0 27.9 %collective-permute-start.9 = (bf16[3,256,640]{2,1,0:T(8,128)(2,1)S(1)}, bf16[3,256,640]{2,1,0:T(8,128)(2,1)}, u32[]{:S(2)}, u32[]{:S(2)}) collective-permute-start(bf16[3,256,640]{2,1,0:T(8,128)(2,1)S(1)} %pad_maximum_fusion.5.rest_0_), channel_id=1, source_target_pairs={{0,16},{4,20},{8,24},{12,28},{16,0},{20,4},{24,8},{28,12},{1,17},{... | collective-permute-start | bytes 2949128 | tf_op jit(solution)/shard_map/ppermute | solution.py:45
  80.5 26.1 %collective-permute-start.10 = (bf16[3,256,128]{2,1,0:T(8,128)(2,1)S(1)}, bf16[3,256,128]{2,1,0:T(8,128)(2,1)S(1)}, u32[]{:S(2)}, u32[]{:S(2)}) collective-permute-start(bf16[3,256,128]{2,1,0:T(8,128)(2,1)S(1)} %get-tuple-element.313), channel_id=1, source_target_pairs={{0,24},{4,28},{8,16},{12,20},{16,8},{20,12},{24,0},{28,4},{1,25},{... | collective-permute-start | bytes 589832 | tf_op jit(solution)/shard_map/ppermute | solution.py:45
  122.6 14.0 %collective-permute-start.16 = (bf16[3,128,640]{2,1,0:T(8,128)(2,1)S(1)}, bf16[3,128,640]{2,1,0:T(8,128)(2,1)}, u32[]{:S(2)}, u32[]{:S(2)}) collective-permute-start(bf16[3,128,640]{2,1,0:T(8,128)(2,1)S(1)} %slice.190), channel_id=1, source_target_pairs={{0,16},{4,20},{8,24},{12,28},{16,0},{20,4},{24,8},{28,12},{1,17},{... | collective-permute-start | bytes 1474568 | tf_op jit(solution)/shard_map/ppermute | solution.py:45
  139.9 25.7 %collective-permute-start.18 = (bf16[4,128,1024]{2,1,0:T(8,128)(2,1)S(1)}, bf16[4,128,1024]{2,1,0:T(8,128)(2,1)}, u32[]{:S(2)}, u32[]{:S(2)}) collective-permute-start(bf16[4,128,1024]{2,1,0:T(8,128)(2,1)S(1)} %get-tuple-element.306), channel_id=1, source_target_pairs={{0,8},{4,12},{8,0},{12,4},{16,24},{20,28},{24,16},{28,20},{1,9},{5... | collective-permute-start | bytes 3145736 | tf_op jit(solution)/shard_map/ppermute | solution.py:45
  141.4 25.4 %collective-permute-start.19 = (bf16[4,128,1024]{2,1,0:T(8,128)(2,1)S(1)}, bf16[4,128,1024]{2,1,0:T(8,128)(2,1)}, u32[]{:S(2)}, u32[]{:S(2)}) collective-permute-start(bf16[4,128,1024]{2,1,0:T(8,128)(2,1)S(1)} %get-tuple-element.305), channel_id=1, source_target_pairs={{0,16},{4,20},{8,24},{12,28},{16,0},{20,4},{24,8},{28,12},{1,17},{... | collective-permute-start | bytes 3145736 | tf_op jit(solution)/shard_map/ppermute | solution.py:45
  174.0 14.4 %collective-permute-start.20 = (bf16[512,1024]{1,0:T(8,128)(2,1)}, bf16[512,1024]{1,0:T(8,128)(2,1)S(1)}, u32[]{:S(2)}, u32[]{:S(2)}) collective-permute-start(bf16[512,1024]{1,0:T(8,128)(2,1)} %feed_down.3), channel_id=1, source_target_pairs={{0,4},{4,0},{8,12},{12,8},{16,20},{20,16},{24,28},{28,24},{1,5},{5... | collective-permute-start | bytes 3145736 | tf_op jit(solution)/shard_map/ppermute | solution.py:45
  174.1 14.3 %collective-permute-start.21 = (bf16[256,1024]{1,0:T(8,128)(2,1)S(1)}, bf16[256,1024]{1,0:T(8,128)(2,1)S(1)}, u32[]{:S(2)}, u32[]{:S(2)}) collective-permute-start(bf16[256,1024]{1,0:T(8,128)(2,1)S(1)} %copy-done.34), channel_id=1, source_target_pairs={{0,16},{4,20},{8,24},{12,28},{16,0},{20,4},{24,8},{28,12},{1,17},{... | collective-permute-start | bytes 1572872 | tf_op jit(solution)/shard_map/ppermute | solution.py:45
  196.4 14.5 %collective-permute-start.23 = (bf16[256,1024]{1,0:T(8,128)(2,1)}, bf16[256,1024]{1,0:T(8,128)(2,1)S(1)}, u32[]{:S(2)}, u32[]{:S(2)}) collective-permute-start(bf16[256,1024]{1,0:T(8,128)(2,1)} %get-tuple-element.224), channel_id=1, source_target_pairs={{0,16},{4,20},{8,24},{12,28},{16,0},{20,4},{24,8},{28,12},{1,17},{... | collective-permute-start | bytes 1572872 | tf_op jit(solution)/shard_map/ppermute | solution.py:45
  210.9 25.0 %collective-permute-start.24 = (bf16[2,256,1024]{2,1,0:T(8,128)(2,1)}, bf16[2,256,1024]{2,1,0:T(8,128)(2,1)S(1)}, u32[]{:S(2)}, u32[]{:S(2)}) collective-permute-start(bf16[2,256,1024]{2,1,0:T(8,128)(2,1)} %get-tuple-element.235), channel_id=1, source_target_pairs={{0,8},{4,12},{8,0},{12,4},{16,24},{20,28},{24,16},{28,20},{1,9},{5... | collective-permute-start | bytes 3145736 | tf_op jit(solution)/shard_map/ppermute | solution.py:45
  211.5 24.7 %collective-permute-start.25 = (bf16[2,256,1024]{2,1,0:T(8,128)(2,1)}, bf16[2,256,1024]{2,1,0:T(8,128)(2,1)S(1)}, u32[]{:S(2)}, u32[]{:S(2)}) collective-permute-start(bf16[2,256,1024]{2,1,0:T(8,128)(2,1)} %get-tuple-element.236), channel_id=1, source_target_pairs={{0,16},{4,20},{8,24},{12,28},{16,0},{20,4},{24,8},{28,12},{1,17},{... | collective-permute-start | bytes 3145736 | tf_op jit(solution)/shard_map/ppermute | solution.py:45
  246.4 19.5 %collective-permute-start.29 = (bf16[4,128,2048]{2,1,0:T(8,128)(2,1)}, bf16[4,128,2048]{2,1,0:T(8,128)(2,1)}, u32[]{:S(2)}, u32[]{:S(2)}) collective-permute-start(bf16[4,128,2048]{2,1,0:T(8,128)(2,1)} %up_grad_other.1), channel_id=1, source_target_pairs={{0,4},{4,0},{8,12},{12,8},{16,20},{20,16},{24,28},{28,24},{1,5},{5... | collective-permute-start | bytes 6291464 | tf_op jit(solution)/shard_map/ppermute | solution.py:45
  261.6 64.5 %collective-permute-start.27 = (bf16[256,1024]{1,0:T(8,128)(2,1)S(1)}, bf16[256,1024]{1,0:T(8,128)(2,1)}, u32[]{:S(2)}, u32[]{:S(2)}) collective-permute-start(bf16[256,1024]{1,0:T(8,128)(2,1)S(1)} %fusion.9), channel_id=1, source_target_pairs={{0,8},{4,12},{8,0},{12,4},{16,24},{20,28},{24,16},{28,20},{1,9},{5... | collective-permute-start | bytes 1572872 | tf_op jit(solution)/shard_map/ppermute | solution.py:45
  263.4 62.8 %collective-permute-start.26 = (bf16[256,1024]{1,0:T(8,128)(2,1)S(1)}, bf16[256,1024]{1,0:T(8,128)(2,1)}, u32[]{:S(2)}, u32[]{:S(2)}) collective-permute-start(bf16[256,1024]{1,0:T(8,128)(2,1)S(1)} %fusion.8), channel_id=1, source_target_pairs={{0,16},{4,20},{8,24},{12,28},{16,0},{20,4},{24,8},{28,12},{1,17},{... | collective-permute-start | bytes 1572872 | tf_op jit(solution)/shard_map/ppermute | solution.py:45
  264.4 17.6 %collective-permute-start.32 = (bf16[512,256]{1,0:T(8,128)(2,1)}, bf16[512,256]{1,0:T(8,128)(2,1)S(1)}, u32[]{:S(2)}, u32[]{:S(2)}) collective-permute-start(bf16[512,256]{1,0:T(8,128)(2,1)} %get-tuple-element.259), channel_id=1, source_target_pairs={{0,8},{4,12},{8,0},{12,4},{16,24},{20,28},{24,16},{28,20},{1,9},{5... | collective-permute-start | bytes 786440 | tf_op jit(solution)/shard_map/ppermute | solution.py:45
  265.9 20.6 %collective-permute-start.33 = (bf16[512,256]{1,0:T(8,128)(2,1)S(1)}, bf16[512,256]{1,0:T(8,128)(2,1)S(1)}, u32[]{:S(2)}, u32[]{:S(2)}) collective-permute-start(bf16[512,256]{1,0:T(8,128)(2,1)S(1)} %copy-done.36), channel_id=1, source_target_pairs={{0,12},{4,8},{8,4},{12,0},{16,28},{20,24},{24,20},{28,16},{1,13},{... | collective-permute-start | bytes 786440 | tf_op jit(solution)/shard_map/ppermute | solution.py:45
  286.5 39.7 %collective-permute-start.34 = (bf16[2,64,5248]{2,1,0:T(8,128)(2,1)}, bf16[2,64,5248]{2,1,0:T(8,128)(2,1)}, u32[]{:S(2)}, u32[]{:S(2)}) collective-permute-start(bf16[2,64,5248]{2,1,0:T(8,128)(2,1)} %get-tuple-element.261), channel_id=1, source_target_pairs={{0,8},{4,12},{8,0},{12,4},{16,24},{20,28},{24,16},{28,20},{1,9},{5... | collective-permute-start | bytes 4030472 | tf_op jit(solution)/shard_map/ppermute | solution.py:45
  288.0 38.2 %collective-permute-start.35 = (bf16[2,64,5248]{2,1,0:T(8,128)(2,1)}, bf16[2,64,5248]{2,1,0:T(8,128)(2,1)}, u32[]{:S(2)}, u32[]{:S(2)}) collective-permute-start(bf16[2,64,5248]{2,1,0:T(8,128)(2,1)} %get-tuple-element.262), channel_id=1, source_target_pairs={{0,16},{4,20},{8,24},{12,28},{16,0},{20,4},{24,8},{28,12},{1,17},{... | collective-permute-start | bytes 4030472 | tf_op jit(solution)/shard_map/ppermute | solution.py:45
  330.7 19.5 %collective-permute-start.37 = (bf16[64,5248]{1,0:T(8,128)(2,1)}, bf16[64,5248]{1,0:T(8,128)(2,1)S(1)}, u32[]{:S(2)}, u32[]{:S(2)}) collective-permute-start(bf16[64,5248]{1,0:T(8,128)(2,1)} %fusion.7), channel_id=1, source_target_pairs={{0,8},{4,12},{8,0},{12,4},{16,24},{20,28},{24,16},{28,20},{1,9},{5... | collective-permute-start | bytes 2015240 | tf_op jit(solution)/shard_map/ppermute | solution.py:45
  332.1 21.3 %collective-permute-start.36 = (bf16[64,5248]{1,0:T(8,128)(2,1)}, bf16[64,5248]{1,0:T(8,128)(2,1)}, u32[]{:S(2)}, u32[]{:S(2)}) collective-permute-start(bf16[64,5248]{1,0:T(8,128)(2,1)} %fusion.6), channel_id=1, source_target_pairs={{0,16},{4,20},{8,24},{12,28},{16,0},{20,4},{24,8},{28,12},{1,17},{... | collective-permute-start | bytes 2015240 | tf_op jit(solution)/shard_map/ppermute | solution.py:45
  342.0 69.0 %reduce-scatter.3.cloned.1.call-start = ((), (), s32[]{:S(2)}) async-start(), calls=%async_computation.4 | async-start | bytes 1679360 | tf_op jit(solution)/shard_map/reduce_scatter | solution.py:1034
  363.9 23.0 %collective-permute-start.38 = (bf16[4,256,1024]{2,1,0:T(8,128)(2,1)}, bf16[4,256,1024]{2,1,0:T(8,128)(2,1)S(1)}, u32[]{:S(2)}, u32[]{:S(2)}) collective-permute-start(bf16[4,256,1024]{2,1,0:T(8,128)(2,1)} %input_grad.2), channel_id=1, source_target_pairs={{0,4},{4,0},{8,12},{12,8},{16,20},{20,16},{24,28},{28,24},{1,5},{5... | collective-permute-start | bytes 6291464 | tf_op jit(solution)/shard_map/ppermute | solution.py:45
  363.9 23.0 %collective-permute-start.39 = (bf16[4,4,32,896]{3,2,1,0:T(8,128)(2,1)}, bf16[4,4,32,896]{3,2,1,0:T(8,128)(2,1)S(1)}, u32[]{:S(2)}, u32[]{:S(2)}) collective-permute-start(bf16[4,4,32,896]{3,2,1,0:T(8,128)(2,1)} %get-tuple-element.283), channel_id=1, source_target_pairs={{0,16},{4,20},{8,24},{12,28},{16,0},{20,4},{24,8},{28,12},{1,17},{... | collective-permute-start | bytes 2752520 | tf_op jit(solution)/shard_map/ppermute | solution.py:45
  392.8 30.3 %all-to-all-start = ((bf16[4,4,32,896]{3,2,1,0:T(8,128)(2,1)}), bf16[4,4,32,896]{3,2,1,0:T(8,128)(2,1)S(1)}, u32[]{:S(2)}, u32[]{:S(2)}) async-start(bf16[4,4,32,896]{3,2,1,0:T(8,128)(2,1)} %add_convert_fusion.2), calls=%async_computation | async-start | bytes 1835008 | tf_op jit(solution)/shard_map/all_to_all | solution.py:1162
  (60 other events, 673.3 us)
Sparse Core Ops, SparseCore 0:
  40.3 35.6 all-gather.4
  77.6 44.9 all-gather.6
  342.1 29.7 reduce-scatter.4
  374.2 30.4 reduce-scatter.2

commit v4 on v3

--- a/solution.py
+++ b/solution.py
@@ -1079,7 +1079,9 @@
     *sent, turned, lse = attention_forward(scal, after(qkv, foreign), chunk)
     up_x, up_y, out_far, *sent = tied(up_x, up_y, out_far, *sent)
     near = jnp.stack([piece[:, :, 512:] for piece in (foreign, up_x, up_y)] + [out_far])
-    away, *came_heads = tied(hop(near, 1), *[hop(sent[k], k) for k in (1, 2, 3)])
+    away, cot_came, *came_heads = tied(
+        hop(near, 1), hop(after(cot_other, sent[0]), 4), *[hop(sent[k], k) for k in (1, 2, 3)]
+    )
     heads = [sent[0], *came_heads]
     far_a, far_b = hop(after(up_y, away)[:, :128], 2), hop(after(up_x, away)[:, 128:], 4)
     ups = (foreign, up_x, up_y, far_a, far_b)
@@ -1096,9 +1098,8 @@
     act_away, slope_away, down_x, down_y = tied(act_away, slope_away, down_x, down_y)
     downs = (down_own, down_y, down_x)
     part_away = hop(feed_down(scal, act_away, downs, BF), 1)
-    cot_came = hop(after(cot_other, act_away), 4)
     part = feed_down(scal, act, downs, F32)
-    part, part_away, cot_came = tied(part, part_away, cot_came)
+    part, part_away = tied(part, part_away)
     out_own, out_away, dh2, dz2, sums2 = second_norm(y1, part, part_away, cot_own, cot_came, vecs)
     dz2_away = hop(dz2, 1)
     dak, das, dbk, dbs = down_grad(scal, (act, act_away), (dz2, dz2_away))
@@ -1142,8 +1143,9 @@
         scal, y1s, dus, all_heads, dao, vec_block, up_came, hop(out_other, 1)
     )
     uak, uas, ubk, ubs, *dattn = tied(uak, uas, ubk, ubs, *dattn)
+    ua_came, ub_came = hop(uas, 2), hop(ubs, 4)
+    da_came, db_came = tied(da_came, db_came, uak)[:2]
     da_next, db_next = add_far(dak, dbk, da_came, db_came)
-    ua_came, ub_came = hop(uas, 2), hop(ubs, 4)
     dqkv = attention_backward(scal, after(qkv, uak), dattn, turned, lse, chunk, 0, 4)
     da_next, db_next, ua_came, ub_came, dqkv = tied(da_next, db_next, ua_came, ub_came, dqkv)
 

time: 451 us -> 436 us (0.967)
  waiting for transfers between devices: 118 us -> 104 us
    ppermute x40, waiting for transfers between devices: 99.1 us -> 85.8 us  [hop(): return lax.ppermute(value, 'ctx', [(i, i ^ mask) for i in range(count)])]
  transfers between devices with their start and end apart: 49 -> 49, of which waited for: 30 -> 28; matrix products, arithmetic and copies ran while one was open for 9% -> 9% of each run, Pallas kernels for 41% -> 42%
where the time goes in v4:
time: 436 us; the launch traced here: 427 us
  Pallas kernels  199 us (46%)
  waiting for transfers between devices  104 us (24%)
  starting transfers between devices  53.6 us (12%)
  other arithmetic  32.8 us (8%)
  local copies, waits for them, and re-layouts  21.1 us (5%)
  between operations  16 us (4%)
    ppermute x40, waiting for transfers between devices, hop(): return lax.ppermute(value, 'ctx', [(i, i ^ mask) for i in range(count)])  85.8 us
    pallas_call x1, Pallas kernels, attention_backward(): pl.pallas_call(partial(attention_backward_kernel, first=first, heads=head...  37.6 us
    ppermute x40, starting transfers between devices, hop(): return lax.ppermute(value, 'ctx', [(i, i ^ mask) for i in range(count)])  36.7 us
    pallas_call x1, Pallas kernels, attention_forward(): pl.pallas_call(partial(attention_forward_kernel, heads=heads, chunk=chunk...  22.2 us
    pallas_call x1, Pallas kernels, feed_back(): pl.pallas_call(back_kernel, out_shape=(du, du, struct((ROWS, D), F32), st...  17.8 us
    pallas_call x2, Pallas kernels, feed_up(): pl.pallas_call(up_kernel, out_shape=(struct((4, ROWS, 512), BF), struct((...  16.1 us
    pallas_call x2, Pallas kernels, feed_down(): pl.pallas_call(down_kernel, out_shape=struct((ROWS, D), dtype), in_specs=...  14 us
    ppermute x3, waiting for transfers between devices, around(): lax.ppermute(value, 'fsdp', [(i, (i + k) % 4) for i in range(4)])  13 us
  transfers between devices with their start and end apart: 49, of which 28 were waited for; matrix products, arithmetic and copies ran while one was open for 9% of the time, Pallas kernels for 42%

profile of v4, /device:TPU:0, one launch (start us, length us, event | category | flops | bytes accessed | tf_op | source)
XLA Modules:
  0.0 427.0 jit_solution(4767459683932825970)
XLA Ops:
  9.6 4.6 %carve.1 = (bf16[256,1024]{1,0:T(8,128)(2,1)}, bf16[256,1024]{1,0:T(8,128)(2,1)}, bf16[256,1024]{1,0:T(8,128)(2,1)}, bf16[256,1024]{1,0:T(8,128)(2,1)}, bf16[256...) custom-call(bf16[2,1,256,1024]{3,2,1,0:T(8,128)(2,1)} %tokens.1, ...), custom_call_target="tpu_custom_call" | custom-call | flops 4600000000 | bytes 1048576 | tf_op jit(solution)/shard_map/carve/pallas_call | solution.py:359
  22.8 5.0 %collective-permute-done = bf16[144,768]{1,0:T(8,128)(2,1)S(1)} collective-permute-done((bf16[144,768]{1,0:T(8,128)(2,1)}, bf16[144,768]{1,0:T(8,128)(2,1)S(1)}, u32[]{:S(2)}, u32[]{:S(2)}) %collective-permute-start) | collective-permute-done | bytes 221216 | tf_op jit(solution)/shard_map/ppermute | solution.py:1059
  27.8 8.1 %collective-permute-done.1 = bf16[144,768]{1,0:T(8,128)(2,1)S(1)} collective-permute-done((bf16[144,768]{1,0:T(8,128)(2,1)}, bf16[144,768]{1,0:T(8,128)(2,1)S(1)}, u32[]{:S(2)}, u32[]{:S(2)}) %collective-permute-start.1) | collective-permute-done | bytes 221216 | tf_op jit(solution)/shard_map/ppermute | solution.py:1059
  40.2 16.2 %collective-permute-done.5.away = bf16[3,144,768]{2,1,0:T(8,128)(2,1)} collective-permute-done((bf16[3,144,768]{2,1,0:T(8,128)(2,1)}, bf16[3,144,768]{2,1,0:T(8,128)(2,1)}, u32[]{:S(2)}, u32[]{:S(2)}) %collective-permute-start.5) | collective-permute-done | bytes 663584 | tf_op jit(solution)/shard_map/ppermute | solution.py:45
  56.4 5.8 %collective-permute-done.4.x = bf16[2,256,1024]{2,1,0:T(8,128)(2,1)S(1)} collective-permute-done((bf16[2,256,1024]{2,1,0:T(8,128)(2,1)S(1)}, bf16[2,256,1024]{2,1,0:T(8,128)(2,1)S(1)}, u32[]{:S(2)}, u32[]{:S(2)}) %collective-permute-start.4) | collective-permute-done | bytes 1048608 | tf_op jit(solution)/shard_map/ppermute | solution.py:45
  66.7 10.2 %project.1 = (bf16[2048,768]{1,0:T(8,128)(2,1)}, bf16[2048,1024]{1,0:T(8,128)(2,1)}, bf16[1024,768]{1,0:T(8,128)(2,1)}, f32[8,1024]{1,0:T(8,128)}, f32[8,512]{1,0:T(8,128)}) custom-call(s32[42]{0:T(128)} %concatenate.48.scal, bf16[256,768]{1,0:T(8,128)(2,1)} %get-tuple-element.163.pack, bf16[16,256]{1,0:T(8,128)(2,1)} %select_select_fusion.small, ...), custom_call_target="tpu_custom_call" | custom-call | flops 9200000000 | bytes 1048576 | tf_op jit(solution)/shard_map/project/pallas_call | solution.py:424
  82.1 22.2 %attention_forward.1 = (bf16[512,256]{1,0:T(8,128)(2,1)}, bf16[512,256]{1,0:T(8,128)(2,1)}, bf16[512,256]{1,0:T(8,128)(2,1)}, bf16[512,256]{1,0:T(8,128)(2,1)}, f32[256,2048]{1,0:T(8,128)}, /*index=5*/f32[4,2048]{1,0:T(4,128)}) custom-call(s32[42]{0:T(128)} %concatenate.48.scal, bf16[2048,768]{1,0:T(8,128)(2,1)} %get-tuple-element.268.qkv), custom_call_target="tpu_custom_call" | custom-call | flops 26449999872 | bytes 1048576 | tf_op jit(solution)/shard_map/attention_forward/pallas_call | solution.py:211
  111.7 7.3 %collective-permute-done.14.h2 = bf16[512,256]{1,0:T(8,128)(2,1)S(1)} collective-permute-done((bf16[512,256]{1,0:T(8,128)(2,1)S(1)}, bf16[512,256]{1,0:T(8,128)(2,1)S(1)}, u32[]{:S(2)}, u32[]{:S(2)}) %collective-permute-start.14) | collective-permute-done | bytes 262176 | tf_op jit(solution)/shard_map/ppermute | solution.py:45
  119.0 4.5 %collective-permute-done.15.h3 = bf16[512,256]{1,0:T(8,128)(2,1)S(1)} collective-permute-done((bf16[512,256]{1,0:T(8,128)(2,1)S(1)}, bf16[512,256]{1,0:T(8,128)(2,1)S(1)}, u32[]{:S(2)}, u32[]{:S(2)}) %collective-permute-start.15) | collective-permute-done | bytes 262176 | tf_op jit(solution)/shard_map/ppermute | solution.py:45
  127.7 9.0 %attention_out.1 = (f32[512,1024]{1,0:T(8,128)}, bf16[512,1024]{1,0:T(8,128)(2,1)}, f32[512,1024]{1,0:T(8,128)}, f32[512,128]{1,0:T(8,128)}) custom-call(s32[42]{0:T(128)} %concatenate.48.scal, bf16[512,256]{1,0:T(8,128)(2,1)} %get-tuple-element.178.h0, bf16[512,256]{1,0:T(8,128)(2,1)} %copy-done.22, bf16[512,256]{1,0:T(8,128)(2,1)} %copy-done.24, ...), custom_call_target="tpu_custom_call" | custom-call | flops 10350000128 | bytes 1048576 | tf_op jit(solution)/shard_map/attention_out/pallas_call | solution.py:492
  144.3 8.1 %feed_up.2 = (bf16[4,512,512]{2,1,0:T(8,128)(2,1)}, bf16[4,512,512]{2,1,0:T(8,128)(2,1)}) custom-call(s32[42]{0:T(128)} %concatenate.48.scal, bf16[512,1024]{1,0:T(8,128)(2,1)} %get-tuple-element.200.y1_low.y1_a, f32[8,512]{1,0:T(8,128)} %get-tuple-element.201.up_bias, bf16[256,4096]{1,0:T(8,128)(2,1)} %w_up.7, bf16[3,256,640]{2,1,0:T(8,128)(2,1)} %copy-done.3, ...), custom_call_target="tpu_custom_call" | custom-call | flops 8049999872 | bytes 1048576 | tf_op jit(solution)/shard_map/feed_up/pallas_call | solution.py:586
  153.3 8.1 %feed_up.3 = (bf16[4,512,512]{2,1,0:T(8,128)(2,1)}, bf16[4,512,512]{2,1,0:T(8,128)(2,1)}) custom-call(s32[42]{0:T(128)} %concatenate.48.scal, bf16[512,1024]{1,0:T(8,128)(2,1)} %copy-done.31, f32[8,512]{1,0:T(8,128)} %get-tuple-element.201.up_bias, bf16[256,4096]{1,0:T(8,128)(2,1)} %w_up.7, bf16[3,256,640]{2,1,0:T(8,128)(2,1)} %copy-done.3, ...), custom_call_target="tpu_custom_call" | custom-call | flops 8049999872 | bytes 1048576 | tf_op jit(solution)/shard_map/feed_up/pallas_call | solution.py:586
  161.4 6.5 %collective-permute-done.19.from_x.rest_7_ = bf16[4,128,1024]{2,1,0:T(8,128)(2,1)} collective-permute-done((bf16[4,128,1024]{2,1,0:T(8,128)(2,1)S(1)}, bf16[4,128,1024]{2,1,0:T(8,128)(2,1)}, u32[]{:S(2)}, u32[]{:S(2)}) %collective-permute-start.19) | collective-permute-done | bytes 1048608 | tf_op jit(solution)/shard_map/ppermute | solution.py:45
  168.2 7.0 %feed_down.3 = bf16[512,1024]{1,0:T(8,128)(2,1)} custom-call(s32[42]{0:T(128)} %concatenate.48.scal, bf16[4,512,512]{2,1,0:T(8,128)(2,1)} %get-tuple-element.215.act.act_b, bf16[4,2,128,1024]{3,2,1,0:T(8,128)(2,1)} %bitcast.91, bf16[4,128,1024]{2,1,0:T(8,128)(2,1)} %collective-permute-done.20.from_y.rest_6_, ...), custom_call_target="tpu_custom_call" | custom-call | flops 5750000128 | bytes 1048576 | tf_op jit(solution)/shard_map/feed_down/pallas_call | solution.py:623
  175.3 7.0 %feed_down.2.part = f32[512,1024]{1,0:T(8,128)} custom-call(s32[42]{0:T(128)} %concatenate.48.scal, bf16[4,512,512]{2,1,0:T(8,128)(2,1)} %get-tuple-element.206.act.act_a, bf16[4,2,128,1024]{3,2,1,0:T(8,128)(2,1)} %bitcast.92, bf16[4,128,1024]{2,1,0:T(8,128)(2,1)} %collective-permute-done.20.from_y.rest_6_, ...), custom_call_target="tpu_custom_call" | custom-call | flops 5750000128 | bytes 1048576 | tf_op jit(solution)/shard_map/feed_down/pallas_call | solution.py:623
  183.3 6.6 %second_norm.1 = (bf16[256,1024]{1,0:T(8,128)(2,1)}, bf16[256,1024]{1,0:T(8,128)(2,1)}, f32[512,1024]{1,0:T(8,128)}, bf16[512,1024]{1,0:T(8,128)(2,1)}, f32[8,1024]{1,0:T(8,128)}) custom-call(f32[512,1024]{1,0:T(8,128)} %get-tuple-element.199.y1, f32[512,1024]{1,0:T(8,128)} %feed_down.2.part, bf16[512,1024]{1,0:T(8,128)(2,1)} %copy-done.33, ...), custom_call_target="tpu_custom_call" | custom-call | flops 4600000000 | bytes 1048576 | tf_op jit(solution)/shard_map/second_norm/pallas_call | solution.py:673
  193.9 9.8 %down_grad.1 = (bf16[2,256,1024]{2,1,0:T(8,128)(2,1)}, bf16[2,256,1024]{2,1,0:T(8,128)(2,1)}, bf16[2,256,1024]{2,1,0:T(8,128)(2,1)}, bf16[2,256,1024]{2,1,0:T(8,128)(2,1)}) custom-call(s32[42]{0:T(128)} %concatenate.48.scal, bf16[4,512,512]{2,1,0:T(8,128)(2,1)} %get-tuple-element.206.act.act_a, bf16[4,512,512]{2,1,0:T(8,128)(2,1)} %get-tuple-element.215.act.act_b, ...), custom_call_target="tpu_custom_call" | custom-call | flops 12650000384 | bytes 1048576 | tf_op jit(solution)/shard_map/down_grad/pallas_call | solution.py:821
  206.7 17.8 %feed_back.1 = (bf16[4,512,512]{2,1,0:T(8,128)(2,1)}, bf16[4,512,512]{2,1,0:T(8,128)(2,1)}, f32[512,1024]{1,0:T(8,128)}, bf16[512,1024]{1,0:T(8,128)(2,1)}, f32[8,512]{1,0:T(8,128)}) custom-call(s32[42]{0:T(128)} %concatenate.48.scal, bf16[512,1024]{1,0:T(8,128)(2,1)} %get-tuple-element.221.dz2_a, bf16[512,1024]{1,0:T(8,128)(2,1)} %copy-done.32, ...), custom_call_target="tpu_custom_call" | custom-call | flops 25300000768 | bytes 1048576 | tf_op jit(solution)/shard_map/feed_back/pallas_call | solution.py:729
  224.5 5.0 %collective-permute-done.24 = bf16[2,256,1024]{2,1,0:T(8,128)(2,1)S(1)} collective-permute-done((bf16[2,256,1024]{2,1,0:T(8,128)(2,1)}, bf16[2,256,1024]{2,1,0:T(8,128)(2,1)S(1)}, u32[]{:S(2)}, u32[]{:S(2)}) %collective-permute-start.24) | collective-permute-done | bytes 1048608 | tf_op jit(solution)/shard_map/ppermute | solution.py:45
  233.2 7.5 %up_grad_other.1 = bf16[4,128,2048]{2,1,0:T(8,128)(2,1)} custom-call(s32[42]{0:T(128)} %concatenate.48.scal, bf16[512,1024]{1,0:T(8,128)(2,1)} %get-tuple-element.200.y1_low.y1_a, bf16[512,1024]{1,0:T(8,128)(2,1)} %copy-done.31, bf16[4,512,512]{2,1,0:T(8,128)(2,1)} %get-tuple-element.241.du_a, bf16[4,512,512]{2,1,0:T(8,128)(2,1)} %get-tuple-element.242.du_b), custom_call_target="tpu_custom_call" | custom-call | flops 6899999744 | bytes 1048576 | tf_op jit(solution)/shard_map/up_grad_other/pallas_call | solution.py:901
  241.1 7.1 %first_norm.1 = (bf16[512,1024]{1,0:T(8,128)(2,1)}, bf16[512,256]{1,0:T(8,128)(2,1)}, bf16[512,256]{1,0:T(8,128)(2,1)}, bf16[512,256]{1,0:T(8,128)(2,1)}, bf16[512,256]{1,0:T(8,128)(2,1)}, /*index=5*/f32[8,1024]{1,0:T(8,128)}) custom-call(s32[42]{0:T(128)} %concatenate.48.scal, f32[512,1024]{1,0:T(8,128)} %get-tuple-element.243.dh2, ...), custom_call_target="tpu_custom_call" | custom-call | flops 8049999872 | bytes 1048576 | tf_op jit(solution)/shard_map/first_norm/pallas_call | solution.py:775
  250.4 5.2 %out_grad_other.1 = bf16[4,128,1152]{2,1,0:T(8,128)(2,1)} custom-call(s32[42]{0:T(128)} %concatenate.48.scal, bf16[4,512,256]{2,1,0:T(8,128)(2,1)} %pad_maximum_fusion.3.heads, bf16[512,1024]{1,0:T(8,128)(2,1)} %get-tuple-element.286.dao, f32[8,128,128]{2,1,0:T(8,128)} %bitcast.102), custom_call_target="tpu_custom_call" | custom-call | flops 3449999872 | bytes 1048576 | tf_op jit(solution)/shard_map/out_grad_other/pallas_call | solution.py:918
  259.1 10.4 %up_grad_own.1 = (bf16[2,64,5248]{2,1,0:T(8,128)(2,1)}, bf16[2,64,5248]{2,1,0:T(8,128)(2,1)}, bf16[2,64,5248]{2,1,0:T(8,128)(2,1)}, bf16[2,64,5248]{2,1,0:T(8,128)(2,1)}) custom-call(s32[42]{0:T(128)} %concatenate.48.scal, bf16[512,1024]{1,0:T(8,128)(2,1)} %get-tuple-element.200.y1_low.y1_a, bf16[512,1024]{1,0:T(8,128)(2,1)} %copy-done.31, ...), custom_call_target="tpu_custom_call" | custom-call | flops 11500000256 | bytes 1048576 | tf_op jit(solution)/shard_map/up_grad_own/pallas_call | solution.py:931
  274.2 37.6 %attention_backward.1.dqkv = bf16[2048,768]{1,0:T(8,128)(2,1)} custom-call(s32[42]{0:T(128)} %concatenate.48.scal, bf16[2048,768]{1,0:T(8,128)(2,1)} %get-tuple-element.268.qkv, bf16[512,256]{1,0:T(8,128)(2,1)} %get-tuple-element.269.grad0, bf16[512,256]{1,0:T(8,128)(2,1)} %collective-permute-done.29.grad1, bf16[512,256]{1,0:T(8,128)(2,1)} %collective-permute-done.30.grad2, ...), custom_call_target="tpu_custom_call" | custom-call | flops 46000001024 | bytes 1048576 | tf_op jit(solution)/shard_map/attention_backward/pallas_call | solution.py:306
  319.7 4.3 %collective-permute-start.36 = (bf16[64,5248]{1,0:T(8,128)(2,1)}, bf16[64,5248]{1,0:T(8,128)(2,1)}, u32[]{:S(2)}, u32[]{:S(2)}) collective-permute-start(bf16[64,5248]{1,0:T(8,128)(2,1)} %fusion.6), channel_id=1, source_target_pairs={{0,16},{4,20},{8,24},{12,28},{16,0},{20,4},{24,8},{28,12},{1,17},{... | collective-permute-start | bytes 2015240 | tf_op jit(solution)/shard_map/ppermute | solution.py:45
  327.9 8.2 %qkv_grad.1 = (bf16[4,4,32,896]{3,2,1,0:T(8,128)(2,1)}, bf16[4,4,32,896]{3,2,1,0:T(8,128)(2,1)}) custom-call(s32[42]{0:T(128)} %concatenate.48.scal, bf16[2048,1024]{1,0:T(8,128)(2,1)} %get-tuple-element.191.x_all.x, bf16[2048,768]{1,0:T(8,128)(2,1)} %attention_backward.1.dqkv), custom_call_target="tpu_custom_call" | custom-call | flops 9200000000 | bytes 1048576 | tf_op jit(solution)/shard_map/qkv_grad/pallas_call | solution.py:966
  342.7 6.4 %input_grad.2 = bf16[4,256,1024]{2,1,0:T(8,128)(2,1)} custom-call(s32[42]{0:T(128)} %concatenate.48.scal, bf16[2048,768]{1,0:T(8,128)(2,1)} %attention_backward.1.dqkv, bf16[1024,768]{1,0:T(8,128)(2,1)} %get-tuple-element.285.weight, bf16[512,1024]{1,0:T(8,128)(2,1)} %get-tuple-element.286.dao), custom_call_target="tpu_custom_call" | custom-call | flops 5750000128 | bytes 1048576 | tf_op jit(solution)/shard_map/input_grad/pallas_call | solution.py:992
  350.9 6.4 %input_grad.3 = bf16[4,256,1024]{2,1,0:T(8,128)(2,1)} custom-call(s32[42]{0:T(128)} %concatenate.48.scal, bf16[2048,768]{1,0:T(8,128)(2,1)} %attention_backward.1.dqkv, bf16[1024,768]{1,0:T(8,128)(2,1)} %get-tuple-element.285.weight, bf16[512,1024]{1,0:T(8,128)(2,1)} %get-tuple-element.286.dao), custom_call_target="tpu_custom_call" | custom-call | flops 5750000128 | bytes 1048576 | tf_op jit(solution)/shard_map/input_grad/pallas_call | solution.py:992
  357.3 14.8 %collective-permute-done.39 = bf16[4,4,32,896]{3,2,1,0:T(8,128)(2,1)S(1)} collective-permute-done((bf16[4,4,32,896]{3,2,1,0:T(8,128)(2,1)}, bf16[4,4,32,896]{3,2,1,0:T(8,128)(2,1)S(1)}, u32[]{:S(2)}, u32[]{:S(2)}) %collective-permute-start.39) | collective-permute-done | bytes 917536 | tf_op jit(solution)/shard_map/ppermute | solution.py:45
  377.2 7.8 %all-to-all-start = ((bf16[4,4,32,896]{3,2,1,0:T(8,128)(2,1)}), bf16[4,4,32,896]{3,2,1,0:T(8,128)(2,1)S(1)}, u32[]{:S(2)}, u32[]{:S(2)}) async-start(bf16[4,4,32,896]{3,2,1,0:T(8,128)(2,1)} %add_convert_fusion.2), calls=%async_computation | async-start | bytes 1835008 | tf_op jit(solution)/shard_map/all_to_all | solution.py:1164
  399.7 3.6 collective-permute-done.42
  409.0 3.4 all-to-all-start.1
  (259 shorter events, 119.7 us)
Async XLA Ops:
  7.2 69.8 %all-gather.5.cloned.1.call-start = ((), (), s32[]{:S(2)}) async-start(), calls=%async_computation.6 | async-start | bytes 1638400 | tf_op jit(solution)/shard_map/all_gather | solution.py:1065
  14.2 21.6 %collective-permute-start.3 = (bf16[256,1024]{1,0:T(8,128)(2,1)}, bf16[256,1024]{1,0:T(8,128)(2,1)S(1)}, u32[]{:S(2)}, u32[]{:S(2)}) collective-permute-start(bf16[256,1024]{1,0:T(8,128)(2,1)} %get-tuple-element.160), channel_id=1, source_target_pairs={{0,16},{4,20},{8,24},{12,28},{16,0},{20,4},{24,8},{28,12},{1,17},{... | collective-permute-start | bytes 1572872 | tf_op jit(solution)/shard_map/ppermute | solution.py:45
  18.9 17.0 %collective-permute-start.1 = (bf16[144,768]{1,0:T(8,128)(2,1)}, bf16[144,768]{1,0:T(8,128)(2,1)S(1)}, u32[]{:S(2)}, u32[]{:S(2)}) collective-permute-start(bf16[144,768]{1,0:T(8,128)(2,1)} %get-tuple-element.159), channel_id=1, source_target_pairs={{0,2},{1,3},{2,0},{3,1},{4,6},{5,7},{6,4},{7,5},{8,10},{9,11},{10,... | collective-permute-start | bytes 663560 | tf_op jit(solution)/shard_map/ppermute | solution.py:1059
  21.4 14.4 %collective-permute-start.2 = (bf16[144,768]{1,0:T(8,128)(2,1)}, bf16[144,768]{1,0:T(8,128)(2,1)S(1)}, u32[]{:S(2)}, u32[]{:S(2)}) collective-permute-start(bf16[144,768]{1,0:T(8,128)(2,1)} %get-tuple-element.159), channel_id=1, source_target_pairs={{0,3},{1,0},{2,1},{3,2},{4,7},{5,4},{6,5},{7,6},{8,11},{9,8},{10,9... | collective-permute-start | bytes 663560 | tf_op jit(solution)/shard_map/ppermute | solution.py:1059
  37.2 25.1 %collective-permute-start.4 = (bf16[2,256,1024]{2,1,0:T(8,128)(2,1)S(1)}, bf16[2,256,1024]{2,1,0:T(8,128)(2,1)S(1)}, u32[]{:S(2)}, u32[]{:S(2)}) collective-permute-start(bf16[2,256,1024]{2,1,0:T(8,128)(2,1)S(1)} %pad_maximum_fusion.2), channel_id=1, source_target_pairs={{0,8},{4,12},{8,0},{12,4},{16,24},{20,28},{24,16},{28,20},{1,9},{5... | collective-permute-start | bytes 3145736 | tf_op jit(solution)/shard_map/ppermute | solution.py:45
  39.6 16.8 %collective-permute-start.5 = (bf16[3,144,768]{2,1,0:T(8,128)(2,1)}, bf16[3,144,768]{2,1,0:T(8,128)(2,1)}, u32[]{:S(2)}, u32[]{:S(2)}) collective-permute-start(bf16[3,144,768]{2,1,0:T(8,128)(2,1)} %pad_maximum_fusion.7.near), channel_id=1, source_target_pairs={{0,16},{4,20},{8,24},{12,28},{16,0},{20,4},{24,8},{28,12},{1,17},{... | collective-permute-start | bytes 1990664 | tf_op jit(solution)/shard_map/ppermute | solution.py:45
  40.2 100.2 %all-gather.7.cloned.1.call-start = ((), (), s32[]{:S(2)}) async-start(), calls=%async_computation.7 | async-start | bytes 2621440 | tf_op jit(solution)/shard_map/all_gather | solution.py:1068
  65.5 328.0 %reduce-scatter.5.cloned.1.call-start = ((), (), s32[]{:S(2)}) async-start(), calls=%async_computation.5 | async-start | bytes 1310720 | tf_op jit(solution)/shard_map/reduce_scatter | solution.py:1034
  78.4 28.2 %collective-permute-start.8 = (bf16[3,256,640]{2,1,0:T(8,128)(2,1)S(1)}, bf16[3,256,640]{2,1,0:T(8,128)(2,1)S(1)}, u32[]{:S(2)}, u32[]{:S(2)}) collective-permute-start(bf16[3,256,640]{2,1,0:T(8,128)(2,1)S(1)} %pad_maximum_fusion.5.rest_0_), channel_id=1, source_target_pairs={{0,8},{4,12},{8,0},{12,4},{16,24},{20,28},{24,16},{28,20},{1,9},{5... | collective-permute-start | bytes 2949128 | tf_op jit(solution)/shard_map/ppermute | solution.py:45
  80.0 27.9 %collective-permute-start.9 = (bf16[3,256,640]{2,1,0:T(8,128)(2,1)S(1)}, bf16[3,256,640]{2,1,0:T(8,128)(2,1)}, u32[]{:S(2)}, u32[]{:S(2)}) collective-permute-start(bf16[3,256,640]{2,1,0:T(8,128)(2,1)S(1)} %pad_maximum_fusion.5.rest_0_), channel_id=1, source_target_pairs={{0,16},{4,20},{8,24},{12,28},{16,0},{20,4},{24,8},{28,12},{1,17},{... | collective-permute-start | bytes 2949128 | tf_op jit(solution)/shard_map/ppermute | solution.py:45
  80.5 26.1 %collective-permute-start.10 = (bf16[3,256,128]{2,1,0:T(8,128)(2,1)S(1)}, bf16[3,256,128]{2,1,0:T(8,128)(2,1)S(1)}, u32[]{:S(2)}, u32[]{:S(2)}) collective-permute-start(bf16[3,256,128]{2,1,0:T(8,128)(2,1)S(1)} %get-tuple-element.317), channel_id=1, source_target_pairs={{0,24},{4,28},{8,16},{12,20},{16,8},{20,12},{24,0},{28,4},{1,25},{... | collective-permute-start | bytes 589832 | tf_op jit(solution)/shard_map/ppermute | solution.py:45
  109.0 15.4 %collective-permute-start.11 = (bf16[4,3,256,128]{3,2,1,0:T(8,128)(2,1)S(1)}, bf16[4,3,256,128]{3,2,1,0:T(8,128)(2,1)}, u32[]{:S(2)}, u32[]{:S(2)}) collective-permute-start(bf16[4,3,256,128]{3,2,1,0:T(8,128)(2,1)S(1)} %pad_maximum_fusion.6.near), channel_id=1, source_target_pairs={{0,4},{4,0},{8,12},{12,8},{16,20},{20,16},{24,28},{28,24},{1,5},{5... | collective-permute-start | bytes 2359304 | tf_op jit(solution)/shard_map/ppermute | solution.py:45
  109.1 14.5 %collective-permute-start.12 = (bf16[256,1024]{1,0:T(8,128)(2,1)S(1)}, bf16[256,1024]{1,0:T(8,128)(2,1)S(1)}, u32[]{:S(2)}, u32[]{:S(2)}) collective-permute-start(bf16[256,1024]{1,0:T(8,128)(2,1)S(1)} %copy-done.34), channel_id=1, source_target_pairs={{0,16},{4,20},{8,24},{12,28},{16,0},{20,4},{24,8},{28,12},{1,17},{... | collective-permute-start | bytes 1572872 | tf_op jit(solution)/shard_map/ppermute | solution.py:45
  124.4 13.7 %collective-permute-start.17 = (bf16[3,128,640]{2,1,0:T(8,128)(2,1)S(1)}, bf16[3,128,640]{2,1,0:T(8,128)(2,1)}, u32[]{:S(2)}, u32[]{:S(2)}) collective-permute-start(bf16[3,128,640]{2,1,0:T(8,128)(2,1)S(1)} %slice.190), channel_id=1, source_target_pairs={{0,16},{4,20},{8,24},{12,28},{16,0},{20,4},{24,8},{28,12},{1,17},{... | collective-permute-start | bytes 1474568 | tf_op jit(solution)/shard_map/ppermute | solution.py:45
  142.1 25.7 %collective-permute-start.19 = (bf16[4,128,1024]{2,1,0:T(8,128)(2,1)S(1)}, bf16[4,128,1024]{2,1,0:T(8,128)(2,1)}, u32[]{:S(2)}, u32[]{:S(2)}) collective-permute-start(bf16[4,128,1024]{2,1,0:T(8,128)(2,1)S(1)} %get-tuple-element.310), channel_id=1, source_target_pairs={{0,8},{4,12},{8,0},{12,4},{16,24},{20,28},{24,16},{28,20},{1,9},{5... | collective-permute-start | bytes 3145736 | tf_op jit(solution)/shard_map/ppermute | solution.py:45
  142.8 25.4 %collective-permute-start.20 = (bf16[4,128,1024]{2,1,0:T(8,128)(2,1)S(1)}, bf16[4,128,1024]{2,1,0:T(8,128)(2,1)}, u32[]{:S(2)}, u32[]{:S(2)}) collective-permute-start(bf16[4,128,1024]{2,1,0:T(8,128)(2,1)S(1)} %get-tuple-element.309), channel_id=1, source_target_pairs={{0,16},{4,20},{8,24},{12,28},{16,0},{20,4},{24,8},{28,12},{1,17},{... | collective-permute-start | bytes 3145736 | tf_op jit(solution)/shard_map/ppermute | solution.py:45
  190.5 14.1 %collective-permute-start.23 = (bf16[256,1024]{1,0:T(8,128)(2,1)}, bf16[256,1024]{1,0:T(8,128)(2,1)S(1)}, u32[]{:S(2)}, u32[]{:S(2)}) collective-permute-start(bf16[256,1024]{1,0:T(8,128)(2,1)} %get-tuple-element.226), channel_id=1, source_target_pairs={{0,16},{4,20},{8,24},{12,28},{16,0},{20,4},{24,8},{28,12},{1,17},{... | collective-permute-start | bytes 1572872 | tf_op jit(solution)/shard_map/ppermute | solution.py:45
  204.6 24.9 %collective-permute-start.24 = (bf16[2,256,1024]{2,1,0:T(8,128)(2,1)}, bf16[2,256,1024]{2,1,0:T(8,128)(2,1)S(1)}, u32[]{:S(2)}, u32[]{:S(2)}) collective-permute-start(bf16[2,256,1024]{2,1,0:T(8,128)(2,1)} %get-tuple-element.237), channel_id=1, source_target_pairs={{0,8},{4,12},{8,0},{12,4},{16,24},{20,28},{24,16},{28,20},{1,9},{5... | collective-permute-start | bytes 3145736 | tf_op jit(solution)/shard_map/ppermute | solution.py:45
  206.1 24.5 %collective-permute-start.25 = (bf16[2,256,1024]{2,1,0:T(8,128)(2,1)}, bf16[2,256,1024]{2,1,0:T(8,128)(2,1)S(1)}, u32[]{:S(2)}, u32[]{:S(2)}) collective-permute-start(bf16[2,256,1024]{2,1,0:T(8,128)(2,1)} %get-tuple-element.238), channel_id=1, source_target_pairs={{0,16},{4,20},{8,24},{12,28},{16,0},{20,4},{24,8},{28,12},{1,17},{... | collective-permute-start | bytes 3145736 | tf_op jit(solution)/shard_map/ppermute | solution.py:45
  240.7 18.4 %collective-permute-start.27 = (bf16[4,128,2048]{2,1,0:T(8,128)(2,1)}, bf16[4,128,2048]{2,1,0:T(8,128)(2,1)}, u32[]{:S(2)}, u32[]{:S(2)}) collective-permute-start(bf16[4,128,2048]{2,1,0:T(8,128)(2,1)} %up_grad_other.1), channel_id=1, source_target_pairs={{0,4},{4,0},{8,12},{12,8},{16,20},{20,16},{24,28},{28,24},{1,5},{5... | collective-permute-start | bytes 6291464 | tf_op jit(solution)/shard_map/ppermute | solution.py:45
  255.8 13.8 %collective-permute-start.29 = (bf16[512,256]{1,0:T(8,128)(2,1)S(1)}, bf16[512,256]{1,0:T(8,128)(2,1)}, u32[]{:S(2)}, u32[]{:S(2)}) collective-permute-start(bf16[512,256]{1,0:T(8,128)(2,1)S(1)} %copy-done.38), channel_id=1, source_target_pairs={{0,4},{4,0},{8,12},{12,8},{16,20},{20,16},{24,28},{28,24},{1,5},{5... | collective-permute-start | bytes 786440 | tf_op jit(solution)/shard_map/ppermute | solution.py:45
  269.8 42.0 %collective-permute-start.33 = (bf16[256,1024]{1,0:T(8,128)(2,1)S(1)}, bf16[256,1024]{1,0:T(8,128)(2,1)}, u32[]{:S(2)}, u32[]{:S(2)}) collective-permute-start(bf16[256,1024]{1,0:T(8,128)(2,1)S(1)} %fusion.9), channel_id=1, source_target_pairs={{0,8},{4,12},{8,0},{12,4},{16,24},{20,28},{24,16},{28,20},{1,9},{5... | collective-permute-start | bytes 1572872 | tf_op jit(solution)/shard_map/ppermute | solution.py:45
  270.6 44.2 %collective-permute-start.34 = (bf16[2,64,5248]{2,1,0:T(8,128)(2,1)}, bf16[2,64,5248]{2,1,0:T(8,128)(2,1)}, u32[]{:S(2)}, u32[]{:S(2)}) collective-permute-start(bf16[2,64,5248]{2,1,0:T(8,128)(2,1)} %get-tuple-element.266), channel_id=1, source_target_pairs={{0,8},{4,12},{8,0},{12,4},{16,24},{20,28},{24,16},{28,20},{1,9},{5... | collective-permute-start | bytes 4030472 | tf_op jit(solution)/shard_map/ppermute | solution.py:45
  271.9 42.8 %collective-permute-start.35 = (bf16[2,64,5248]{2,1,0:T(8,128)(2,1)}, bf16[2,64,5248]{2,1,0:T(8,128)(2,1)}, u32[]{:S(2)}, u32[]{:S(2)}) collective-permute-start(bf16[2,64,5248]{2,1,0:T(8,128)(2,1)} %get-tuple-element.267), channel_id=1, source_target_pairs={{0,16},{4,20},{8,24},{12,28},{16,0},{20,4},{24,8},{28,12},{1,17},{... | collective-permute-start | bytes 4030472 | tf_op jit(solution)/shard_map/ppermute | solution.py:45
  272.6 42.1 %collective-permute-start.32 = (bf16[256,1024]{1,0:T(8,128)(2,1)S(1)}, bf16[256,1024]{1,0:T(8,128)(2,1)}, u32[]{:S(2)}, u32[]{:S(2)}) collective-permute-start(bf16[256,1024]{1,0:T(8,128)(2,1)S(1)} %fusion.8), channel_id=1, source_target_pairs={{0,16},{4,20},{8,24},{12,28},{16,0},{20,4},{24,8},{28,12},{1,17},{... | collective-permute-start | bytes 1572872 | tf_op jit(solution)/shard_map/ppermute | solution.py:45
  319.1 16.9 %collective-permute-start.37 = (bf16[64,5248]{1,0:T(8,128)(2,1)}, bf16[64,5248]{1,0:T(8,128)(2,1)S(1)}, u32[]{:S(2)}, u32[]{:S(2)}) collective-permute-start(bf16[64,5248]{1,0:T(8,128)(2,1)} %fusion.7), channel_id=1, source_target_pairs={{0,8},{4,12},{8,0},{12,4},{16,24},{20,28},{24,16},{28,20},{1,9},{5... | collective-permute-start | bytes 2015240 | tf_op jit(solution)/shard_map/ppermute | solution.py:45
  319.7 18.9 %collective-permute-start.36 = (bf16[64,5248]{1,0:T(8,128)(2,1)}, bf16[64,5248]{1,0:T(8,128)(2,1)}, u32[]{:S(2)}, u32[]{:S(2)}) collective-permute-start(bf16[64,5248]{1,0:T(8,128)(2,1)} %fusion.6), channel_id=1, source_target_pairs={{0,16},{4,20},{8,24},{12,28},{16,0},{20,4},{24,8},{28,12},{1,17},{... | collective-permute-start | bytes 2015240 | tf_op jit(solution)/shard_map/ppermute | solution.py:45
  327.8 67.5 %reduce-scatter.3.cloned.1.call-start = ((), (), s32[]{:S(2)}) async-start(), calls=%async_computation.4 | async-start | bytes 1679360 | tf_op jit(solution)/shard_map/reduce_scatter | solution.py:1034
  349.1 23.0 %collective-permute-start.38 = (bf16[4,256,1024]{2,1,0:T(8,128)(2,1)}, bf16[4,256,1024]{2,1,0:T(8,128)(2,1)S(1)}, u32[]{:S(2)}, u32[]{:S(2)}) collective-permute-start(bf16[4,256,1024]{2,1,0:T(8,128)(2,1)} %input_grad.2), channel_id=1, source_target_pairs={{0,4},{4,0},{8,12},{12,8},{16,20},{20,16},{24,28},{28,24},{1,5},{5... | collective-permute-start | bytes 6291464 | tf_op jit(solution)/shard_map/ppermute | solution.py:45
  349.1 23.0 %collective-permute-start.39 = (bf16[4,4,32,896]{3,2,1,0:T(8,128)(2,1)}, bf16[4,4,32,896]{3,2,1,0:T(8,128)(2,1)S(1)}, u32[]{:S(2)}, u32[]{:S(2)}) collective-permute-start(bf16[4,4,32,896]{3,2,1,0:T(8,128)(2,1)} %get-tuple-element.287), channel_id=1, source_target_pairs={{0,16},{4,20},{8,24},{12,28},{16,0},{20,4},{24,8},{28,12},{1,17},{... | collective-permute-start | bytes 2752520 | tf_op jit(solution)/shard_map/ppermute | solution.py:45
  375.4 13.7 %collective-permute-start.40 = (bf16[256,1024]{1,0:T(8,128)(2,1)S(1)}, bf16[256,1024]{1,0:T(8,128)(2,1)S(1)}, u32[]{:S(2)}, u32[]{:S(2)}) collective-permute-start(bf16[256,1024]{1,0:T(8,128)(2,1)S(1)} %get-tuple-element.314), channel_id=1, source_target_pairs={{0,8},{4,12},{8,0},{12,4},{16,24},{20,28},{24,16},{28,20},{1,9},{5... | collective-permute-start | bytes 1572872 | tf_op jit(solution)/shard_map/ppermute | solution.py:45
  377.2 31.0 %all-to-all-start = ((bf16[4,4,32,896]{3,2,1,0:T(8,128)(2,1)}), bf16[4,4,32,896]{3,2,1,0:T(8,128)(2,1)S(1)}, u32[]{:S(2)}, u32[]{:S(2)}) async-start(bf16[4,4,32,896]{3,2,1,0:T(8,128)(2,1)} %add_convert_fusion.2), calls=%async_computation | async-start | bytes 1835008 | tf_op jit(solution)/shard_map/all_to_all | solution.py:1164
  (59 other events, 707.5 us)
Sparse Core Ops, SparseCore 0:
  40.3 35.6 all-gather.4
  77.6 44.9 all-gather.6
  327.9 29.0 reduce-scatter.4
  359.3 30.3 reduce-scatter.2
